TPU v7x, 32 devices: a whole 2x2x4 slice. The times are simulated.
32 devices in a mesh: groups: 2 (over x), seq: 16 (over z, y, core).
Axes of the slice: x: 2, y: 2, z: 4, core: 2. Of those that a mesh axis runs over, the one named last changes fastest.
Arguments:
- signal: bfloat16 [8192, 2048], P(('groups', 'seq')), parts along dimension 0, may hold values from -6 to 6
- input_gate: bfloat16 [8192, 2048], P(('groups', 'seq')), parts along dimension 0, may hold values from -6 to 6
- output_gate: bfloat16 [8192, 2048], P(('groups', 'seq')), parts along dimension 0, may hold values from -6 to 6
- filter_spectrum: float32 [2, 128, 64, 2048], P(None, 'seq'), may hold values from -6 to 6
- skip_gain: float32 [2048], replicated, may hold values from -1 to 1
Outputs:
- mixed_out: bfloat16 [8192, 2048], P(('groups', 'seq')), parts along dimension 0
There are 2 independent parts, one for each index of `groups`. A program takes and returns all parts, laid end to end along the dimension named above; an argument that names none is the same for every part. Nothing has to cross between parts.
All inputs are finite; a program needn't handle non-finite values.
Results may differ from a plain program's by a relative error of at most 0.005.
Values may be sent and summed in bfloat16 or wider, within the bound.
No kernel may reach another device: no remote copies, remote signals or barrier semaphores. Data moves between devices by JAX's collectives and lax.ppermute only.
A program may use at most 128 MiB of HBM per device.

v0:
```python
import functools
import math

import jax
import jax.numpy as jnp
import ml_dtypes
import numpy as np
from jax import lax
from jax.experimental import pallas as pl
from jax.experimental.pallas import tpu as pltpu
from jax.sharding import PartitionSpec as P

EVERY = ("groups", "seq")
LANES = 128
HALF = LANES // 2
BF16 = jnp.bfloat16
F32 = jnp.float32


def exchange(values):
    return lax.all_to_all(values, EVERY, split_axis=0, concat_axis=0, tiled=True)


def left_lanes(rows):
    return lax.broadcasted_iota(jnp.int32, (rows, LANES), 1) < HALF


def swap_halves(first, second):
    left = left_lanes(first.shape[0])
    return (
        jnp.where(left, first, pltpu.roll(second, HALF, 1)),
        jnp.where(left, pltpu.roll(first, HALF, 1), second),
    )


def hi_lo(matrix):
    high = matrix.astype(ml_dtypes.bfloat16)
    low = (matrix - high.astype(np.float64)).astype(ml_dtypes.bfloat16)
    return high, low


@functools.lru_cache(None)
def tables(half_rows, width):
    full_rows = 2 * half_rows
    length = full_rows * width
    low_index = np.arange(half_rows)
    angle = 2 * np.pi * (np.outer(low_index, low_index) % full_rows) / full_rows
    real_part, imag_part = np.cos(angle), -np.sin(angle)
    imag_part[0] = 1.0 - 2.0 * (low_index % 2)
    first = np.concatenate([real_part, imag_part], 0)
    last = first.T / length
    inner = np.arange(width)
    angle = 2 * np.pi * (np.outer(inner, inner) % width) / width
    cosine, sine = np.cos(angle), np.sin(angle)
    second = np.block([[cosine, sine], [-sine, cosine]])
    third = np.block([[cosine, -sine], [sine, cosine]])
    first_hi, first_lo = hi_lo(first)
    second_hi, second_lo = hi_lo(second)
    third_hi, third_lo = hi_lo(third)
    last_hi, last_lo = hi_lo(last)
    turn = np.zeros((half_rows // 8 + 1, width, LANES), np.float32)
    for block in range(half_rows // 8 + 1):
        angle = 2 * np.pi * np.outer(inner, 8 * block + np.arange(8)) / length
        turn[block, :, :8] = np.cos(angle)
        turn[block, :, 8:16] = np.sin(angle)
    return (
        np.concatenate([first_hi, first_lo], 1),
        np.concatenate([second_hi, second_lo, second_hi], 1),
        np.concatenate([third_hi, third_lo], 1),
        np.concatenate([last_hi, last_lo], 1),
        turn,
    )


def pack_input_kernel(signal_ref, gate_ref, out_ref):
    rows = signal_ref.shape[0] // 2
    for block in range(signal_ref.shape[1] // LANES):
        lanes = pl.ds(block * LANES, LANES)
        gated = signal_ref[:, lanes].astype(F32) * gate_ref[:, lanes].astype(F32)
        first, second = swap_halves(gated[:rows], gated[rows:])
        out_ref[2 * block] = first.astype(BF16)
        out_ref[2 * block + 1] = second.astype(BF16)


def pack_input(signal, input_gate, parts):
    tok_rows, channels = signal.shape
    wide = 4 * LANES
    return pl.pallas_call(
        pack_input_kernel,
        out_shape=jax.ShapeDtypeStruct((parts, tok_rows // 2, LANES), BF16),
        grid=(channels // wide,),
        in_specs=[pl.BlockSpec((tok_rows, wide), lambda b: (0, b))] * 2,
        out_specs=pl.BlockSpec((8, tok_rows // 2, LANES), lambda b: (b, 0, 0)),
        cost_estimate=pl.CostEstimate(
            flops=signal.size, bytes_accessed=6 * signal.size, transcendentals=0
        ),
        name="pack_input",
    )(signal, input_gate)


def pack_filter_kernel(first_low_ref, filter_ref, out_ref, *, middle):
    share, width = filter_ref.shape[1:3]
    row = lax.broadcasted_iota(jnp.int32, (width, width), 0)
    col = lax.broadcasted_iota(jnp.int32, (width, width), 1)
    for low in range(share):
        mirrored = first_low_ref[1] + low > middle
        order = jnp.where(col == jnp.where(mirrored, width - 1 - row, row), 1.0, 0.0).astype(BF16)
        sign = jnp.where(mirrored, -1.0, 1.0).astype(F32)
        for block in range(filter_ref.shape[3] // LANES):
            lanes = pl.ds(block * LANES, LANES)
            both = jnp.concatenate(
                [filter_ref[0, low, :, lanes], filter_ref[1, low, :, lanes]], 1
            ).astype(BF16)
            both = jnp.dot(order, both, preferred_element_type=F32)
            first, second = swap_halves(both[:, :LANES], sign * both[:, LANES:])
            rows = pl.ds(low * width, width)
            out_ref[2 * block, rows, :] = first.astype(BF16)
            out_ref[2 * block + 1, rows, :] = second.astype(BF16)


def pack_filter(filter_spectrum, groups, devices_seq):
    _, low, width, channels = filter_spectrum.shape
    share = low // groups
    group = lax.axis_index("groups")
    first_low = lax.axis_index("seq") * low + group * share
    wide = 2 * LANES
    chunks = wide // HALF
    size = share * width * channels
    return pl.pallas_call(
        functools.partial(pack_filter_kernel, middle=low * devices_seq // 2),
        out_shape=jax.ShapeDtypeStruct((channels // HALF, share * width, LANES), BF16),
        grid_spec=pltpu.PrefetchScalarGridSpec(
            num_scalar_prefetch=1,
            grid=(channels // wide,),
            in_specs=[pl.BlockSpec((2, share, width, wide), lambda b, at: (0, at[0], 0, b))],
            out_specs=pl.BlockSpec((chunks, share * width, LANES), lambda b, at: (b, 0, 0)),
        ),
        cost_estimate=pl.CostEstimate(
            flops=4 * width * size, bytes_accessed=12 * size, transcendentals=0
        ),
        name="pack_filter",
    )(jnp.stack([group, first_low]), filter_spectrum)


def split_bf16(values):
    high = values.astype(BF16)
    return high, (values - high.astype(F32)).astype(BF16)


def forward_kernel(
    got_ref, first_ref, second_ref, turn_ref, out_ref, top_ref, rows_ref, stage_ref, *, devices_seq
):
    width = turn_ref.shape[1]
    half_rows = rows_ref.shape[0] // width
    full_rows = 2 * half_rows
    piece = got_ref.shape[1]
    for source in range(devices_seq):
        first, second = swap_halves(
            got_ref[source].astype(F32), got_ref[devices_seq + source].astype(F32)
        )
        rows_ref[pl.ds(2 * source * piece, piece), :] = first
        rows_ref[pl.ds((2 * source + 1) * piece, piece), :] = second
    first_matrix = first_ref[...]
    second_matrix = second_ref[...]

    def first_stage(step, carry):
        for u in range(0, 8, 2):
            pair = jnp.concatenate(
                [
                    rows_ref[pl.ds(8 * step + u + v, half_rows, stride=width), :].astype(BF16)
                    for v in range(2)
                ],
                1,
            )
            pair = jnp.concatenate([pair, pair], 0)
            done = jnp.dot(first_matrix, pair, preferred_element_type=F32)
            for v in range(2):
                at = pl.multiple_of((8 * step + u + v) * full_rows, full_rows)
                stage_ref[pl.ds(at, full_rows), :] = done[:, v * LANES : (v + 1) * LANES]
        return carry

    lax.fori_loop(0, width // 8, first_stage, 0)

    def turned(real, imag, block, u):
        cosine = turn_ref[block, :, u : u + 1]
        sine = turn_ref[block, :, 8 + u : 9 + u]
        if imag is None:
            return jnp.concatenate([real * cosine, -real * sine], 0)
        return jnp.concatenate([real * cosine + imag * sine, imag * cosine - real * sine], 0)

    def transform(values):
        high, low = split_bf16(values)
        return jnp.dot(
            second_matrix, jnp.concatenate([high, high, low], 0), preferred_element_type=F32
        )

    def second_stage(block, carry):
        for u in range(0, 8, 2):
            pair = []
            for v in range(u, u + 2):
                at = 8 * block + v
                real = stage_ref[pl.ds(at, width, stride=full_rows), :]
                imag = stage_ref[pl.ds(half_rows + at, width, stride=full_rows), :]
                if v == 0:
                    imag = imag * jnp.where(block == 0, 0.0, 1.0).astype(F32)
                pair.append(turned(real, imag, block, v))
            done = transform(jnp.concatenate(pair, 1))
            for v in range(2):
                out_ref[8 * block + u + v] = done[:, v * LANES : (v + 1) * LANES]
        return carry

    lax.fori_loop(0, half_rows // 8, second_stage, 0)
    real = stage_ref[pl.ds(half_rows, width, stride=full_rows), :]
    top_ref[...] = transform(turned(real, None, half_rows // 8, 0))


def forward(got, devices_seq, width):
    half_rows = got.shape[0] * got.shape[1] // width
    first, second, _, _, turn = tables(half_rows, width)
    return pl.pallas_call(
        functools.partial(forward_kernel, devices_seq=devices_seq),
        out_shape=(
            jax.ShapeDtypeStruct((half_rows, 2 * width, LANES), F32),
            jax.ShapeDtypeStruct((2 * width, LANES), F32),
        ),
        scratch_shapes=[
            pltpu.VMEM((half_rows * width, LANES), F32),
            pltpu.VMEM((2 * half_rows * width, LANES), F32),
        ],
        compiler_params=pltpu.CompilerParams(vmem_limit_bytes=32 << 20),
        cost_estimate=pl.CostEstimate(
            flops=2 * LANES * (first.size * width + second.size * half_rows),
            bytes_accessed=2 * got.size + 8 * half_rows * width * LANES,
            transcendentals=0,
        ),
        name="forward",
    )(got, first, second, turn)


def inverse_kernel(
    spec_ref, top_ref, filter_ref, third_ref, last_ref, turn_ref, out_ref,
    real_ref, imag_ref, rows_ref, *, devices_seq, share
):
    width = turn_ref.shape[1]
    half_rows = spec_ref.shape[0]
    third_matrix = third_ref[...]
    last_matrix = last_ref[...]
    per_source = 2 * share
    left = left_lanes(width)

    def place(source, at):
        return (at // share) * devices_seq * share + source * share + at % share

    def filtered(spec, response):
        turned = pltpu.roll(response, HALF, 1)
        real_part = jnp.where(left, response, turned)
        imag_part = jnp.where(left, turned, response)
        real, imag = spec[:width], spec[width:]
        return jnp.concatenate(
            [real * real_part - imag * imag_part, real * imag_part + imag * real_part], 0
        ).astype(BF16)

    def transform(values):
        return jnp.dot(
            third_matrix, jnp.concatenate([values, values], 0), preferred_element_type=F32
        )

    def turned_back(values, block, u):
        cosine = turn_ref[block, :, u : u + 1]
        sine = turn_ref[block, :, 8 + u : 9 + u]
        real, imag = values[:width], values[width:]
        return real * cosine - imag * sine, real * sine + imag * cosine

    def third_stage(block, carry):
        for u in range(0, per_source, 2):
            pair = []
            for v in range(u, u + 2):
                response = filter_ref[place(block, v)].astype(F32)
                if v == 0:
                    source = jnp.where(block == 0, 0, devices_seq - block)
                    mirror = filter_ref[place(source, 0)].astype(F32)
                    mirror = mirror * jnp.where(block == 0, 0.0, 1.0).astype(F32)
                else:
                    mirror = filter_ref[place(devices_seq - 1 - block, per_source - v)].astype(F32)
                pair.append(filtered(spec_ref[per_source * block + v], response + mirror))
            done = transform(jnp.concatenate(pair, 1))
            for v in range(2):
                real, imag = turned_back(done[:, v * LANES : (v + 1) * LANES], block, u + v)
                at = pl.multiple_of((per_source * block + u + v) * width, width)
                real_ref[pl.ds(at, width), :] = real
                imag_ref[pl.ds(at, width), :] = imag
        return carry

    lax.fori_loop(0, half_rows // per_source, third_stage, 0)
    top_block = half_rows // per_source
    response = filter_ref[place(top_block, 0)].astype(F32)
    done = transform(filtered(top_ref[...], response))
    imag_ref[pl.ds(0, width), :] = turned_back(done, top_block, 0)[0]

    def last_stage(step, carry):
        for u in range(0, 8, 2):
            pair = []
            for v in range(u, u + 2):
                rows = pl.ds(8 * step + v, half_rows, stride=width)
                pair.append(jnp.concatenate([real_ref[rows, :], imag_ref[rows, :]], 0).astype(BF16))
            pair = jnp.concatenate(pair, 1)
            done = jnp.dot(
                last_matrix, jnp.concatenate([pair, pair], 0), preferred_element_type=F32
            )
            for v in range(2):
                rows = pl.ds(8 * step + u + v, half_rows, stride=width)
                rows_ref[rows, :] = done[:, v * LANES : (v + 1) * LANES]
        return carry

    lax.fori_loop(0, width // 8, last_stage, 0)
    piece = out_ref.shape[1]
    for source in range(devices_seq):
        first, second = swap_halves(
            rows_ref[pl.ds(2 * source * piece, piece), :],
            rows_ref[pl.ds((2 * source + 1) * piece, piece), :],
        )
        out_ref[source] = first.astype(BF16)
        out_ref[devices_seq + source] = second.astype(BF16)


def inverse(spectrum, top, arrived, devices_seq, share, piece):
    half_rows, rows, _ = spectrum.shape
    width = rows // 2
    _, _, third, last, turn = tables(half_rows, width)
    return pl.pallas_call(
        functools.partial(inverse_kernel, devices_seq=devices_seq, share=share),
        out_shape=jax.ShapeDtypeStruct((2 * devices_seq, piece, LANES), BF16),
        scratch_shapes=[pltpu.VMEM((half_rows * width, LANES), F32)] * 3,
        compiler_params=pltpu.CompilerParams(vmem_limit_bytes=32 << 20),
        cost_estimate=pl.CostEstimate(
            flops=2 * LANES * (third.size * half_rows + last.size * width),
            bytes_accessed=4 * spectrum.size + 2 * arrived.size,
            transcendentals=0,
        ),
        name="inverse",
    )(spectrum, top, arrived, third, last, turn)


def mix_kernel(conv_ref, signal_ref, gate_ref, out_gate_ref, gain_ref, out_ref):
    rows = signal_ref.shape[0] // 2
    for block in range(signal_ref.shape[1] // LANES):
        lanes = pl.ds(block * LANES, LANES)
        gain = gain_ref[:, lanes]
        halves = swap_halves(
            conv_ref[2 * block].astype(F32), conv_ref[2 * block + 1].astype(F32)
        )
        for half, convolved in enumerate(halves):
            at = pl.ds(half * rows, rows)
            gated = signal_ref[at, lanes].astype(F32) * gate_ref[at, lanes].astype(F32)
            gated = gated.astype(BF16).astype(F32)
            mixed = out_gate_ref[at, lanes].astype(F32) * (convolved + gain * gated)
            out_ref[at, lanes] = mixed.astype(BF16)


def mix(conv, signal, input_gate, output_gate, skip_gain):
    tok_rows, channels = signal.shape
    wide = 4 * LANES
    block = pl.BlockSpec((tok_rows, wide), lambda b: (0, b))
    return pl.pallas_call(
        mix_kernel,
        out_shape=jax.ShapeDtypeStruct(signal.shape, BF16),
        grid=(channels // wide,),
        in_specs=[
            pl.BlockSpec((8, tok_rows // 2, LANES), lambda b: (b, 0, 0)),
            block,
            block,
            block,
            pl.BlockSpec((1, wide), lambda b: (0, b)),
        ],
        out_specs=block,
        cost_estimate=pl.CostEstimate(
            flops=4 * signal.size, bytes_accessed=10 * signal.size, transcendentals=0
        ),
        name="mix",
    )(conv, signal, input_gate, output_gate, skip_gain[None, :])


def spread_kernels(signal, input_gate, output_gate, filter_spectrum, skip_gain):
    groups = lax.axis_size("groups")
    devices_seq = lax.axis_size("seq")
    low, high = filter_spectrum.shape[1:3]
    share = low // groups
    piece = signal.shape[0] // 2
    got = exchange(pack_input(signal, input_gate, groups * devices_seq))
    arrived = exchange(pack_filter(filter_spectrum, groups, devices_seq))
    spectrum, top = forward(got, devices_seq, high)
    conv = inverse(
        spectrum, top, arrived.reshape(-1, high, LANES), devices_seq, share, piece
    )
    return mix(exchange(conv), signal, input_gate, output_gate, skip_gain)


def angle_table(rows_count, cols_count, length):
    row_index = lax.iota(jnp.int32, rows_count)
    col_index = lax.iota(jnp.int32, cols_count)
    product = row_index[:, None] * col_index[None, :] % length
    angles = product.astype(jnp.float32) * (2.0 * math.pi / length)
    return (jnp.cos(angles), jnp.sin(angles))


def contract_first(matrix, values):
    return jnp.einsum("kn,nbc->kbc", matrix, values, precision=lax.Precision.HIGH)


def contract_second(matrix, values):
    return jnp.einsum("kn,anc->akc", matrix, values, precision=lax.Precision.HIGH)


def convolve(signal_rows, spectra_real, spectra_imag):
    half_rows, width, _ = signal_rows.shape
    full_rows = 2 * half_rows
    length = full_rows * width
    cos_one, sin_one = angle_table(full_rows, half_rows, full_rows)
    cos_two, sin_two = angle_table(width, width, width)
    turn_cos, turn_sin = angle_table(full_rows, width, length)
    turn_cos = turn_cos[:, :, None]
    turn_sin = turn_sin[:, :, None]
    first_real = contract_first(cos_one, signal_rows)
    first_imag = -contract_first(sin_one, signal_rows)
    twist_real = first_real * turn_cos + first_imag * turn_sin
    twist_imag = first_imag * turn_cos - first_real * turn_sin
    spec_real = contract_second(cos_two, twist_real) + contract_second(sin_two, twist_imag)
    spec_imag = contract_second(cos_two, twist_imag) - contract_second(sin_two, twist_real)
    prod_real = spec_real * spectra_real - spec_imag * spectra_imag
    prod_imag = spec_real * spectra_imag + spec_imag * spectra_real
    back_real = contract_second(cos_two, prod_real) - contract_second(sin_two, prod_imag)
    back_imag = contract_second(sin_two, prod_real) + contract_second(cos_two, prod_imag)
    rotated_real = back_real * turn_cos - back_imag * turn_sin
    rotated_imag = back_real * turn_sin + back_imag * turn_cos
    summed = contract_first(cos_one.T, rotated_real) - contract_first(sin_one.T, rotated_imag)
    return summed * (1.0 / length)


def spread_plain(signal, input_gate, output_gate, filter_spectrum, skip_gain):
    tok_rows, channels = signal.shape
    groups = lax.axis_size("groups")
    devices_seq = lax.axis_size("seq")
    parts = groups * devices_seq
    width = channels // parts
    low, high = filter_spectrum.shape[1:3]
    share = low // groups
    gated_input = (input_gate.astype(jnp.float32) * signal.astype(jnp.float32)).astype(jnp.bfloat16)

    sent = gated_input.reshape(tok_rows, parts, width).transpose(1, 0, 2).reshape(parts, -1, 128)
    got = exchange(sent).reshape(groups, devices_seq, tok_rows, width)
    rows = got.transpose(1, 2, 0, 3).reshape(-1, high, groups * width)

    mine = lax.dynamic_slice_in_dim(filter_spectrum, lax.axis_index("groups") * share, share, axis=1)
    mine = mine.astype(jnp.bfloat16).reshape(2, share, high, parts, width)
    mine = mine.transpose(3, 0, 1, 2, 4).reshape(parts, -1, 128)
    spectra = exchange(mine).reshape(groups, devices_seq, 2, share, high, width)
    spectra = spectra.transpose(2, 1, 0, 3, 4, 5).reshape(2, -1, high, 1, width)
    spectra = jnp.broadcast_to(spectra, spectra.shape[:3] + (groups, width))
    spectra = spectra.reshape(2, -1, high, groups * width).astype(jnp.float32)

    conv = convolve(rows.astype(jnp.float32), spectra[0], spectra[1]).astype(jnp.bfloat16)
    conv = conv.reshape(devices_seq, tok_rows, groups, width).transpose(2, 0, 1, 3)
    back = exchange(conv.reshape(parts, -1, 128)).reshape(parts, tok_rows, width)
    convolved = back.transpose(1, 0, 2).reshape(tok_rows, channels).astype(jnp.float32)
    mixed_out = output_gate.astype(jnp.float32) * (
        convolved + skip_gain[None, :] * gated_input.astype(jnp.float32)
    )
    return mixed_out.astype(jnp.bfloat16)


def on_device(signal, input_gate, output_gate, filter_spectrum, skip_gain):
    groups = lax.axis_size("groups")
    devices_seq = lax.axis_size("seq")
    tok_rows, channels = signal.shape
    low, high = filter_spectrum.shape[1:3]
    fits = (
        groups == 2
        and channels == groups * devices_seq * HALF
        and low == 8
        and tok_rows == low * high // 2
        and tok_rows % 32 == 0
        and devices_seq % 2 == 0
    )
    plan = spread_kernels if fits else spread_plain
    return plan(signal, input_gate, output_gate, filter_spectrum, skip_gain)


def solution(mesh):
    return jax.shard_map(
        on_device,
        mesh=mesh,
        in_specs=(P(EVERY, None), P(EVERY, None), P(EVERY, None), P(None, "seq", None, None), P()),
        out_specs=P(EVERY, None),
        check_vma=False,
    )
```

profile of v0, /device:TPU:0, one launch (start us, length us, event | category | flops | bytes accessed | tf_op | source)
XLA Modules:
  0.0 135.9 jit_solution(18215919487842463654)
XLA Ops:
  0.0 3.8 %pack_input.1 = bf16[32,128,128]{2,1,0:T(8,128)(2,1)} custom-call(bf16[256,2048]{1,0:T(8,128)(2,1)} %signal_ref.3, bf16[256,2048]{1,0:T(8,128)(2,1)} %gate_ref.3), custom_call_target="tpu_custom_call" | custom-call | flops 524288 | bytes 3145728 | tf_op jit(solution)/shard_map/pack_input/pallas_call | solution.py:88
  3.8 7.3 %all-to-all-start = ((bf16[32,128,128]{2,1,0:T(8,128)(2,1)}), bf16[32,128,128]{2,1,0:T(8,128)(2,1)S(1)}, u32[]{:S(2)}, u32[]{:S(2)}) async-start(bf16[32,128,128]{2,1,0:T(8,128)(2,1)} %pack_input.1), calls=%async_computation | async-start | bytes 2097152 | tf_op jit(solution)/shard_map/all_to_all | solution.py:21
  11.1 0.6 pad_add_fusion.first_low_ref
  11.7 0.0 copy-start.2
  11.7 7.9 %pack_filter.1 = bf16[32,256,128]{2,1,0:T(8,128)(2,1)} custom-call(s32[2]{0:T(128)} %pad_add_fusion.first_low_ref, f32[2,8,64,2048]{3,2,1,0:T(8,128)} %filter_ref.1), custom_call_target="tpu_custom_call" | custom-call | flops 134217728 | bytes 6291456 | tf_op jit(solution)/shard_map/pack_filter/pallas_call | solution.py:129
  19.6 0.0 copy-start.3
  19.6 0.0 copy-start.6
  19.6 18.7 %all-to-all-done.got_ref = bf16[32,128,128]{2,1,0:T(8,128)(2,1)S(1)} async-done(((bf16[32,128,128]{2,1,0:T(8,128)(2,1)}), bf16[32,128,128]{2,1,0:T(8,128)(2,1)S(1)}, u32[]{:S(2)}, u32[]{:S(2)}) %all-to-all-start) | async-done | bytes 1048608 | tf_op jit(solution)/shard_map/all_to_all | solution.py:21
  38.3 2.7 %all-to-all-start.1 = ((bf16[32,256,128]{2,1,0:T(8,128)(2,1)}), bf16[32,256,128]{2,1,0:T(8,128)(2,1)S(1)}, u32[]{:S(2)}, u32[]{:S(2)}) async-start(bf16[32,256,128]{2,1,0:T(8,128)(2,1)} %pack_filter.1), calls=%async_computation.1 | async-start | bytes 4194304 | tf_op jit(solution)/shard_map/all_to_all | solution.py:21
  41.0 0.0 copy-done.2
  41.0 0.0 copy-start.7
  41.0 0.9 copy-done.7
  41.9 0.0 copy-start.8
  41.9 0.8 copy-done.8
  42.7 8.3 %forward.1 = (f32[64,128,128]{2,1,0:T(8,128)S(1)}, f32[128,128]{1,0:T(8,128)S(1)}) custom-call(bf16[32,128,128]{2,1,0:T(8,128)(2,1)S(1)} %all-to-all-done.got_ref, bf16[128,128]{1,0:T(8,128)(2,1)S(1)} %copy-done.8, bf16[128,384]{1,0:T(8,128)(2,1)S(1)} %copy-done.7, f32[9,64,128]{2,1,0:T(8,128)S(1)} %copy-done.2), custom_call_target="tpu_custom_call" | custom-call | flops 1073741824 | bytes 5242880 | tf_op jit(solution)/shard_map/forward/pallas_call | solution.py:220
  51.0 0.0 copy-start
  51.0 1.9 %copy-done = f32[64,128,128]{2,1,0:T(8,128)} copy-done((f32[64,128,128]{2,1,0:T(8,128)}, f32[64,128,128]{2,1,0:T(8,128)S(1)}, u32[]{:S(2)}) %copy-start) | copy-done | bytes 4194328
  53.0 0.0 copy-start.4
  53.0 0.6 copy-done.4
  53.6 37.6 %all-to-all-done.1 = bf16[32,256,128]{2,1,0:T(8,128)(2,1)S(1)} async-done(((bf16[32,256,128]{2,1,0:T(8,128)(2,1)}), bf16[32,256,128]{2,1,0:T(8,128)(2,1)S(1)}, u32[]{:S(2)}, u32[]{:S(2)}) %all-to-all-start.1) | async-done | bytes 2097184 | tf_op jit(solution)/shard_map/all_to_all | solution.py:21
  91.2 0.0 copy-done.3
  91.2 0.0 copy-done.6
  91.2 0.0 copy-start.1
  91.2 2.2 %copy-done.1 = f32[64,128,128]{2,1,0:T(8,128)S(1)} copy-done((f32[64,128,128]{2,1,0:T(8,128)S(1)}, f32[64,128,128]{2,1,0:T(8,128)}, u32[]{:S(2)}) %copy-start.1) | copy-done | bytes 4194328
  93.4 0.0 copy-start.5
  93.4 0.8 copy-done.5
  94.2 7.8 %inverse.1 = bf16[32,128,128]{2,1,0:T(8,128)(2,1)S(1)} custom-call(f32[64,128,128]{2,1,0:T(8,128)S(1)} %copy-done.1, f32[128,128]{1,0:T(8,128)S(1)} %copy-done.5, bf16[128,64,128]{2,1,0:T(8,128)(2,1)S(1)} %bitcast.4, bf16[128,256]{1,0:T(8,128)(2,1)S(1)} %copy-done.3, bf16[64,256]{1,0:T(8,128)(2,1)S(1)} %copy-done.6, f32[9,64,128]{2,1,0:T(8,128)S(1)} %copy-done.2), custom_call_target="tpu_custom_call" | custom-call | flops 805306368 | bytes 6291456 | tf_op jit(solution)/shard_map/inverse/pallas_call | solution.py:330
  102.0 29.6 %all_to_all.15.conv_ref = bf16[32,128,128]{2,1,0:T(8,128)(2,1)} all-to-all(bf16[32,128,128]{2,1,0:T(8,128)(2,1)S(1)} %inverse.1), channel_id=1, replica_groups=mesh['groups'=2,'seq'=16] {'groups','seq'}, dimensions={0} | all-to-all | bytes 2097152 | tf_op jit(solution)/shard_map/all_to_all | solution.py:21
  131.6 4.4 %mix.1 = bf16[256,2048]{1,0:T(8,128)(2,1)} custom-call(bf16[32,128,128]{2,1,0:T(8,128)(2,1)} %all_to_all.15.conv_ref, bf16[256,2048]{1,0:T(8,128)(2,1)} %signal_ref.3, bf16[256,2048]{1,0:T(8,128)(2,1)} %gate_ref.3, bf16[256,2048]{1,0:T(8,128)(2,1)} %out_gate_ref.1, f32[1,2048]{1,0:T(1,128)} %bitcast.5), custom_call_target="tpu_custom_call" | custom-call | flops 2097152 | bytes 5242880 | tf_op jit(solution)/shard_map/mix/pallas_call | solution.py:364
Async XLA Ops:
  3.8 34.5 %all-to-all-start = ((bf16[32,128,128]{2,1,0:T(8,128)(2,1)}), bf16[32,128,128]{2,1,0:T(8,128)(2,1)S(1)}, u32[]{:S(2)}, u32[]{:S(2)}) async-start(bf16[32,128,128]{2,1,0:T(8,128)(2,1)} %pack_input.1), calls=%async_computation | async-start | bytes 2097152 | tf_op jit(solution)/shard_map/all_to_all | solution.py:21
  11.7 29.3 %copy-start.2 = (f32[9,64,128]{2,1,0:T(8,128)S(1)}, f32[9,64,128]{2,1,0:T(8,128)}, u32[]{:S(2)}) copy-start(f32[9,64,128]{2,1,0:T(8,128)} %constant.25.clone.turn_ref) | copy-start | bytes 884740
  19.6 71.6 %copy-start.3 = (bf16[128,256]{1,0:T(8,128)(2,1)S(1)}, bf16[128,256]{1,0:T(8,128)(2,1)}, u32[]{:S(2)}) copy-start(bf16[128,256]{1,0:T(8,128)(2,1)} %constant.26.clone.third_ref) | copy-start | bytes 196612
  19.6 71.6 %copy-start.6 = (bf16[64,256]{1,0:T(8,128)(2,1)S(1)}, bf16[64,256]{1,0:T(8,128)(2,1)}, u32[]{:S(2)}) copy-start(bf16[64,256]{1,0:T(8,128)(2,1)} %constant.27.clone.last_ref) | copy-start | bytes 98308
  38.3 52.9 %all-to-all-start.1 = ((bf16[32,256,128]{2,1,0:T(8,128)(2,1)}), bf16[32,256,128]{2,1,0:T(8,128)(2,1)S(1)}, u32[]{:S(2)}, u32[]{:S(2)}) async-start(bf16[32,256,128]{2,1,0:T(8,128)(2,1)} %pack_filter.1), calls=%async_computation.1 | async-start | bytes 4194304 | tf_op jit(solution)/shard_map/all_to_all | solution.py:21
  41.0 0.9 copy-start.7
  41.9 0.8 copy-start.8
  51.0 1.9 %copy-start = (f32[64,128,128]{2,1,0:T(8,128)}, f32[64,128,128]{2,1,0:T(8,128)S(1)}, u32[]{:S(2)}) copy-start(f32[64,128,128]{2,1,0:T(8,128)S(1)} %get-tuple-element.7.spec_ref) | copy-start | bytes 12582916
  53.0 0.6 copy-start.4
  91.2 2.2 %copy-start.1 = (f32[64,128,128]{2,1,0:T(8,128)S(1)}, f32[64,128,128]{2,1,0:T(8,128)}, u32[]{:S(2)}) copy-start(f32[64,128,128]{2,1,0:T(8,128)} %copy-done) | copy-start | bytes 12582916
  93.4 0.8 copy-start.5
where the time goes:
time: 137 us; the launch traced here: 136 us
  waiting for transfers between devices  56.3 us (41%)
  Pallas kernels  32.1 us (23%)
  blocking collectives  29.6 us (22%)
  starting transfers between devices  10 us (7%)
  local copies, waits for them, and re-layouts  7.25 us (5%)
    all_to_all x2, waiting for transfers between devices, exchange(): lax.all_to_all(values, EVERY, split_axis=0, concat_axis=0, tiled=True)  56.3 us
    all_to_all x1, blocking collectives, exchange(): lax.all_to_all(values, EVERY, split_axis=0, concat_axis=0, tiled=True)  29.6 us
    all_to_all x2, starting transfers between devices, exchange(): lax.all_to_all(values, EVERY, split_axis=0, concat_axis=0, tiled=True)  10 us
    pallas_call x1, Pallas kernels, forward(): pl.pallas_call(functools.partial(forward_kernel, devices_seq=devices_seq)...  8.34 us
    pallas_call x1, Pallas kernels, pack_filter(): pl.pallas_call(functools.partial(pack_filter_kernel, middle=low * devices...  7.88 us
    pallas_call x1, Pallas kernels, inverse(): pl.pallas_call(functools.partial(inverse_kernel, devices_seq=devices_seq,...  7.78 us
    unnamed x18, local copies, waits for them, and re-layouts  7.25 us
    pallas_call x1, Pallas kernels, mix(): pl.pallas_call(mix_kernel, out_shape=jax.ShapeDtypeStruct(signal.shape, B...  4.36 us
  transfers between devices with their start and end apart: 2, of which 2 were waited for; matrix products, arithmetic and copies ran while one was open for 0% of the time, Pallas kernels for 12%

commit v1 on v0

--- a/solution.py
+++ b/solution.py
@@ -13,6 +13,7 @@
 EVERY = ("groups", "seq")
 LANES = 128
 HALF = LANES // 2
+PAD = 8
 BF16 = jnp.bfloat16
 F32 = jnp.float32
 
@@ -84,13 +85,13 @@
 
 def pack_input(signal, input_gate, parts):
     tok_rows, channels = signal.shape
-    wide = 4 * LANES
+    wide = 8 * LANES
     return pl.pallas_call(
         pack_input_kernel,
         out_shape=jax.ShapeDtypeStruct((parts, tok_rows // 2, LANES), BF16),
         grid=(channels // wide,),
         in_specs=[pl.BlockSpec((tok_rows, wide), lambda b: (0, b))] * 2,
-        out_specs=pl.BlockSpec((8, tok_rows // 2, LANES), lambda b: (b, 0, 0)),
+        out_specs=pl.BlockSpec((16, tok_rows // 2, LANES), lambda b: (b, 0, 0)),
         cost_estimate=pl.CostEstimate(
             flops=signal.size, bytes_accessed=6 * signal.size, transcendentals=0
         ),
@@ -123,7 +124,7 @@
     share = low // groups
     group = lax.axis_index("groups")
     first_low = lax.axis_index("seq") * low + group * share
-    wide = 2 * LANES
+    wide = 8 * LANES
     chunks = wide // HALF
     size = share * width * channels
     return pl.pallas_call(
@@ -151,15 +152,21 @@
     got_ref, first_ref, second_ref, turn_ref, out_ref, top_ref, rows_ref, stage_ref, *, devices_seq
 ):
     width = turn_ref.shape[1]
-    half_rows = rows_ref.shape[0] // width
+    half_rows = out_ref.shape[0]
     full_rows = 2 * half_rows
-    piece = got_ref.shape[1]
+    pitch = width + PAD
+    tall = full_rows + PAD
+    lines = got_ref.shape[1] // width
     for source in range(devices_seq):
-        first, second = swap_halves(
-            got_ref[source].astype(F32), got_ref[devices_seq + source].astype(F32)
-        )
-        rows_ref[pl.ds(2 * source * piece, piece), :] = first
-        rows_ref[pl.ds((2 * source + 1) * piece, piece), :] = second
+        for line in range(lines):
+            at = pl.ds(line * width, width)
+            halves = swap_halves(
+                got_ref[source, at, :].astype(F32),
+                got_ref[devices_seq + source, at, :].astype(F32),
+            )
+            for half in range(2):
+                row = (2 * source + half) * lines + line
+                rows_ref[pl.ds(row * pitch, width), :] = halves[half]
     first_matrix = first_ref[...]
     second_matrix = second_ref[...]
 
@@ -167,7 +174,7 @@
         for u in range(0, 8, 2):
             pair = jnp.concatenate(
                 [
-                    rows_ref[pl.ds(8 * step + u + v, half_rows, stride=width), :].astype(BF16)
+                    rows_ref[pl.ds(8 * step + u + v, half_rows, stride=pitch), :].astype(BF16)
                     for v in range(2)
                 ],
                 1,
@@ -175,7 +182,7 @@
             pair = jnp.concatenate([pair, pair], 0)
             done = jnp.dot(first_matrix, pair, preferred_element_type=F32)
             for v in range(2):
-                at = pl.multiple_of((8 * step + u + v) * full_rows, full_rows)
+                at = pl.multiple_of((8 * step + u + v) * tall, PAD)
                 stage_ref[pl.ds(at, full_rows), :] = done[:, v * LANES : (v + 1) * LANES]
         return carry
 
@@ -199,8 +206,8 @@
             pair = []
             for v in range(u, u + 2):
                 at = 8 * block + v
-                real = stage_ref[pl.ds(at, width, stride=full_rows), :]
-                imag = stage_ref[pl.ds(half_rows + at, width, stride=full_rows), :]
+                real = stage_ref[pl.ds(at, width, stride=tall), :]
+                imag = stage_ref[pl.ds(half_rows + at, width, stride=tall), :]
                 if v == 0:
                     imag = imag * jnp.where(block == 0, 0.0, 1.0).astype(F32)
                 pair.append(turned(real, imag, block, v))
@@ -210,7 +217,7 @@
         return carry
 
     lax.fori_loop(0, half_rows // 8, second_stage, 0)
-    real = stage_ref[pl.ds(half_rows, width, stride=full_rows), :]
+    real = stage_ref[pl.ds(half_rows, width, stride=tall), :]
     top_ref[...] = transform(turned(real, None, half_rows // 8, 0))
 
 
@@ -224,10 +231,10 @@
             jax.ShapeDtypeStruct((2 * width, LANES), F32),
         ),
         scratch_shapes=[
-            pltpu.VMEM((half_rows * width, LANES), F32),
-            pltpu.VMEM((2 * half_rows * width, LANES), F32),
+            pltpu.VMEM((half_rows * (width + PAD), LANES), F32),
+            pltpu.VMEM((width * (2 * half_rows + PAD), LANES), F32),
         ],
-        compiler_params=pltpu.CompilerParams(vmem_limit_bytes=32 << 20),
+        compiler_params=pltpu.CompilerParams(vmem_limit_bytes=16 << 20),
         cost_estimate=pl.CostEstimate(
             flops=2 * LANES * (first.size * width + second.size * half_rows),
             bytes_accessed=2 * got.size + 8 * half_rows * width * LANES,
@@ -238,15 +245,23 @@
 
 
 def inverse_kernel(
-    spec_ref, top_ref, filter_ref, third_ref, last_ref, turn_ref, out_ref,
-    real_ref, imag_ref, rows_ref, *, devices_seq, share
+    spec_hbm, top_ref, filter_ref, third_ref, last_ref, turn_ref, out_ref,
+    spec_ref, real_ref, imag_ref, rows_ref, sems, *, devices_seq, share
 ):
     width = turn_ref.shape[1]
     half_rows = spec_ref.shape[0]
+    pitch = width + PAD
     third_matrix = third_ref[...]
     last_matrix = last_ref[...]
     per_source = 2 * share
     left = left_lanes(width)
+
+    def fetch(block):
+        at = pl.ds(per_source * block, per_source)
+        return pltpu.make_async_copy(spec_hbm.at[at], spec_ref.at[at], sems.at[block])
+
+    for block in range(half_rows // per_source):
+        fetch(block).start()
 
     def place(source, at):
         return (at // share) * devices_seq * share + source * share + at % share
@@ -272,6 +287,7 @@
         return real * cosine - imag * sine, real * sine + imag * cosine
 
     def third_stage(block, carry):
+        fetch(block).wait()
         for u in range(0, per_source, 2):
             pair = []
             for v in range(u, u + 2):
@@ -286,12 +302,12 @@
             done = transform(jnp.concatenate(pair, 1))
             for v in range(2):
                 real, imag = turned_back(done[:, v * LANES : (v + 1) * LANES], block, u + v)
-                at = pl.multiple_of((per_source * block + u + v) * width, width)
+                at = pl.multiple_of((per_source * block + u + v) * pitch, PAD)
                 real_ref[pl.ds(at, width), :] = real
                 imag_ref[pl.ds(at, width), :] = imag
         return carry
 
-    lax.fori_loop(0, half_rows // per_source, third_stage, 0)
+    lax.fori_loop(0, half_rows // per_source, third_stage, 0, unroll=True)
     top_block = half_rows // per_source
     response = filter_ref[place(top_block, 0)].astype(F32)
     done = transform(filtered(top_ref[...], response))
@@ -301,26 +317,30 @@
         for u in range(0, 8, 2):
             pair = []
             for v in range(u, u + 2):
-                rows = pl.ds(8 * step + v, half_rows, stride=width)
+                rows = pl.ds(8 * step + v, half_rows, stride=pitch)
                 pair.append(jnp.concatenate([real_ref[rows, :], imag_ref[rows, :]], 0).astype(BF16))
             pair = jnp.concatenate(pair, 1)
             done = jnp.dot(
                 last_matrix, jnp.concatenate([pair, pair], 0), preferred_element_type=F32
             )
             for v in range(2):
-                rows = pl.ds(8 * step + u + v, half_rows, stride=width)
+                rows = pl.ds(8 * step + u + v, half_rows, stride=pitch)
                 rows_ref[rows, :] = done[:, v * LANES : (v + 1) * LANES]
         return carry
 
-    lax.fori_loop(0, width // 8, last_stage, 0)
-    piece = out_ref.shape[1]
+    lax.fori_loop(0, width // 8, last_stage, 0, unroll=True)
+    lines = out_ref.shape[1] // width
     for source in range(devices_seq):
-        first, second = swap_halves(
-            rows_ref[pl.ds(2 * source * piece, piece), :],
-            rows_ref[pl.ds((2 * source + 1) * piece, piece), :],
-        )
-        out_ref[source] = first.astype(BF16)
-        out_ref[devices_seq + source] = second.astype(BF16)
+        for line in range(lines):
+            first, second = swap_halves(
+                *(
+                    rows_ref[pl.ds(((2 * source + half) * lines + line) * pitch, width), :]
+                    for half in range(2)
+                )
+            )
+            at = pl.ds(line * width, width)
+            out_ref[source, at, :] = first.astype(BF16)
+            out_ref[devices_seq + source, at, :] = second.astype(BF16)
 
 
 def inverse(spectrum, top, arrived, devices_seq, share, piece):
@@ -330,8 +350,12 @@
     return pl.pallas_call(
         functools.partial(inverse_kernel, devices_seq=devices_seq, share=share),
         out_shape=jax.ShapeDtypeStruct((2 * devices_seq, piece, LANES), BF16),
-        scratch_shapes=[pltpu.VMEM((half_rows * width, LANES), F32)] * 3,
-        compiler_params=pltpu.CompilerParams(vmem_limit_bytes=32 << 20),
+        in_specs=[pl.BlockSpec(memory_space=pl.ANY)]
+        + [pl.BlockSpec(memory_space=pltpu.VMEM)] * 5,
+        scratch_shapes=[pltpu.VMEM(spectrum.shape, F32)]
+        + [pltpu.VMEM((half_rows * (width + PAD), LANES), F32)] * 3
+        + [pltpu.SemaphoreType.DMA((half_rows // (2 * share),))],
+        compiler_params=pltpu.CompilerParams(vmem_limit_bytes=16 << 20),
         cost_estimate=pl.CostEstimate(
             flops=2 * LANES * (third.size * half_rows + last.size * width),
             bytes_accessed=4 * spectrum.size + 2 * arrived.size,
@@ -359,14 +383,14 @@
 
 def mix(conv, signal, input_gate, output_gate, skip_gain):
     tok_rows, channels = signal.shape
-    wide = 4 * LANES
+    wide = 8 * LANES
     block = pl.BlockSpec((tok_rows, wide), lambda b: (0, b))
     return pl.pallas_call(
         mix_kernel,
         out_shape=jax.ShapeDtypeStruct(signal.shape, BF16),
         grid=(channels // wide,),
         in_specs=[
-            pl.BlockSpec((8, tok_rows // 2, LANES), lambda b: (b, 0, 0)),
+            pl.BlockSpec((16, tok_rows // 2, LANES), lambda b: (b, 0, 0)),
             block,
             block,
             block,

time: 137 us -> 131 us (0.956)
  Pallas kernels: 32.1 us -> 22.1 us
  waiting for transfers between devices: 56.3 us -> 61.2 us
    all_to_all x2, waiting for transfers between devices: 56.3 us -> 61.2 us  [exchange(): lax.all_to_all(values, EVERY, split_axis=0, concat_axis=0, tiled=True)]
    pallas_call x1, Pallas kernels: 7.88 us -> 4.57 us  [pack_filter(): pl.pallas_call(functools.partial(pack_filter_kernel, middle=low * devices...]
    pallas_call x1, Pallas kernels: 7.78 us -> 4.82 us  [inverse(): pl.pallas_call(functools.partial(inverse_kernel, devices_seq=devices_seq,...]
    pallas_call x1, Pallas kernels: 8.34 us -> 6.7 us  [forward(): pl.pallas_call(functools.partial(forward_kernel, devices_seq=devices_seq)...]
  transfers between devices with their start and end apart: 2 -> 2, of which waited for: 2 -> 2; matrix products, arithmetic and copies ran while one was open for 0% -> 0% of each run, Pallas kernels for 12% -> 9%
where the time goes in v1:
time: 131 us
  waiting for transfers between devices  61.2 us (47%)
  blocking collectives  29.6 us (23%)
  Pallas kernels  22.1 us (17%)
  starting transfers between devices  10 us (8%)
  local copies, waits for them, and re-layouts  7.25 us (6%)
    all_to_all x2, waiting for transfers between devices, exchange(): lax.all_to_all(values, EVERY, split_axis=0, concat_axis=0, tiled=True)  61.2 us
    all_to_all x1, blocking collectives, exchange(): lax.all_to_all(values, EVERY, split_axis=0, concat_axis=0, tiled=True)  29.6 us
    all_to_all x2, starting transfers between devices, exchange(): lax.all_to_all(values, EVERY, split_axis=0, concat_axis=0, tiled=True)  10 us
    unnamed x18, local copies, waits for them, and re-layouts  7.25 us
    pallas_call x1, Pallas kernels, forward(): pl.pallas_call(functools.partial(forward_kernel, devices_seq=devices_seq)...  6.7 us
    pallas_call x1, Pallas kernels, inverse(): pl.pallas_call(functools.partial(inverse_kernel, devices_seq=devices_seq,...  4.82 us
    pallas_call x1, Pallas kernels, pack_filter(): pl.pallas_call(functools.partial(pack_filter_kernel, middle=low * devices...  4.57 us
    pallas_call x1, Pallas kernels, mix(): pl.pallas_call(mix_kernel, out_shape=jax.ShapeDtypeStruct(signal.shape, B...  3.46 us
  transfers between devices with their start and end apart: 2, of which 2 were waited for; matrix products, arithmetic and copies ran while one was open for 0% of the time, Pallas kernels for 9%

profile of v1, /device:TPU:0, one launch (start us, length us, event | category | flops | bytes accessed | tf_op | source)
XLA Modules:
  0.0 130.8 jit_solution(17435698821054956760)
XLA Ops:
  0.0 2.6 %pack_input.1 = bf16[32,128,128]{2,1,0:T(8,128)(2,1)} custom-call(bf16[256,2048]{1,0:T(8,128)(2,1)} %signal_ref.3, bf16[256,2048]{1,0:T(8,128)(2,1)} %gate_ref.3), custom_call_target="tpu_custom_call" | custom-call | flops 524288 | bytes 3145728 | tf_op jit(solution)/shard_map/pack_input/pallas_call | solution.py:89
  2.6 7.3 %all-to-all-start = ((bf16[32,128,128]{2,1,0:T(8,128)(2,1)}), bf16[32,128,128]{2,1,0:T(8,128)(2,1)S(1)}, u32[]{:S(2)}, u32[]{:S(2)}) async-start(bf16[32,128,128]{2,1,0:T(8,128)(2,1)} %pack_input.1), calls=%async_computation | async-start | bytes 2097152 | tf_op jit(solution)/shard_map/all_to_all | solution.py:22
  9.9 0.6 pad_add_fusion.first_low_ref
  10.5 0.0 copy-start.2
  10.5 4.6 %pack_filter.1 = bf16[32,256,128]{2,1,0:T(8,128)(2,1)} custom-call(s32[2]{0:T(128)} %pad_add_fusion.first_low_ref, f32[2,8,64,2048]{3,2,1,0:T(8,128)} %filter_ref.1), custom_call_target="tpu_custom_call" | custom-call | flops 134217728 | bytes 6291456 | tf_op jit(solution)/shard_map/pack_filter/pallas_call | solution.py:130
  15.1 0.0 copy-start.3
  15.1 0.0 copy-start.6
  15.1 22.0 %all-to-all-done.got_ref = bf16[32,128,128]{2,1,0:T(8,128)(2,1)S(1)} async-done(((bf16[32,128,128]{2,1,0:T(8,128)(2,1)}), bf16[32,128,128]{2,1,0:T(8,128)(2,1)S(1)}, u32[]{:S(2)}, u32[]{:S(2)}) %all-to-all-start) | async-done | bytes 1048608 | tf_op jit(solution)/shard_map/all_to_all | solution.py:22
  37.1 2.7 %all-to-all-start.1 = ((bf16[32,256,128]{2,1,0:T(8,128)(2,1)}), bf16[32,256,128]{2,1,0:T(8,128)(2,1)S(1)}, u32[]{:S(2)}, u32[]{:S(2)}) async-start(bf16[32,256,128]{2,1,0:T(8,128)(2,1)} %pack_filter.1), calls=%async_computation.1 | async-start | bytes 4194304 | tf_op jit(solution)/shard_map/all_to_all | solution.py:22
  39.8 0.0 copy-done.2
  39.8 0.0 copy-start.7
  39.8 0.9 copy-done.7
  40.7 0.0 copy-start.8
  40.7 0.8 copy-done.8
  41.5 6.7 %forward.1 = (f32[64,128,128]{2,1,0:T(8,128)S(1)}, f32[128,128]{1,0:T(8,128)S(1)}) custom-call(bf16[32,128,128]{2,1,0:T(8,128)(2,1)S(1)} %all-to-all-done.got_ref, bf16[128,128]{1,0:T(8,128)(2,1)S(1)} %copy-done.8, bf16[128,384]{1,0:T(8,128)(2,1)S(1)} %copy-done.7, f32[9,64,128]{2,1,0:T(8,128)S(1)} %copy-done.2), custom_call_target="tpu_custom_call" | custom-call | flops 1073741824 | bytes 5242880 | tf_op jit(solution)/shard_map/forward/pallas_call | solution.py:227
  48.2 0.0 copy-start
  48.2 1.9 %copy-done = f32[64,128,128]{2,1,0:T(8,128)} copy-done((f32[64,128,128]{2,1,0:T(8,128)}, f32[64,128,128]{2,1,0:T(8,128)S(1)}, u32[]{:S(2)}) %copy-start) | copy-done | bytes 4194328
  50.1 0.0 copy-start.4
  50.1 0.6 copy-done.4
  50.7 39.2 %all-to-all-done.1 = bf16[32,256,128]{2,1,0:T(8,128)(2,1)S(1)} async-done(((bf16[32,256,128]{2,1,0:T(8,128)(2,1)}), bf16[32,256,128]{2,1,0:T(8,128)(2,1)S(1)}, u32[]{:S(2)}, u32[]{:S(2)}) %all-to-all-start.1) | async-done | bytes 2097184 | tf_op jit(solution)/shard_map/all_to_all | solution.py:22
  90.0 0.0 copy-done.3
  90.0 0.0 copy-done.6
  90.0 0.0 copy-start.1
  90.0 2.2 %copy-done.1 = f32[64,128,128]{2,1,0:T(8,128)S(1)} copy-done((f32[64,128,128]{2,1,0:T(8,128)S(1)}, f32[64,128,128]{2,1,0:T(8,128)}, u32[]{:S(2)}) %copy-start.1) | copy-done | bytes 4194328
  92.1 0.0 copy-start.5
  92.1 0.8 copy-done.5
  93.0 4.8 %inverse.1 = bf16[32,128,128]{2,1,0:T(8,128)(2,1)S(1)} custom-call(f32[64,128,128]{2,1,0:T(8,128)S(1)} %copy-done.1, f32[128,128]{1,0:T(8,128)S(1)} %copy-done.5, bf16[128,64,128]{2,1,0:T(8,128)(2,1)S(1)} %bitcast.4, bf16[128,256]{1,0:T(8,128)(2,1)S(1)} %copy-done.3, bf16[64,256]{1,0:T(8,128)(2,1)S(1)} %copy-done.6, f32[9,64,128]{2,1,0:T(8,128)S(1)} %copy-done.2), custom_call_target="tpu_custom_call" | custom-call | flops 805306368 | bytes 6291456 | tf_op jit(solution)/shard_map/inverse/pallas_call | solution.py:350
  97.8 29.6 %all_to_all.15.conv_ref = bf16[32,128,128]{2,1,0:T(8,128)(2,1)} all-to-all(bf16[32,128,128]{2,1,0:T(8,128)(2,1)S(1)} %inverse.1), channel_id=1, replica_groups=mesh['groups'=2,'seq'=16] {'groups','seq'}, dimensions={0} | all-to-all | bytes 2097152 | tf_op jit(solution)/shard_map/all_to_all | solution.py:22
  127.4 3.5 %mix.1 = bf16[256,2048]{1,0:T(8,128)(2,1)} custom-call(bf16[32,128,128]{2,1,0:T(8,128)(2,1)} %all_to_all.15.conv_ref, bf16[256,2048]{1,0:T(8,128)(2,1)} %signal_ref.3, bf16[256,2048]{1,0:T(8,128)(2,1)} %gate_ref.3, bf16[256,2048]{1,0:T(8,128)(2,1)} %out_gate_ref.1, f32[1,2048]{1,0:T(1,128)} %bitcast.5), custom_call_target="tpu_custom_call" | custom-call | flops 2097152 | bytes 5242880 | tf_op jit(solution)/shard_map/mix/pallas_call | solution.py:388
Async XLA Ops:
  2.6 34.5 %all-to-all-start = ((bf16[32,128,128]{2,1,0:T(8,128)(2,1)}), bf16[32,128,128]{2,1,0:T(8,128)(2,1)S(1)}, u32[]{:S(2)}, u32[]{:S(2)}) async-start(bf16[32,128,128]{2,1,0:T(8,128)(2,1)} %pack_input.1), calls=%async_computation | async-start | bytes 2097152 | tf_op jit(solution)/shard_map/all_to_all | solution.py:22
  10.5 29.3 %copy-start.2 = (f32[9,64,128]{2,1,0:T(8,128)S(1)}, f32[9,64,128]{2,1,0:T(8,128)}, u32[]{:S(2)}) copy-start(f32[9,64,128]{2,1,0:T(8,128)} %constant.25.clone.turn_ref) | copy-start | bytes 884740
  15.1 74.9 %copy-start.3 = (bf16[128,256]{1,0:T(8,128)(2,1)S(1)}, bf16[128,256]{1,0:T(8,128)(2,1)}, u32[]{:S(2)}) copy-start(bf16[128,256]{1,0:T(8,128)(2,1)} %constant.26.clone.third_ref) | copy-start | bytes 196612
  15.1 74.9 %copy-start.6 = (bf16[64,256]{1,0:T(8,128)(2,1)S(1)}, bf16[64,256]{1,0:T(8,128)(2,1)}, u32[]{:S(2)}) copy-start(bf16[64,256]{1,0:T(8,128)(2,1)} %constant.27.clone.last_ref) | copy-start | bytes 98308
  37.1 52.9 %all-to-all-start.1 = ((bf16[32,256,128]{2,1,0:T(8,128)(2,1)}), bf16[32,256,128]{2,1,0:T(8,128)(2,1)S(1)}, u32[]{:S(2)}, u32[]{:S(2)}) async-start(bf16[32,256,128]{2,1,0:T(8,128)(2,1)} %pack_filter.1), calls=%async_computation.1 | async-start | bytes 4194304 | tf_op jit(solution)/shard_map/all_to_all | solution.py:22
  39.8 0.9 copy-start.7
  40.7 0.8 copy-start.8
  48.2 1.9 %copy-start = (f32[64,128,128]{2,1,0:T(8,128)}, f32[64,128,128]{2,1,0:T(8,128)S(1)}, u32[]{:S(2)}) copy-start(f32[64,128,128]{2,1,0:T(8,128)S(1)} %get-tuple-element.7.spec_hbm) | copy-start | bytes 12582916
  50.1 0.6 copy-start.4
  90.0 2.2 %copy-start.1 = (f32[64,128,128]{2,1,0:T(8,128)S(1)}, f32[64,128,128]{2,1,0:T(8,128)}, u32[]{:S(2)}) copy-start(f32[64,128,128]{2,1,0:T(8,128)} %copy-done) | copy-start | bytes 12582916
  92.1 0.8 copy-start.5

commit v2 on v1

--- a/solution.py
+++ b/solution.py
@@ -11,6 +11,7 @@
 from jax.sharding import PartitionSpec as P
 
 EVERY = ("groups", "seq")
+PAIRS = ("seq", "groups")
 LANES = 128
 HALF = LANES // 2
 PAD = 8
@@ -18,8 +19,8 @@
 F32 = jnp.float32
 
 
-def exchange(values):
-    return lax.all_to_all(values, EVERY, split_axis=0, concat_axis=0, tiled=True)
+def exchange(values, axes=EVERY):
+    return lax.all_to_all(values, axes, split_axis=0, concat_axis=0, tiled=True)
 
 
 def left_lanes(rows):
@@ -67,8 +68,7 @@
     return (
         np.concatenate([first_hi, first_lo], 1),
         np.concatenate([second_hi, second_lo, second_hi], 1),
-        np.concatenate([third_hi, third_lo], 1),
-        np.concatenate([last_hi, last_lo], 1),
+        np.block([[third_hi, third_lo], [last_hi, last_lo]]),
         turn,
     )
 
@@ -79,19 +79,19 @@
         lanes = pl.ds(block * LANES, LANES)
         gated = signal_ref[:, lanes].astype(F32) * gate_ref[:, lanes].astype(F32)
         first, second = swap_halves(gated[:rows], gated[rows:])
-        out_ref[2 * block] = first.astype(BF16)
-        out_ref[2 * block + 1] = second.astype(BF16)
-
-
-def pack_input(signal, input_gate, parts):
+        out_ref[2 * block, 0] = first.astype(BF16)
+        out_ref[2 * block + 1, 0] = second.astype(BF16)
+
+
+def pack_input(signal, input_gate, devices_seq):
     tok_rows, channels = signal.shape
-    wide = 8 * LANES
+    wide = channels // 2
     return pl.pallas_call(
         pack_input_kernel,
-        out_shape=jax.ShapeDtypeStruct((parts, tok_rows // 2, LANES), BF16),
-        grid=(channels // wide,),
+        out_shape=jax.ShapeDtypeStruct((devices_seq, 2, tok_rows // 2, LANES), BF16),
+        grid=(2,),
         in_specs=[pl.BlockSpec((tok_rows, wide), lambda b: (0, b))] * 2,
-        out_specs=pl.BlockSpec((16, tok_rows // 2, LANES), lambda b: (b, 0, 0)),
+        out_specs=pl.BlockSpec((devices_seq, 1, tok_rows // 2, LANES), lambda b: (0, b, 0, 0)),
         cost_estimate=pl.CostEstimate(
             flops=signal.size, bytes_accessed=6 * signal.size, transcendentals=0
         ),
@@ -119,28 +119,34 @@
             out_ref[2 * block + 1, rows, :] = second.astype(BF16)
 
 
-def pack_filter(filter_spectrum, groups, devices_seq):
+def pack_filter(filter_spectrum, devices_seq):
     _, low, width, channels = filter_spectrum.shape
-    share = low // groups
     group = lax.axis_index("groups")
-    first_low = lax.axis_index("seq") * low + group * share
-    wide = 8 * LANES
-    chunks = wide // HALF
-    size = share * width * channels
+    wide = 4 * LANES
+    steps = channels // 2 // wide
+    size = low * width * channels // 2
     return pl.pallas_call(
         functools.partial(pack_filter_kernel, middle=low * devices_seq // 2),
-        out_shape=jax.ShapeDtypeStruct((channels // HALF, share * width, LANES), BF16),
+        out_shape=jax.ShapeDtypeStruct((devices_seq, low * width, LANES), BF16),
         grid_spec=pltpu.PrefetchScalarGridSpec(
             num_scalar_prefetch=1,
-            grid=(channels // wide,),
-            in_specs=[pl.BlockSpec((2, share, width, wide), lambda b, at: (0, at[0], 0, b))],
-            out_specs=pl.BlockSpec((chunks, share * width, LANES), lambda b, at: (b, 0, 0)),
+            grid=(steps,),
+            in_specs=[
+                pl.BlockSpec(
+                    (2, low, width, wide), lambda b, at: (0, 0, 0, at[0] * steps + b)
+                )
+            ],
+            out_specs=pl.BlockSpec((wide // HALF, low * width, LANES), lambda b, at: (b, 0, 0)),
         ),
+        compiler_params=pltpu.CompilerParams(vmem_limit_bytes=16 << 20),
         cost_estimate=pl.CostEstimate(
             flops=4 * width * size, bytes_accessed=12 * size, transcendentals=0
         ),
         name="pack_filter",
-    )(jnp.stack([group, first_low]), filter_spectrum)
+    )(
+        jnp.stack([group, lax.axis_index("seq") * low]),
+        pltpu.with_memory_space_constraint(filter_spectrum, pltpu.HBM),
+    )
 
 
 def split_bf16(values):
@@ -149,20 +155,19 @@
 
 
 def forward_kernel(
-    got_ref, first_ref, second_ref, turn_ref, out_ref, top_ref, rows_ref, stage_ref, *, devices_seq
+    got_ref, first_ref, second_ref, turn_ref, out_ref, rows_ref, stage_ref, *, devices_seq
 ):
     width = turn_ref.shape[1]
-    half_rows = out_ref.shape[0]
+    half_rows = out_ref.shape[0] - 1
     full_rows = 2 * half_rows
     pitch = width + PAD
     tall = full_rows + PAD
-    lines = got_ref.shape[1] // width
+    lines = got_ref.shape[2] // width
     for source in range(devices_seq):
         for line in range(lines):
             at = pl.ds(line * width, width)
             halves = swap_halves(
-                got_ref[source, at, :].astype(F32),
-                got_ref[devices_seq + source, at, :].astype(F32),
+                got_ref[source, 0, at, :].astype(F32), got_ref[source, 1, at, :].astype(F32)
             )
             for half in range(2):
                 row = (2 * source + half) * lines + line
@@ -218,18 +223,15 @@
 
     lax.fori_loop(0, half_rows // 8, second_stage, 0)
     real = stage_ref[pl.ds(half_rows, width, stride=tall), :]
-    top_ref[...] = transform(turned(real, None, half_rows // 8, 0))
+    out_ref[half_rows] = transform(turned(real, None, half_rows // 8, 0))
 
 
 def forward(got, devices_seq, width):
-    half_rows = got.shape[0] * got.shape[1] // width
-    first, second, _, _, turn = tables(half_rows, width)
+    half_rows = got.size // (LANES * width)
+    first, second, _, turn = tables(half_rows, width)
     return pl.pallas_call(
         functools.partial(forward_kernel, devices_seq=devices_seq),
-        out_shape=(
-            jax.ShapeDtypeStruct((half_rows, 2 * width, LANES), F32),
-            jax.ShapeDtypeStruct((2 * width, LANES), F32),
-        ),
+        out_shape=jax.ShapeDtypeStruct((half_rows + 1, 2 * width, LANES), F32),
         scratch_shapes=[
             pltpu.VMEM((half_rows * (width + PAD), LANES), F32),
             pltpu.VMEM((width * (2 * half_rows + PAD), LANES), F32),
@@ -245,26 +247,29 @@
 
 
 def inverse_kernel(
-    spec_hbm, top_ref, filter_ref, third_ref, last_ref, turn_ref, out_ref,
-    spec_ref, real_ref, imag_ref, rows_ref, sems, *, devices_seq, share
+    spec_hbm, matrices_hbm, filter_ref, turn_ref, out_ref,
+    spec_ref, matrices_ref, real_ref, imag_ref, rows_ref, sems, *, devices_seq
 ):
     width = turn_ref.shape[1]
-    half_rows = spec_ref.shape[0]
+    half_rows = spec_ref.shape[0] - 1
     pitch = width + PAD
-    third_matrix = third_ref[...]
-    last_matrix = last_ref[...]
-    per_source = 2 * share
+    per_source = 8
     left = left_lanes(width)
 
-    def fetch(block):
-        at = pl.ds(per_source * block, per_source)
+    top_block = half_rows // per_source
+
+    def fetch(block, count=per_source):
+        at = pl.ds(per_source * block, count)
         return pltpu.make_async_copy(spec_hbm.at[at], spec_ref.at[at], sems.at[block])
 
-    for block in range(half_rows // per_source):
+    matrices = pltpu.make_async_copy(matrices_hbm, matrices_ref, sems.at[top_block + 1])
+    matrices.start()
+    for block in range(top_block):
         fetch(block).start()
-
-    def place(source, at):
-        return (at // share) * devices_seq * share + source * share + at % share
+    fetch(top_block, 1).start()
+    matrices.wait()
+    third_matrix = matrices_ref[: 2 * width]
+    last_matrix = matrices_ref[2 * width :]
 
     def filtered(spec, response):
         turned = pltpu.roll(response, HALF, 1)
@@ -291,13 +296,13 @@
         for u in range(0, per_source, 2):
             pair = []
             for v in range(u, u + 2):
-                response = filter_ref[place(block, v)].astype(F32)
+                response = filter_ref[per_source * block + v].astype(F32)
                 if v == 0:
-                    source = jnp.where(block == 0, 0, devices_seq - block)
-                    mirror = filter_ref[place(source, 0)].astype(F32)
+                    at = jnp.where(block == 0, 0, 2 * half_rows - per_source * block)
+                    mirror = filter_ref[at].astype(F32)
                     mirror = mirror * jnp.where(block == 0, 0.0, 1.0).astype(F32)
                 else:
-                    mirror = filter_ref[place(devices_seq - 1 - block, per_source - v)].astype(F32)
+                    mirror = filter_ref[2 * half_rows - per_source * block - v].astype(F32)
                 pair.append(filtered(spec_ref[per_source * block + v], response + mirror))
             done = transform(jnp.concatenate(pair, 1))
             for v in range(2):
@@ -308,9 +313,9 @@
         return carry
 
     lax.fori_loop(0, half_rows // per_source, third_stage, 0, unroll=True)
-    top_block = half_rows // per_source
-    response = filter_ref[place(top_block, 0)].astype(F32)
-    done = transform(filtered(top_ref[...], response))
+    fetch(top_block, 1).wait()
+    response = filter_ref[half_rows].astype(F32)
+    done = transform(filtered(spec_ref[half_rows], response))
     imag_ref[pl.ds(0, width), :] = turned_back(done, top_block, 0)[0]
 
     def last_stage(step, carry):
@@ -329,7 +334,7 @@
         return carry
 
     lax.fori_loop(0, width // 8, last_stage, 0, unroll=True)
-    lines = out_ref.shape[1] // width
+    lines = out_ref.shape[2] // width
     for source in range(devices_seq):
         for line in range(lines):
             first, second = swap_halves(
@@ -339,30 +344,35 @@
                 )
             )
             at = pl.ds(line * width, width)
-            out_ref[source, at, :] = first.astype(BF16)
-            out_ref[devices_seq + source, at, :] = second.astype(BF16)
-
-
-def inverse(spectrum, top, arrived, devices_seq, share, piece):
-    half_rows, rows, _ = spectrum.shape
-    width = rows // 2
-    _, _, third, last, turn = tables(half_rows, width)
+            out_ref[source, 0, at, :] = first.astype(BF16)
+            out_ref[source, 1, at, :] = second.astype(BF16)
+
+
+def inverse(spectrum, arrived, devices_seq, piece):
+    width = spectrum.shape[1] // 2
+    half_rows = spectrum.shape[0] - 1
+    _, _, matrices, turn = tables(half_rows, width)
     return pl.pallas_call(
-        functools.partial(inverse_kernel, devices_seq=devices_seq, share=share),
-        out_shape=jax.ShapeDtypeStruct((2 * devices_seq, piece, LANES), BF16),
-        in_specs=[pl.BlockSpec(memory_space=pl.ANY)]
-        + [pl.BlockSpec(memory_space=pltpu.VMEM)] * 5,
-        scratch_shapes=[pltpu.VMEM(spectrum.shape, F32)]
+        functools.partial(inverse_kernel, devices_seq=devices_seq),
+        out_shape=jax.ShapeDtypeStruct((devices_seq, 2, piece, LANES), BF16),
+        in_specs=[pl.BlockSpec(memory_space=pltpu.HBM)] * 2
+        + [pl.BlockSpec(memory_space=pltpu.VMEM)] * 2,
+        scratch_shapes=[pltpu.VMEM(spectrum.shape, F32), pltpu.VMEM(matrices.shape, BF16)]
         + [pltpu.VMEM((half_rows * (width + PAD), LANES), F32)] * 3
-        + [pltpu.SemaphoreType.DMA((half_rows // (2 * share),))],
-        compiler_params=pltpu.CompilerParams(vmem_limit_bytes=16 << 20),
+        + [pltpu.SemaphoreType.DMA((half_rows // 8 + 2,))],
+        compiler_params=pltpu.CompilerParams(vmem_limit_bytes=20 << 20),
         cost_estimate=pl.CostEstimate(
-            flops=2 * LANES * (third.size * half_rows + last.size * width),
+            flops=2 * LANES * matrices.size * width,
             bytes_accessed=4 * spectrum.size + 2 * arrived.size,
             transcendentals=0,
         ),
         name="inverse",
-    )(spectrum, top, arrived, third, last, turn)
+    )(
+        pltpu.with_memory_space_constraint(spectrum, pltpu.HBM),
+        pltpu.with_memory_space_constraint(jnp.asarray(matrices), pltpu.HBM),
+        arrived,
+        turn,
+    )
 
 
 def mix_kernel(conv_ref, signal_ref, gate_ref, out_gate_ref, gain_ref, out_ref):
@@ -370,8 +380,9 @@
     for block in range(signal_ref.shape[1] // LANES):
         lanes = pl.ds(block * LANES, LANES)
         gain = gain_ref[:, lanes]
+        place = divmod(2 * block, conv_ref.shape[0])
         halves = swap_halves(
-            conv_ref[2 * block].astype(F32), conv_ref[2 * block + 1].astype(F32)
+            conv_ref[place[1], place[0]].astype(F32), conv_ref[place[1] + 1, place[0]].astype(F32)
         )
         for half, convolved in enumerate(halves):
             at = pl.ds(half * rows, rows)
@@ -382,21 +393,11 @@
 
 
 def mix(conv, signal, input_gate, output_gate, skip_gain):
-    tok_rows, channels = signal.shape
-    wide = 8 * LANES
-    block = pl.BlockSpec((tok_rows, wide), lambda b: (0, b))
     return pl.pallas_call(
         mix_kernel,
         out_shape=jax.ShapeDtypeStruct(signal.shape, BF16),
-        grid=(channels // wide,),
-        in_specs=[
-            pl.BlockSpec((16, tok_rows // 2, LANES), lambda b: (b, 0, 0)),
-            block,
-            block,
-            block,
-            pl.BlockSpec((1, wide), lambda b: (0, b)),
-        ],
-        out_specs=block,
+        in_specs=[pl.BlockSpec(memory_space=pltpu.VMEM)] * 5,
+        compiler_params=pltpu.CompilerParams(vmem_limit_bytes=16 << 20),
         cost_estimate=pl.CostEstimate(
             flops=4 * signal.size, bytes_accessed=10 * signal.size, transcendentals=0
         ),
@@ -405,18 +406,19 @@
 
 
 def spread_kernels(signal, input_gate, output_gate, filter_spectrum, skip_gain):
-    groups = lax.axis_size("groups")
     devices_seq = lax.axis_size("seq")
-    low, high = filter_spectrum.shape[1:3]
-    share = low // groups
-    piece = signal.shape[0] // 2
-    got = exchange(pack_input(signal, input_gate, groups * devices_seq))
-    arrived = exchange(pack_filter(filter_spectrum, groups, devices_seq))
-    spectrum, top = forward(got, devices_seq, high)
+    width = filter_spectrum.shape[2]
+
+    def pairs(values):
+        return exchange(values.reshape(-1, *values.shape[2:]), PAIRS).reshape(values.shape)
+
+    got = pairs(pack_input(signal, input_gate, devices_seq))
+    arrived = exchange(pack_filter(filter_spectrum, devices_seq), "seq")
+    spectrum = forward(got, devices_seq, width)
     conv = inverse(
-        spectrum, top, arrived.reshape(-1, high, LANES), devices_seq, share, piece
-    )
-    return mix(exchange(conv), signal, input_gate, output_gate, skip_gain)
+        spectrum, arrived.reshape(-1, width, LANES), devices_seq, signal.shape[0] // 2
+    )
+    return mix(pairs(conv), signal, input_gate, output_gate, skip_gain)
 
 
 def angle_table(rows_count, cols_count, length):

time: 131 us -> 127 us (0.969)
  waiting for transfers between devices: 61.2 us -> 53.2 us
  blocking collectives: 29.6 us -> 37.1 us
  local copies, waits for them, and re-layouts: 7.25 us -> 4.1 us
  Pallas kernels: 22.1 us -> 20.6 us
    all_to_all x2, waiting for transfers between devices: 61.2 us -> 53.2 us  [exchange(): return lax.all_to_all(values, axes, split_axis=0, concat_axis=0, tiled=True)]
    all_to_all x1, blocking collectives: 29.6 us -> 37.1 us  [exchange(): return lax.all_to_all(values, axes, split_axis=0, concat_axis=0, tiled=True)]
    unnamed x18, local copies, waits for them, and re-layouts: 7.25 us -> 4.1 us
    pallas_call x1, Pallas kernels: 3.46 us -> 1.98 us  [mix(): pl.pallas_call(mix_kernel, out_shape=jax.ShapeDtypeStruct(signal.shape, B...]
  transfers between devices with their start and end apart: 2 -> 2, of which waited for: 2 -> 2; matrix products, arithmetic and copies ran while one was open for 0% -> 0% of each run, Pallas kernels for 9% -> 8%
where the time goes in v2:
time: 127 us; the launch traced here: 126 us
  waiting for transfers between devices  53.2 us (42%)
  blocking collectives  37.1 us (29%)
  Pallas kernels  20.6 us (16%)
  starting transfers between devices  11.1 us (9%)
  local copies, waits for them, and re-layouts  4.1 us (3%)
    all_to_all x2, waiting for transfers between devices, exchange(): return lax.all_to_all(values, axes, split_axis=0, concat_axis=0, tiled=True)  53.2 us
    all_to_all x1, blocking collectives, exchange(): return lax.all_to_all(values, axes, split_axis=0, concat_axis=0, tiled=True)  37.1 us
    all_to_all x2, starting transfers between devices, exchange(): return lax.all_to_all(values, axes, split_axis=0, concat_axis=0, tiled=True)  11.1 us
    pallas_call x1, Pallas kernels, forward(): pl.pallas_call(functools.partial(forward_kernel, devices_seq=devices_seq)...  6.66 us
    pallas_call x1, Pallas kernels, inverse(): pl.pallas_call(functools.partial(inverse_kernel, devices_seq=devices_seq)...  6.04 us
    unnamed x18, local copies, waits for them, and re-layouts  4.1 us
    pallas_call x1, Pallas kernels, pack_filter(): pl.pallas_call(functools.partial(pack_filter_kernel, middle=low * devices...  3.31 us
    pallas_call x1, Pallas kernels, pack_input(): pl.pallas_call(pack_input_kernel, out_shape=jax.ShapeDtypeStruct((devices...  2.58 us
  transfers between devices with their start and end apart: 2, of which 2 were waited for; matrix products, arithmetic and copies ran while one was open for 0% of the time, Pallas kernels for 8%

profile of v2, /device:TPU:0, one launch (start us, length us, event | category | flops | bytes accessed | tf_op | source)
XLA Modules:
  0.0 126.2 jit_solution(12869802831400811459)
XLA Ops:
  0.0 2.6 %pack_input.1 = bf16[16,2,128,128]{3,2,1,0:T(8,128)(2,1)} custom-call(bf16[256,2048]{1,0:T(8,128)(2,1)} %signal_ref.3, bf16[256,2048]{1,0:T(8,128)(2,1)} %gate_ref.3), custom_call_target="tpu_custom_call" | custom-call | flops 524288 | bytes 3145728 | tf_op jit(solution)/shard_map/pack_input/pallas_call | solution.py:89
  2.6 7.3 %all-to-all-start = ((bf16[32,128,128]{2,1,0:T(8,128)(2,1)}), bf16[32,128,128]{2,1,0:T(8,128)(2,1)S(1)}, u32[]{:S(2)}, u32[]{:S(2)}) async-start(bf16[32,128,128]{2,1,0:T(8,128)(2,1)} %bitcast.13), calls=%async_computation | async-start | bytes 2097152 | tf_op jit(solution)/shard_map/all_to_all | solution.py:23
  9.9 0.1 pad_add_fusion.first_low_ref
  10.0 3.3 %pack_filter.1 = bf16[16,512,128]{2,1,0:T(8,128)(2,1)S(1)} custom-call(s32[2]{0:T(128)S(1)} %pad_add_fusion.first_low_ref, f32[2,8,64,2048]{3,2,1,0:T(8,128)} %filter_ref.1), custom_call_target="tpu_custom_call" | custom-call | flops 134217728 | bytes 6291456 | tf_op jit(solution)/shard_map/pack_filter/pallas_call | solution.py:128
  13.3 0.0 copy-start.1
  13.3 1.3 %copy-done.1 = bf16[16,512,128]{2,1,0:T(8,128)(2,1)} copy-done((bf16[16,512,128]{2,1,0:T(8,128)(2,1)}, bf16[16,512,128]{2,1,0:T(8,128)(2,1)S(1)}, u32[]{:S(2)}) %copy-start.1) | copy-done | bytes 2097176
  14.6 0.0 copy-start.4
  14.6 0.0 copy-start.6
  14.6 21.5 %all-to-all-done = bf16[32,128,128]{2,1,0:T(8,128)(2,1)S(1)} async-done(((bf16[32,128,128]{2,1,0:T(8,128)(2,1)}), bf16[32,128,128]{2,1,0:T(8,128)(2,1)S(1)}, u32[]{:S(2)}, u32[]{:S(2)}) %all-to-all-start) | async-done | bytes 1048608 | tf_op jit(solution)/shard_map/all_to_all | solution.py:23
  36.1 3.8 %all-to-all-start.1 = ((bf16[16,512,128]{2,1,0:T(8,128)(2,1)}), bf16[16,512,128]{2,1,0:T(8,128)(2,1)S(1)}, u32[]{:S(2)}, u32[]{:S(2)}) async-start(bf16[16,512,128]{2,1,0:T(8,128)(2,1)} %copy-done.1), calls=%async_computation.1 | async-start | bytes 4194304 | tf_op jit(solution)/shard_map/all_to_all | solution.py:23
  39.9 0.0 copy-done.4
  39.9 0.0 copy-done.6
  39.9 0.0 copy-start.7
  40.0 0.7 copy-done.7
  40.7 6.7 %forward.1.spec_hbm = f32[65,128,128]{2,1,0:T(8,128)S(1)} custom-call(bf16[16,2,128,128]{3,2,1,0:T(8,128)(2,1)S(1)} %bitcast.10, bf16[128,128]{1,0:T(8,128)(2,1)S(1)} %copy-done.7, bf16[128,384]{1,0:T(8,128)(2,1)S(1)} %copy-done.6, f32[9,64,128]{2,1,0:T(8,128)S(1)} %copy-done.4), custom_call_target="tpu_custom_call" | custom-call | flops 1073741824 | bytes 5242880 | tf_op jit(solution)/shard_map/forward/pallas_call | solution.py:232
  47.4 0.0 copy-start
  47.4 2.0 %copy-done = f32[65,128,128]{2,1,0:T(8,128)} copy-done((f32[65,128,128]{2,1,0:T(8,128)}, f32[65,128,128]{2,1,0:T(8,128)S(1)}, u32[]{:S(2)}) %copy-start) | copy-done | bytes 4259864
  49.4 31.7 %all-to-all-done.1 = bf16[16,512,128]{2,1,0:T(8,128)(2,1)S(1)} async-done(((bf16[16,512,128]{2,1,0:T(8,128)(2,1)}), bf16[16,512,128]{2,1,0:T(8,128)(2,1)S(1)}, u32[]{:S(2)}, u32[]{:S(2)}) %all-to-all-start.1) | async-done | bytes 2097184 | tf_op jit(solution)/shard_map/all_to_all | solution.py:23
  81.0 0.0 copy-start.2
  81.0 0.0 copy-start.3
  81.0 0.0 copy-start.5
  81.0 0.0 copy-start.8
  81.0 6.0 %inverse.1 = bf16[16,2,128,128]{3,2,1,0:T(8,128)(2,1)S(1)} custom-call(f32[65,128,128]{2,1,0:T(8,128)} %copy-done, bf16[192,256]{1,0:T(8,128)(2,1)} %constant.22.clone.matrices_hbm, bf16[128,64,128]{2,1,0:T(8,128)(2,1)S(1)} %bitcast.8, f32[9,64,128]{2,1,0:T(8,128)S(1)} %copy-done.4), custom_call_target="tpu_custom_call" | custom-call | flops 805306368 | bytes 6356992 | tf_op jit(solution)/shard_map/inverse/pallas_call | solution.py:355
  87.1 37.1 %all_to_all.15 = bf16[32,128,128]{2,1,0:T(8,128)(2,1)S(1)} all-to-all(bf16[32,128,128]{2,1,0:T(8,128)(2,1)S(1)} %bitcast.11), channel_id=1, replica_groups=mesh['groups'=2,'seq'=16] {'seq','groups'}, dimensions={0} | all-to-all | bytes 2097152 | tf_op jit(solution)/shard_map/all_to_all | solution.py:23
  124.2 0.0 copy-done.2
  124.2 0.0 copy-done.3
  124.2 0.0 copy-done.5
  124.2 0.0 copy-done.8
  124.2 2.0 %mix.1 = bf16[256,2048]{1,0:T(8,128)(2,1)} custom-call(bf16[16,2,128,128]{3,2,1,0:T(8,128)(2,1)S(1)} %bitcast.9, bf16[256,2048]{1,0:T(8,128)(2,1)S(1)} %copy-done.2, bf16[256,2048]{1,0:T(8,128)(2,1)S(1)} %copy-done.3, bf16[256,2048]{1,0:T(8,128)(2,1)S(1)} %copy-done.5, f32[1,2048]{1,0:T(1,128)S(1)} %bitcast.12), custom_call_target="tpu_custom_call" | custom-call | flops 2097152 | bytes 5242880 | tf_op jit(solution)/shard_map/mix/pallas_call | solution.py:396
Async XLA Ops:
  2.6 33.5 %all-to-all-start = ((bf16[32,128,128]{2,1,0:T(8,128)(2,1)}), bf16[32,128,128]{2,1,0:T(8,128)(2,1)S(1)}, u32[]{:S(2)}, u32[]{:S(2)}) async-start(bf16[32,128,128]{2,1,0:T(8,128)(2,1)} %bitcast.13), calls=%async_computation | async-start | bytes 2097152 | tf_op jit(solution)/shard_map/all_to_all | solution.py:23
  13.3 1.4 %copy-start.1 = (bf16[16,512,128]{2,1,0:T(8,128)(2,1)}, bf16[16,512,128]{2,1,0:T(8,128)(2,1)S(1)}, u32[]{:S(2)}) copy-start(bf16[16,512,128]{2,1,0:T(8,128)(2,1)S(1)} %pack_filter.1) | copy-start | bytes 6291460
  14.6 25.3 %copy-start.4 = (f32[9,64,128]{2,1,0:T(8,128)S(1)}, f32[9,64,128]{2,1,0:T(8,128)}, u32[]{:S(2)}) copy-start(f32[9,64,128]{2,1,0:T(8,128)} %constant.21.clone.turn_ref) | copy-start | bytes 884740
  14.6 25.3 %copy-start.6 = (bf16[128,384]{1,0:T(8,128)(2,1)S(1)}, bf16[128,384]{1,0:T(8,128)(2,1)}, u32[]{:S(2)}) copy-start(bf16[128,384]{1,0:T(8,128)(2,1)} %constant.20.clone.second_ref) | copy-start | bytes 294916
  36.1 44.9 %all-to-all-start.1 = ((bf16[16,512,128]{2,1,0:T(8,128)(2,1)}), bf16[16,512,128]{2,1,0:T(8,128)(2,1)S(1)}, u32[]{:S(2)}, u32[]{:S(2)}) async-start(bf16[16,512,128]{2,1,0:T(8,128)(2,1)} %copy-done.1), calls=%async_computation.1 | async-start | bytes 4194304 | tf_op jit(solution)/shard_map/all_to_all | solution.py:23
  39.9 0.8 copy-start.7
  47.4 2.0 %copy-start = (f32[65,128,128]{2,1,0:T(8,128)}, f32[65,128,128]{2,1,0:T(8,128)S(1)}, u32[]{:S(2)}) copy-start(f32[65,128,128]{2,1,0:T(8,128)S(1)} %forward.1.spec_hbm) | copy-start | bytes 12779524
  81.0 43.1 %copy-start.2 = (bf16[256,2048]{1,0:T(8,128)(2,1)S(1)}, bf16[256,2048]{1,0:T(8,128)(2,1)}, u32[]{:S(2)}) copy-start(bf16[256,2048]{1,0:T(8,128)(2,1)} %signal_ref.3) | copy-start | bytes 3145732
  81.0 43.1 %copy-start.3 = (bf16[256,2048]{1,0:T(8,128)(2,1)S(1)}, bf16[256,2048]{1,0:T(8,128)(2,1)}, u32[]{:S(2)}) copy-start(bf16[256,2048]{1,0:T(8,128)(2,1)} %gate_ref.3) | copy-start | bytes 3145732
  81.0 43.1 %copy-start.5 = (bf16[256,2048]{1,0:T(8,128)(2,1)S(1)}, bf16[256,2048]{1,0:T(8,128)(2,1)}, u32[]{:S(2)}) copy-start(bf16[256,2048]{1,0:T(8,128)(2,1)} %out_gate_ref.1) | copy-start | bytes 3145732
  81.0 43.2 %copy-start.8 = (f32[2048]{0:T(1024)S(1)}, f32[2048]{0:T(1024)}, u32[]{:S(2)}) copy-start(f32[2048]{0:T(1024)} %param.13) | copy-start | bytes 24580

commit v3 on v2

--- a/solution.py
+++ b/solution.py
@@ -99,44 +99,56 @@
     )(signal, input_gate)
 
 
-def pack_filter_kernel(first_low_ref, filter_ref, out_ref, *, middle):
-    share, width = filter_ref.shape[1:3]
+def pack_filter_kernel(place_ref, filter_ref, *refs, middle):
+    out_refs, chunks_ref = refs[:-1], refs[-1]
+    low_count, width = filter_ref.shape[1:3]
+    chunks = chunks_ref.shape[0]
+    seq = place_ref[1]
     row = lax.broadcasted_iota(jnp.int32, (width, width), 0)
     col = lax.broadcasted_iota(jnp.int32, (width, width), 1)
-    for low in range(share):
-        mirrored = first_low_ref[1] + low > middle
+    for low in range(low_count):
+        mirrored = seq * low_count + low > middle
         order = jnp.where(col == jnp.where(mirrored, width - 1 - row, row), 1.0, 0.0).astype(BF16)
         sign = jnp.where(mirrored, -1.0, 1.0).astype(F32)
-        for block in range(filter_ref.shape[3] // LANES):
+        for block in range(chunks // 2):
             lanes = pl.ds(block * LANES, LANES)
             both = jnp.concatenate(
                 [filter_ref[0, low, :, lanes], filter_ref[1, low, :, lanes]], 1
             ).astype(BF16)
             both = jnp.dot(order, both, preferred_element_type=F32)
-            first, second = swap_halves(both[:, :LANES], sign * both[:, LANES:])
+            halves = swap_halves(both[:, :LANES], sign * both[:, LANES:])
             rows = pl.ds(low * width, width)
-            out_ref[2 * block, rows, :] = first.astype(BF16)
-            out_ref[2 * block + 1, rows, :] = second.astype(BF16)
+            for half in range(2):
+                near = (2 * block + half) ^ (seq % chunks)
+                chunks_ref[near, rows, :] = halves[half].astype(BF16)
+    for step in range(len(out_refs) // chunks):
+
+        @pl.when(pl.program_id(0) == step)
+        def _():
+            for near in range(chunks):
+                out_refs[chunks * step + near][...] = chunks_ref[near]
 
 
 def pack_filter(filter_spectrum, devices_seq):
     _, low, width, channels = filter_spectrum.shape
-    group = lax.axis_index("groups")
-    wide = 4 * LANES
-    steps = channels // 2 // wide
+    chunks = 4
+    wide = chunks * HALF
+    steps = devices_seq // chunks
     size = low * width * channels // 2
+    block = (low * width, LANES)
+
+    def lanes_of(step, place):
+        return (0, 0, 0, place[0] * steps + ((place[1] // chunks) ^ step))
+
     return pl.pallas_call(
         functools.partial(pack_filter_kernel, middle=low * devices_seq // 2),
-        out_shape=jax.ShapeDtypeStruct((devices_seq, low * width, LANES), BF16),
+        out_shape=[jax.ShapeDtypeStruct(block, BF16)] * devices_seq,
         grid_spec=pltpu.PrefetchScalarGridSpec(
             num_scalar_prefetch=1,
             grid=(steps,),
-            in_specs=[
-                pl.BlockSpec(
-                    (2, low, width, wide), lambda b, at: (0, 0, 0, at[0] * steps + b)
-                )
-            ],
-            out_specs=pl.BlockSpec((wide // HALF, low * width, LANES), lambda b, at: (b, 0, 0)),
+            in_specs=[pl.BlockSpec((2, low, width, wide), lanes_of)],
+            out_specs=[pl.BlockSpec(block, lambda step, place: (0, 0))] * devices_seq,
+            scratch_shapes=[pltpu.VMEM((chunks, *block), BF16)],
         ),
         compiler_params=pltpu.CompilerParams(vmem_limit_bytes=16 << 20),
         cost_estimate=pl.CostEstimate(
@@ -144,9 +156,14 @@
         ),
         name="pack_filter",
     )(
-        jnp.stack([group, lax.axis_index("seq") * low]),
+        jnp.stack([lax.axis_index("groups"), lax.axis_index("seq")]),
         pltpu.with_memory_space_constraint(filter_spectrum, pltpu.HBM),
     )
+
+
+def swap_with(values, distance):
+    count = lax.axis_size("seq")
+    return lax.ppermute(values, "seq", [(i, i ^ distance) for i in range(count)])
 
 
 def split_bf16(values):
@@ -247,9 +264,11 @@
 
 
 def inverse_kernel(
-    spec_hbm, matrices_hbm, filter_ref, turn_ref, out_ref,
-    spec_ref, matrices_ref, real_ref, imag_ref, rows_ref, sems, *, devices_seq
+    place_ref, spec_hbm, matrices_hbm, *refs, devices_seq
 ):
+    filter_hbm = refs[:devices_seq]
+    turn_ref, out_ref, spec_ref, filter_ref, matrices_ref = refs[devices_seq : devices_seq + 5]
+    real_ref, imag_ref, rows_ref, sems, filter_sems = refs[devices_seq + 5 :]
     width = turn_ref.shape[1]
     half_rows = spec_ref.shape[0] - 1
     pitch = width + PAD
@@ -264,10 +283,24 @@
 
     matrices = pltpu.make_async_copy(matrices_hbm, matrices_ref, sems.at[top_block + 1])
     matrices.start()
-    for block in range(top_block):
+    fetch(0).start()
+    for distance in range(devices_seq):
+        source = place_ref[0] ^ distance
+        pltpu.make_async_copy(
+            filter_hbm[distance], filter_ref.at[source], filter_sems.at[source]
+        ).start()
+    for block in range(1, top_block):
         fetch(block).start()
     fetch(top_block, 1).start()
     matrices.wait()
+
+    def arrival(source):
+        return pltpu.make_async_copy(
+            filter_hbm[0], filter_ref.at[source], filter_sems.at[source]
+        )
+
+    def response_of(low):
+        return filter_ref[low // per_source, pl.ds(low % per_source * width, width), :].astype(F32)
     third_matrix = matrices_ref[: 2 * width]
     last_matrix = matrices_ref[2 * width :]
 
@@ -291,31 +324,26 @@
         real, imag = values[:width], values[width:]
         return real * cosine - imag * sine, real * sine + imag * cosine
 
-    def third_stage(block, carry):
+    for block in range(top_block):
         fetch(block).wait()
+        arrival(block).wait()
+        arrival(devices_seq - 1 - block).wait()
         for u in range(0, per_source, 2):
             pair = []
             for v in range(u, u + 2):
-                response = filter_ref[per_source * block + v].astype(F32)
-                if v == 0:
-                    at = jnp.where(block == 0, 0, 2 * half_rows - per_source * block)
-                    mirror = filter_ref[at].astype(F32)
-                    mirror = mirror * jnp.where(block == 0, 0.0, 1.0).astype(F32)
-                else:
-                    mirror = filter_ref[2 * half_rows - per_source * block - v].astype(F32)
-                pair.append(filtered(spec_ref[per_source * block + v], response + mirror))
+                low = per_source * block + v
+                response = response_of(low)
+                if low:
+                    response = response + response_of(2 * half_rows - low)
+                pair.append(filtered(spec_ref[low], response))
             done = transform(jnp.concatenate(pair, 1))
             for v in range(2):
                 real, imag = turned_back(done[:, v * LANES : (v + 1) * LANES], block, u + v)
-                at = pl.multiple_of((per_source * block + u + v) * pitch, PAD)
-                real_ref[pl.ds(at, width), :] = real
-                imag_ref[pl.ds(at, width), :] = imag
-        return carry
-
-    lax.fori_loop(0, half_rows // per_source, third_stage, 0, unroll=True)
+                at = pl.ds((per_source * block + u + v) * pitch, width)
+                real_ref[at, :] = real
+                imag_ref[at, :] = imag
     fetch(top_block, 1).wait()
-    response = filter_ref[half_rows].astype(F32)
-    done = transform(filtered(spec_ref[half_rows], response))
+    done = transform(filtered(spec_ref[half_rows], response_of(half_rows)))
     imag_ref[pl.ds(0, width), :] = turned_back(done, top_block, 0)[0]
 
     def last_stage(step, carry):
@@ -355,22 +383,29 @@
     return pl.pallas_call(
         functools.partial(inverse_kernel, devices_seq=devices_seq),
         out_shape=jax.ShapeDtypeStruct((devices_seq, 2, piece, LANES), BF16),
-        in_specs=[pl.BlockSpec(memory_space=pltpu.HBM)] * 2
-        + [pl.BlockSpec(memory_space=pltpu.VMEM)] * 2,
-        scratch_shapes=[pltpu.VMEM(spectrum.shape, F32), pltpu.VMEM(matrices.shape, BF16)]
+        in_specs=[pl.BlockSpec(memory_space=pltpu.SMEM)]
+        + [pl.BlockSpec(memory_space=pltpu.HBM)] * (2 + devices_seq)
+        + [pl.BlockSpec(memory_space=pltpu.VMEM)],
+        scratch_shapes=[
+            pltpu.VMEM(spectrum.shape, F32),
+            pltpu.VMEM((devices_seq, *arrived[0].shape), BF16),
+            pltpu.VMEM(matrices.shape, BF16),
+        ]
         + [pltpu.VMEM((half_rows * (width + PAD), LANES), F32)] * 3
-        + [pltpu.SemaphoreType.DMA((half_rows // 8 + 2,))],
+        + [pltpu.SemaphoreType.DMA((half_rows // 8 + 2,)), pltpu.SemaphoreType.DMA((devices_seq,))],
         compiler_params=pltpu.CompilerParams(vmem_limit_bytes=20 << 20),
         cost_estimate=pl.CostEstimate(
             flops=2 * LANES * matrices.size * width,
-            bytes_accessed=4 * spectrum.size + 2 * arrived.size,
+            bytes_accessed=4 * spectrum.size + 2 * devices_seq * arrived[0].size,
             transcendentals=0,
         ),
         name="inverse",
     )(
-        pltpu.with_memory_space_constraint(spectrum, pltpu.HBM),
-        pltpu.with_memory_space_constraint(jnp.asarray(matrices), pltpu.HBM),
-        arrived,
+        lax.axis_index("seq").reshape(1),
+        *(
+            pltpu.with_memory_space_constraint(operand, pltpu.HBM)
+            for operand in (spectrum, jnp.asarray(matrices), *arrived)
+        ),
         turn,
     )
 
@@ -413,11 +448,10 @@
         return exchange(values.reshape(-1, *values.shape[2:]), PAIRS).reshape(values.shape)
 
     got = pairs(pack_input(signal, input_gate, devices_seq))
-    arrived = exchange(pack_filter(filter_spectrum, devices_seq), "seq")
+    packed = pack_filter(filter_spectrum, devices_seq)
+    arrived = [packed[0]] + [swap_with(packed[d], d) for d in range(1, devices_seq)]
     spectrum = forward(got, devices_seq, width)
-    conv = inverse(
-        spectrum, arrived.reshape(-1, width, LANES), devices_seq, signal.shape[0] // 2
-    )
+    conv = inverse(spectrum, arrived, devices_seq, signal.shape[0] // 2)
     return mix(pairs(conv), signal, input_gate, output_gate, skip_gain)
 
 
@@ -505,7 +539,8 @@
         and low == 8
         and tok_rows == low * high // 2
         and tok_rows % 32 == 0
-        and devices_seq % 2 == 0
+        and devices_seq >= 4
+        and devices_seq & (devices_seq - 1) == 0
     )
     plan = spread_kernels if fits else spread_plain
     return plan(signal, input_gate, output_gate, filter_spectrum, skip_gain)

time: 127 us -> 119 us (0.937)
  waiting for transfers between devices: 53.2 us -> 26.6 us
  starting transfers between devices: 11.1 us -> 30.8 us
  blocking collectives: 37.1 us -> 32.9 us
  Pallas kernels: 20.6 us -> 24.4 us
    all_to_all x2 -> x1, waiting for transfers between devices: 53.2 us -> 0.01 us  [exchange(): return lax.all_to_all(values, axes, split_axis=0, concat_axis=0, tiled=True)]
    ppermute x0 -> x15, waiting for transfers between devices: none -> 26.6 us  [swap_with(): lax.ppermute(values, 'seq', [(i, i ^ distance) for i in range(count)])]
    ppermute x0 -> x15, starting transfers between devices: none -> 23.5 us  [swap_with(): lax.ppermute(values, 'seq', [(i, i ^ distance) for i in range(count)])]
    all_to_all x1, blocking collectives: 37.1 us -> 32.9 us  [exchange(): return lax.all_to_all(values, axes, split_axis=0, concat_axis=0, tiled=True)]
    all_to_all x2 -> x1, starting transfers between devices: 11.1 us -> 7.3 us  [exchange(): return lax.all_to_all(values, axes, split_axis=0, concat_axis=0, tiled=True)]
    pallas_call x1, Pallas kernels: 3.31 us -> 5.2 us  [pack_filter(): pl.pallas_call(functools.partial(pack_filter_kernel, middle=low * devices...]
    pallas_call x1, Pallas kernels: 6.04 us -> 7.89 us  [inverse(): pl.pallas_call(functools.partial(inverse_kernel, devices_seq=devices_seq)...]
    unnamed x18 -> x38, local copies, waits for them, and re-layouts: 4.1 us -> 4.12 us
  transfers between devices with their start and end apart: 2 -> 16, of which waited for: 2 -> 5; matrix products, arithmetic and copies ran while one was open for 0% -> 0% of each run, Pallas kernels for 8% -> 10%
where the time goes in v3:
time: 119 us
  blocking collectives  32.9 us (28%)
  starting transfers between devices  30.8 us (26%)
  waiting for transfers between devices  26.6 us (22%)
  Pallas kernels  24.4 us (21%)
  local copies, waits for them, and re-layouts  4.12 us (3%)
    all_to_all x1, blocking collectives, exchange(): return lax.all_to_all(values, axes, split_axis=0, concat_axis=0, tiled=True)  32.9 us
    ppermute x15, waiting for transfers between devices, swap_with(): lax.ppermute(values, 'seq', [(i, i ^ distance) for i in range(count)])  26.6 us
    ppermute x15, starting transfers between devices, swap_with(): lax.ppermute(values, 'seq', [(i, i ^ distance) for i in range(count)])  23.5 us
    pallas_call x1, Pallas kernels, inverse(): pl.pallas_call(functools.partial(inverse_kernel, devices_seq=devices_seq)...  7.89 us
    all_to_all x1, starting transfers between devices, exchange(): return lax.all_to_all(values, axes, split_axis=0, concat_axis=0, tiled=True)  7.3 us
    pallas_call x1, Pallas kernels, forward(): pl.pallas_call(functools.partial(forward_kernel, devices_seq=devices_seq)...  6.7 us
    pallas_call x1, Pallas kernels, pack_filter(): pl.pallas_call(functools.partial(pack_filter_kernel, middle=low * devices...  5.2 us
    unnamed x38, local copies, waits for them, and re-layouts  4.12 us
  transfers between devices with their start and end apart: 16, of which 5 were waited for; matrix products, arithmetic and copies ran while one was open for 0% of the time, Pallas kernels for 10%

profile of v3, /device:TPU:0, one launch (start us, length us, event | category | flops | bytes accessed | tf_op | source)
XLA Modules:
  0.0 119.1 jit_solution(7097004602337729607)
XLA Ops:
  0.0 2.6 %pack_input.1 = bf16[16,2,128,128]{3,2,1,0:T(8,128)(2,1)} custom-call(bf16[256,2048]{1,0:T(8,128)(2,1)} %signal_ref.3, bf16[256,2048]{1,0:T(8,128)(2,1)} %gate_ref.3), custom_call_target="tpu_custom_call" | custom-call | flops 524288 | bytes 3145728 | tf_op jit(solution)/shard_map/pack_input/pallas_call | solution.py:89
  2.6 7.3 %all-to-all-start = ((bf16[32,128,128]{2,1,0:T(8,128)(2,1)}), bf16[32,128,128]{2,1,0:T(8,128)(2,1)S(1)}, u32[]{:S(2)}, u32[]{:S(2)}) async-start(bf16[32,128,128]{2,1,0:T(8,128)(2,1)} %bitcast.11), calls=%async_computation | async-start | bytes 2097152 | tf_op jit(solution)/shard_map/all_to_all | solution.py:23
  9.9 0.1 pad_add_fusion.place_ref
  10.0 5.2 %pack_filter.1 = (bf16[512,128]{1,0:T(8,128)(2,1)S(1)}, bf16[512,128]{1,0:T(8,128)(2,1)S(1)}, bf16[512,128]{1,0:T(8,128)(2,1)S(1)}, bf16[512,128]{1,0:T(8,128)(2...) custom-call(s32[2]{0:T(128)S(1)} %pad_add_fusion.place_ref, ...), custom_call_target="tpu_custom_call" | custom-call | flops 134217728 | bytes 6291456 | tf_op jit(solution)/shard_map/pack_filter/pallas_call | solution.py:143
  15.2 0.7 copy-done.5
  15.9 0.2 collective-permute-start
  16.1 1.7 %collective-permute-start.1 = (bf16[512,128]{1,0:T(8,128)(2,1)S(1)}, bf16[512,128]{1,0:T(8,128)(2,1)S(1)}, u32[]{:S(2)}, u32[]{:S(2)}) collective-permute-start(bf16[512,128]{1,0:T(8,128)(2,1)S(1)} %get-tuple-element.23), channel_id=1, source_target_pairs={{0,2},{1,3},{2,0},{3,1},{4,6},{5,7},{6,4},{7,5},{8,10},{9,11},{10,... | collective-permute-start | bytes 393224 | tf_op jit(solution)/shard_map/ppermute | solution.py:166
  17.8 0.0 collective-permute-start.2
  17.8 1.7 %collective-permute-start.3 = (bf16[512,128]{1,0:T(8,128)(2,1)S(1)}, bf16[512,128]{1,0:T(8,128)(2,1)S(1)}, u32[]{:S(2)}, u32[]{:S(2)}) collective-permute-start(bf16[512,128]{1,0:T(8,128)(2,1)S(1)} %get-tuple-element.25), channel_id=1, source_target_pairs={{0,4},{1,5},{2,6},{3,7},{4,0},{5,1},{6,2},{7,3},{8,12},{9,13},{10,... | collective-permute-start | bytes 393224 | tf_op jit(solution)/shard_map/ppermute | solution.py:166
  19.5 0.1 collective-permute-start.4
  19.6 2.6 %collective-permute-start.5 = (bf16[512,128]{1,0:T(8,128)(2,1)S(1)}, bf16[512,128]{1,0:T(8,128)(2,1)S(1)}, u32[]{:S(2)}, u32[]{:S(2)}) collective-permute-start(bf16[512,128]{1,0:T(8,128)(2,1)S(1)} %get-tuple-element.27), channel_id=1, source_target_pairs={{0,6},{1,7},{2,4},{3,5},{4,2},{5,3},{6,0},{7,1},{8,14},{9,15},{10,... | collective-permute-start | bytes 393224 | tf_op jit(solution)/shard_map/ppermute | solution.py:166
  22.2 3.1 %collective-permute-done.1.refs_2_ = bf16[512,128]{1,0:T(8,128)(2,1)S(1)} collective-permute-done((bf16[512,128]{1,0:T(8,128)(2,1)S(1)}, bf16[512,128]{1,0:T(8,128)(2,1)S(1)}, u32[]{:S(2)}, u32[]{:S(2)}) %collective-permute-start.1) | collective-permute-done | bytes 131104 | tf_op jit(solution)/shard_map/ppermute | solution.py:166
  25.3 1.8 %collective-permute-start.6 = (bf16[512,128]{1,0:T(8,128)(2,1)S(1)}, bf16[512,128]{1,0:T(8,128)(2,1)S(1)}, u32[]{:S(2)}, u32[]{:S(2)}) collective-permute-start(bf16[512,128]{1,0:T(8,128)(2,1)S(1)} %get-tuple-element.28), channel_id=1, source_target_pairs={{0,7},{1,6},{2,5},{3,4},{4,3},{5,2},{6,1},{7,0},{8,15},{9,14},{10,... | collective-permute-start | bytes 393224 | tf_op jit(solution)/shard_map/ppermute | solution.py:166
  27.1 1.0 collective-permute-done.2.refs_3_
  28.1 2.9 %collective-permute-start.7 = (bf16[512,128]{1,0:T(8,128)(2,1)S(1)}, bf16[512,128]{1,0:T(8,128)(2,1)S(1)}, u32[]{:S(2)}, u32[]{:S(2)}) collective-permute-start(bf16[512,128]{1,0:T(8,128)(2,1)S(1)} %get-tuple-element.29), channel_id=1, source_target_pairs={{0,8},{1,9},{2,10},{3,11},{4,12},{5,13},{6,14},{7,15},{8,0},{9,1},... | collective-permute-start | bytes 393224 | tf_op jit(solution)/shard_map/ppermute | solution.py:166
  31.0 3.2 %collective-permute-start.8 = (bf16[512,128]{1,0:T(8,128)(2,1)S(1)}, bf16[512,128]{1,0:T(8,128)(2,1)S(1)}, u32[]{:S(2)}, u32[]{:S(2)}) collective-permute-start(bf16[512,128]{1,0:T(8,128)(2,1)S(1)} %get-tuple-element.30), channel_id=1, source_target_pairs={{0,9},{1,8},{2,11},{3,10},{4,13},{5,12},{6,15},{7,14},{8,1},{9,0},... | collective-permute-start | bytes 393224 | tf_op jit(solution)/shard_map/ppermute | solution.py:166
  34.1 4.0 %collective-permute-start.9 = (bf16[512,128]{1,0:T(8,128)(2,1)S(1)}, bf16[512,128]{1,0:T(8,128)(2,1)S(1)}, u32[]{:S(2)}, u32[]{:S(2)}) collective-permute-start(bf16[512,128]{1,0:T(8,128)(2,1)S(1)} %get-tuple-element.31), channel_id=1, source_target_pairs={{0,10},{1,11},{2,8},{3,9},{4,14},{5,15},{6,12},{7,13},{8,2},{9,3},... | collective-permute-start | bytes 393224 | tf_op jit(solution)/shard_map/ppermute | solution.py:166
  38.1 7.9 %collective-permute-done.5.refs_6_ = bf16[512,128]{1,0:T(8,128)(2,1)S(1)} collective-permute-done((bf16[512,128]{1,0:T(8,128)(2,1)S(1)}, bf16[512,128]{1,0:T(8,128)(2,1)S(1)}, u32[]{:S(2)}, u32[]{:S(2)}) %collective-permute-start.5) | collective-permute-done | bytes 131104 | tf_op jit(solution)/shard_map/ppermute | solution.py:166
  46.1 1.9 %collective-permute-done.6.refs_7_ = bf16[512,128]{1,0:T(8,128)(2,1)S(1)} collective-permute-done((bf16[512,128]{1,0:T(8,128)(2,1)S(1)}, bf16[512,128]{1,0:T(8,128)(2,1)S(1)}, u32[]{:S(2)}, u32[]{:S(2)}) %collective-permute-start.6) | collective-permute-done | bytes 131104 | tf_op jit(solution)/shard_map/ppermute | solution.py:166
  48.0 1.8 %collective-permute-start.11 = (bf16[512,128]{1,0:T(8,128)(2,1)}, bf16[512,128]{1,0:T(8,128)(2,1)}, u32[]{:S(2)}, u32[]{:S(2)}) collective-permute-start(bf16[512,128]{1,0:T(8,128)(2,1)} %get-tuple-element.33), channel_id=1, source_target_pairs={{0,12},{1,13},{2,14},{3,15},{4,8},{5,9},{6,10},{7,11},{8,4},{9,5},... | collective-permute-start | bytes 393224 | tf_op jit(solution)/shard_map/ppermute | solution.py:166
  49.8 1.9 %collective-permute-start.12 = (bf16[512,128]{1,0:T(8,128)(2,1)}, bf16[512,128]{1,0:T(8,128)(2,1)}, u32[]{:S(2)}, u32[]{:S(2)}) collective-permute-start(bf16[512,128]{1,0:T(8,128)(2,1)} %get-tuple-element.34), channel_id=1, source_target_pairs={{0,13},{1,12},{2,15},{3,14},{4,9},{5,8},{6,11},{7,10},{8,5},{9,4},... | collective-permute-start | bytes 393224 | tf_op jit(solution)/shard_map/ppermute | solution.py:166
  51.7 1.2 %collective-permute-start.13 = (bf16[512,128]{1,0:T(8,128)(2,1)}, bf16[512,128]{1,0:T(8,128)(2,1)}, u32[]{:S(2)}, u32[]{:S(2)}) collective-permute-start(bf16[512,128]{1,0:T(8,128)(2,1)} %get-tuple-element.35), channel_id=1, source_target_pairs={{0,14},{1,15},{2,12},{3,13},{4,10},{5,11},{6,8},{7,9},{8,6},{9,7},... | collective-permute-start | bytes 393224 | tf_op jit(solution)/shard_map/ppermute | solution.py:166
  52.9 12.8 %collective-permute-done.9.refs_10_ = bf16[512,128]{1,0:T(8,128)(2,1)S(1)} collective-permute-done((bf16[512,128]{1,0:T(8,128)(2,1)S(1)}, bf16[512,128]{1,0:T(8,128)(2,1)S(1)}, u32[]{:S(2)}, u32[]{:S(2)}) %collective-permute-start.9) | collective-permute-done | bytes 131104 | tf_op jit(solution)/shard_map/ppermute | solution.py:166
  65.8 0.6 copy-done.18
  66.3 0.4 collective-permute-start.14
  66.8 0.0 copy-start.7
  66.8 0.8 copy-done.7
  67.6 6.7 %forward.1.spec_hbm = f32[65,128,128]{2,1,0:T(8,128)S(1)} custom-call(bf16[16,2,128,128]{3,2,1,0:T(8,128)(2,1)S(1)} %bitcast.9, bf16[128,128]{1,0:T(8,128)(2,1)S(1)} %copy-done.7, bf16[128,384]{1,0:T(8,128)(2,1)S(1)} %copy-done.6, f32[9,64,128]{2,1,0:T(8,128)S(1)} %copy-done.3), custom_call_target="tpu_custom_call" | custom-call | flops 1073741824 | bytes 5242880 | tf_op jit(solution)/shard_map/forward/pallas_call | solution.py:249
  74.3 2.0 %copy-done = f32[65,128,128]{2,1,0:T(8,128)} copy-done((f32[65,128,128]{2,1,0:T(8,128)}, f32[65,128,128]{2,1,0:T(8,128)S(1)}, u32[]{:S(2)}) %copy-start) | copy-done | bytes 4259864
  76.3 7.9 %inverse.1 = bf16[16,2,128,128]{3,2,1,0:T(8,128)(2,1)S(1)} custom-call(s32[1]{0:T(128)} %bitcast.place_ref, f32[65,128,128]{2,1,0:T(8,128)} %copy-done, bf16[192,256]{1,0:T(8,128)(2,1)} %constant.20.clone.matrices_hbm, bf16[512,128]{1,0:T(8,128)(2,1)} %copy-done.5, bf16[512,128]{1,0:T(8,128)(2,1)} %copy-done.9, bf16[512,128]{1,0:T(8,128)(2,1)} %copy-done.10, ...), custom_call_target="tpu_custom_call" | custom-call | flops 805306368 | bytes 6356992 | tf_op jit(solution)/shard_map/inverse/pallas_call | solution.py:383
  84.2 32.9 %all_to_all.10 = bf16[32,128,128]{2,1,0:T(8,128)(2,1)S(1)} all-to-all(bf16[32,128,128]{2,1,0:T(8,128)(2,1)S(1)} %bitcast.7), channel_id=1, replica_groups=mesh['groups'=2,'seq'=16] {'seq','groups'}, dimensions={0} | all-to-all | bytes 2097152 | tf_op jit(solution)/shard_map/all_to_all | solution.py:23
  117.2 2.0 %mix.1 = bf16[256,2048]{1,0:T(8,128)(2,1)} custom-call(bf16[16,2,128,128]{3,2,1,0:T(8,128)(2,1)S(1)} %bitcast.8, bf16[256,2048]{1,0:T(8,128)(2,1)S(1)} %copy-done.1, bf16[256,2048]{1,0:T(8,128)(2,1)S(1)} %copy-done.2, bf16[256,2048]{1,0:T(8,128)(2,1)S(1)} %copy-done.4, f32[1,2048]{1,0:T(1,128)S(1)} %bitcast.10), custom_call_target="tpu_custom_call" | custom-call | flops 2097152 | bytes 5242880 | tf_op jit(solution)/shard_map/mix/pallas_call | solution.py:431
  (45 shorter events, 0.1 us)
Async XLA Ops:
  0.0 66.7 %copy-start.3 = (f32[9,64,128]{2,1,0:T(8,128)S(1)}, f32[9,64,128]{2,1,0:T(8,128)}, u32[]{:S(2)}) copy-start(f32[9,64,128]{2,1,0:T(8,128)} %constant.19.clone.turn_ref.refs_16_) | copy-start | bytes 884740
  0.0 66.8 %copy-start.6 = (bf16[128,384]{1,0:T(8,128)(2,1)S(1)}, bf16[128,384]{1,0:T(8,128)(2,1)}, u32[]{:S(2)}) copy-start(bf16[128,384]{1,0:T(8,128)(2,1)} %constant.18.clone.second_ref) | copy-start | bytes 294916
  2.6 64.1 %all-to-all-start = ((bf16[32,128,128]{2,1,0:T(8,128)(2,1)}), bf16[32,128,128]{2,1,0:T(8,128)(2,1)S(1)}, u32[]{:S(2)}, u32[]{:S(2)}) async-start(bf16[32,128,128]{2,1,0:T(8,128)(2,1)} %bitcast.11), calls=%async_computation | async-start | bytes 2097152 | tf_op jit(solution)/shard_map/all_to_all | solution.py:23
  10.0 107.1 %copy-start.8 = (f32[2048]{0:T(1024)S(1)}, f32[2048]{0:T(1024)}, u32[]{:S(2)}) copy-start(f32[2048]{0:T(1024)} %param.13) | copy-start | bytes 24580
  15.9 101.3 %copy-start.1 = (bf16[256,2048]{1,0:T(8,128)(2,1)S(1)}, bf16[256,2048]{1,0:T(8,128)(2,1)}, u32[]{:S(2)}) copy-start(bf16[256,2048]{1,0:T(8,128)(2,1)} %signal_ref.3) | copy-start | bytes 3145732
  15.9 101.3 %copy-start.2 = (bf16[256,2048]{1,0:T(8,128)(2,1)S(1)}, bf16[256,2048]{1,0:T(8,128)(2,1)}, u32[]{:S(2)}) copy-start(bf16[256,2048]{1,0:T(8,128)(2,1)} %gate_ref.3) | copy-start | bytes 3145732
  15.9 3.7 %collective-permute-start = (bf16[512,128]{1,0:T(8,128)(2,1)S(1)}, bf16[512,128]{1,0:T(8,128)(2,1)S(1)}, u32[]{:S(2)}, u32[]{:S(2)}) collective-permute-start(bf16[512,128]{1,0:T(8,128)(2,1)S(1)} %get-tuple-element.22), channel_id=1, source_target_pairs={{0,1},{1,0},{2,3},{3,2},{4,5},{5,4},{6,7},{7,6},{8,9},{9,8},{10,11... | collective-permute-start | bytes 393224 | tf_op jit(solution)/shard_map/ppermute | solution.py:166
  16.1 9.2 %collective-permute-start.1 = (bf16[512,128]{1,0:T(8,128)(2,1)S(1)}, bf16[512,128]{1,0:T(8,128)(2,1)S(1)}, u32[]{:S(2)}, u32[]{:S(2)}) collective-permute-start(bf16[512,128]{1,0:T(8,128)(2,1)S(1)} %get-tuple-element.23), channel_id=1, source_target_pairs={{0,2},{1,3},{2,0},{3,1},{4,6},{5,7},{6,4},{7,5},{8,10},{9,11},{10,... | collective-permute-start | bytes 393224 | tf_op jit(solution)/shard_map/ppermute | solution.py:166
  17.8 10.2 %collective-permute-start.2 = (bf16[512,128]{1,0:T(8,128)(2,1)S(1)}, bf16[512,128]{1,0:T(8,128)(2,1)S(1)}, u32[]{:S(2)}, u32[]{:S(2)}) collective-permute-start(bf16[512,128]{1,0:T(8,128)(2,1)S(1)} %get-tuple-element.24), channel_id=1, source_target_pairs={{0,3},{1,2},{2,1},{3,0},{4,7},{5,6},{6,5},{7,4},{8,11},{9,10},{10,... | collective-permute-start | bytes 393224 | tf_op jit(solution)/shard_map/ppermute | solution.py:166
  17.8 13.1 %collective-permute-start.3 = (bf16[512,128]{1,0:T(8,128)(2,1)S(1)}, bf16[512,128]{1,0:T(8,128)(2,1)S(1)}, u32[]{:S(2)}, u32[]{:S(2)}) collective-permute-start(bf16[512,128]{1,0:T(8,128)(2,1)S(1)} %get-tuple-element.25), channel_id=1, source_target_pairs={{0,4},{1,5},{2,6},{3,7},{4,0},{5,1},{6,2},{7,3},{8,12},{9,13},{10,... | collective-permute-start | bytes 393224 | tf_op jit(solution)/shard_map/ppermute | solution.py:166
  19.5 14.6 %collective-permute-start.4 = (bf16[512,128]{1,0:T(8,128)(2,1)S(1)}, bf16[512,128]{1,0:T(8,128)(2,1)S(1)}, u32[]{:S(2)}, u32[]{:S(2)}) collective-permute-start(bf16[512,128]{1,0:T(8,128)(2,1)S(1)} %get-tuple-element.26), channel_id=1, source_target_pairs={{0,5},{1,4},{2,7},{3,6},{4,1},{5,0},{6,3},{7,2},{8,13},{9,12},{10,... | collective-permute-start | bytes 393224 | tf_op jit(solution)/shard_map/ppermute | solution.py:166
  19.6 46.1 %copy-start.9 = (bf16[512,128]{1,0:T(8,128)(2,1)}, bf16[512,128]{1,0:T(8,128)(2,1)S(1)}, u32[]{:S(2)}) copy-start(bf16[512,128]{1,0:T(8,128)(2,1)S(1)} %collective-permute-done.refs_1_) | copy-start | bytes 393220
  19.6 26.5 %collective-permute-start.5 = (bf16[512,128]{1,0:T(8,128)(2,1)S(1)}, bf16[512,128]{1,0:T(8,128)(2,1)S(1)}, u32[]{:S(2)}, u32[]{:S(2)}) collective-permute-start(bf16[512,128]{1,0:T(8,128)(2,1)S(1)} %get-tuple-element.27), channel_id=1, source_target_pairs={{0,6},{1,7},{2,4},{3,5},{4,2},{5,3},{6,0},{7,1},{8,14},{9,15},{10,... | collective-permute-start | bytes 393224 | tf_op jit(solution)/shard_map/ppermute | solution.py:166
  25.3 40.4 %copy-start.10 = (bf16[512,128]{1,0:T(8,128)(2,1)}, bf16[512,128]{1,0:T(8,128)(2,1)S(1)}, u32[]{:S(2)}) copy-start(bf16[512,128]{1,0:T(8,128)(2,1)S(1)} %collective-permute-done.1.refs_2_) | copy-start | bytes 393220
  25.3 22.6 %collective-permute-start.6 = (bf16[512,128]{1,0:T(8,128)(2,1)S(1)}, bf16[512,128]{1,0:T(8,128)(2,1)S(1)}, u32[]{:S(2)}, u32[]{:S(2)}) collective-permute-start(bf16[512,128]{1,0:T(8,128)(2,1)S(1)} %get-tuple-element.28), channel_id=1, source_target_pairs={{0,7},{1,6},{2,5},{3,4},{4,3},{5,2},{6,1},{7,0},{8,15},{9,14},{10,... | collective-permute-start | bytes 393224 | tf_op jit(solution)/shard_map/ppermute | solution.py:166
  28.1 37.6 %copy-start.11 = (bf16[512,128]{1,0:T(8,128)(2,1)}, bf16[512,128]{1,0:T(8,128)(2,1)S(1)}, u32[]{:S(2)}) copy-start(bf16[512,128]{1,0:T(8,128)(2,1)S(1)} %collective-permute-done.2.refs_3_) | copy-start | bytes 393220
  28.1 21.7 %collective-permute-start.7 = (bf16[512,128]{1,0:T(8,128)(2,1)S(1)}, bf16[512,128]{1,0:T(8,128)(2,1)S(1)}, u32[]{:S(2)}, u32[]{:S(2)}) collective-permute-start(bf16[512,128]{1,0:T(8,128)(2,1)S(1)} %get-tuple-element.29), channel_id=1, source_target_pairs={{0,8},{1,9},{2,10},{3,11},{4,12},{5,13},{6,14},{7,15},{8,0},{9,1},... | collective-permute-start | bytes 393224 | tf_op jit(solution)/shard_map/ppermute | solution.py:166
  30.9 34.8 %copy-start.12 = (bf16[512,128]{1,0:T(8,128)(2,1)}, bf16[512,128]{1,0:T(8,128)(2,1)S(1)}, u32[]{:S(2)}) copy-start(bf16[512,128]{1,0:T(8,128)(2,1)S(1)} %collective-permute-done.3.refs_4_) | copy-start | bytes 393220
  31.0 20.8 %collective-permute-start.8 = (bf16[512,128]{1,0:T(8,128)(2,1)S(1)}, bf16[512,128]{1,0:T(8,128)(2,1)S(1)}, u32[]{:S(2)}, u32[]{:S(2)}) collective-permute-start(bf16[512,128]{1,0:T(8,128)(2,1)S(1)} %get-tuple-element.30), channel_id=1, source_target_pairs={{0,9},{1,8},{2,11},{3,10},{4,13},{5,12},{6,15},{7,14},{8,1},{9,0},... | collective-permute-start | bytes 393224 | tf_op jit(solution)/shard_map/ppermute | solution.py:166
  34.1 31.6 %copy-start.13 = (bf16[512,128]{1,0:T(8,128)(2,1)}, bf16[512,128]{1,0:T(8,128)(2,1)S(1)}, u32[]{:S(2)}) copy-start(bf16[512,128]{1,0:T(8,128)(2,1)S(1)} %collective-permute-done.4.refs_5_) | copy-start | bytes 393220
  34.1 31.6 %collective-permute-start.9 = (bf16[512,128]{1,0:T(8,128)(2,1)S(1)}, bf16[512,128]{1,0:T(8,128)(2,1)S(1)}, u32[]{:S(2)}, u32[]{:S(2)}) collective-permute-start(bf16[512,128]{1,0:T(8,128)(2,1)S(1)} %get-tuple-element.31), channel_id=1, source_target_pairs={{0,10},{1,11},{2,8},{3,9},{4,14},{5,15},{6,12},{7,13},{8,2},{9,3},... | collective-permute-start | bytes 393224 | tf_op jit(solution)/shard_map/ppermute | solution.py:166
  46.1 19.6 %copy-start.14 = (bf16[512,128]{1,0:T(8,128)(2,1)}, bf16[512,128]{1,0:T(8,128)(2,1)S(1)}, u32[]{:S(2)}) copy-start(bf16[512,128]{1,0:T(8,128)(2,1)S(1)} %collective-permute-done.5.refs_6_) | copy-start | bytes 393220
  46.1 30.2 %collective-permute-start.10 = (bf16[512,128]{1,0:T(8,128)(2,1)}, bf16[512,128]{1,0:T(8,128)(2,1)}, u32[]{:S(2)}, u32[]{:S(2)}) collective-permute-start(bf16[512,128]{1,0:T(8,128)(2,1)} %get-tuple-element.32), channel_id=1, source_target_pairs={{0,11},{1,10},{2,9},{3,8},{4,15},{5,14},{6,13},{7,12},{8,3},{9,2},... | collective-permute-start | bytes 393224 | tf_op jit(solution)/shard_map/ppermute | solution.py:166
  48.0 17.8 %copy-start.15 = (bf16[512,128]{1,0:T(8,128)(2,1)}, bf16[512,128]{1,0:T(8,128)(2,1)S(1)}, u32[]{:S(2)}) copy-start(bf16[512,128]{1,0:T(8,128)(2,1)S(1)} %collective-permute-done.6.refs_7_) | copy-start | bytes 393220
  48.0 28.4 %collective-permute-start.11 = (bf16[512,128]{1,0:T(8,128)(2,1)}, bf16[512,128]{1,0:T(8,128)(2,1)}, u32[]{:S(2)}, u32[]{:S(2)}) collective-permute-start(bf16[512,128]{1,0:T(8,128)(2,1)} %get-tuple-element.33), channel_id=1, source_target_pairs={{0,12},{1,13},{2,14},{3,15},{4,8},{5,9},{6,10},{7,11},{8,4},{9,5},... | collective-permute-start | bytes 393224 | tf_op jit(solution)/shard_map/ppermute | solution.py:166
  49.8 16.0 %copy-start.16 = (bf16[512,128]{1,0:T(8,128)(2,1)}, bf16[512,128]{1,0:T(8,128)(2,1)S(1)}, u32[]{:S(2)}) copy-start(bf16[512,128]{1,0:T(8,128)(2,1)S(1)} %collective-permute-done.7.refs_8_) | copy-start | bytes 393220
  49.8 26.5 %collective-permute-start.12 = (bf16[512,128]{1,0:T(8,128)(2,1)}, bf16[512,128]{1,0:T(8,128)(2,1)}, u32[]{:S(2)}, u32[]{:S(2)}) collective-permute-start(bf16[512,128]{1,0:T(8,128)(2,1)} %get-tuple-element.34), channel_id=1, source_target_pairs={{0,13},{1,12},{2,15},{3,14},{4,9},{5,8},{6,11},{7,10},{8,5},{9,4},... | collective-permute-start | bytes 393224 | tf_op jit(solution)/shard_map/ppermute | solution.py:166
  51.7 14.1 %copy-start.17 = (bf16[512,128]{1,0:T(8,128)(2,1)}, bf16[512,128]{1,0:T(8,128)(2,1)S(1)}, u32[]{:S(2)}) copy-start(bf16[512,128]{1,0:T(8,128)(2,1)S(1)} %collective-permute-done.8.refs_9_) | copy-start | bytes 393220
  51.7 24.6 %collective-permute-start.13 = (bf16[512,128]{1,0:T(8,128)(2,1)}, bf16[512,128]{1,0:T(8,128)(2,1)}, u32[]{:S(2)}, u32[]{:S(2)}) collective-permute-start(bf16[512,128]{1,0:T(8,128)(2,1)} %get-tuple-element.35), channel_id=1, source_target_pairs={{0,14},{1,15},{2,12},{3,13},{4,10},{5,11},{6,8},{7,9},{8,6},{9,7},... | collective-permute-start | bytes 393224 | tf_op jit(solution)/shard_map/ppermute | solution.py:166
  66.3 10.0 %collective-permute-start.14 = (bf16[512,128]{1,0:T(8,128)(2,1)}, bf16[512,128]{1,0:T(8,128)(2,1)}, u32[]{:S(2)}, u32[]{:S(2)}) collective-permute-start(bf16[512,128]{1,0:T(8,128)(2,1)} %get-tuple-element.36), channel_id=1, source_target_pairs={{0,15},{1,14},{2,13},{3,12},{4,11},{5,10},{6,9},{7,8},{8,7},{9,6},... | collective-permute-start | bytes 393224 | tf_op jit(solution)/shard_map/ppermute | solution.py:166
  66.7 50.4 %copy-start.4 = (bf16[256,2048]{1,0:T(8,128)(2,1)S(1)}, bf16[256,2048]{1,0:T(8,128)(2,1)}, u32[]{:S(2)}) copy-start(bf16[256,2048]{1,0:T(8,128)(2,1)} %out_gate_ref.1) | copy-start | bytes 3145732
  74.3 2.0 %copy-start = (f32[65,128,128]{2,1,0:T(8,128)}, f32[65,128,128]{2,1,0:T(8,128)S(1)}, u32[]{:S(2)}) copy-start(f32[65,128,128]{2,1,0:T(8,128)S(1)} %forward.1.spec_hbm) | copy-start | bytes 12779524
  (3 other events, 2.2 us)

commit v4 on v3

--- a/solution.py
+++ b/solution.py
@@ -142,7 +142,7 @@
 
     return pl.pallas_call(
         functools.partial(pack_filter_kernel, middle=low * devices_seq // 2),
-        out_shape=[jax.ShapeDtypeStruct(block, BF16)] * devices_seq,
+        out_shape=[pltpu.HBM(block, BF16)] * devices_seq,
         grid_spec=pltpu.PrefetchScalarGridSpec(
             num_scalar_prefetch=1,
             grid=(steps,),
@@ -248,7 +248,7 @@
     first, second, _, turn = tables(half_rows, width)
     return pl.pallas_call(
         functools.partial(forward_kernel, devices_seq=devices_seq),
-        out_shape=jax.ShapeDtypeStruct((half_rows + 1, 2 * width, LANES), F32),
+        out_shape=pltpu.HBM((half_rows + 1, 2 * width, LANES), F32),
         scratch_shapes=[
             pltpu.VMEM((half_rows * (width + PAD), LANES), F32),
             pltpu.VMEM((width * (2 * half_rows + PAD), LANES), F32),
@@ -267,8 +267,10 @@
     place_ref, spec_hbm, matrices_hbm, *refs, devices_seq
 ):
     filter_hbm = refs[:devices_seq]
-    turn_ref, out_ref, spec_ref, filter_ref, matrices_ref = refs[devices_seq : devices_seq + 5]
-    real_ref, imag_ref, rows_ref, sems, filter_sems = refs[devices_seq + 5 :]
+    turn_ref, out_ref, spec_ref, filter_ref, lead_ref, matrices_ref = refs[
+        devices_seq : devices_seq + 6
+    ]
+    real_ref, imag_ref, rows_ref, sems, filter_sems = refs[devices_seq + 6 :]
     width = turn_ref.shape[1]
     half_rows = spec_ref.shape[0] - 1
     pitch = width + PAD
@@ -277,32 +279,44 @@
 
     top_block = half_rows // per_source
 
-    def fetch(block, count=per_source):
-        at = pl.ds(per_source * block, count)
-        return pltpu.make_async_copy(spec_hbm.at[at], spec_ref.at[at], sems.at[block])
-
+    place = place_ref[0]
+    upper = place >= top_block
+
+    def block_of(distance):
+        source = place ^ distance
+        return jnp.where(upper, devices_seq - 1 - source, source)
+
+    def fetch(distance):
+        at = pl.ds(per_source * block_of(distance), per_source)
+        return pltpu.make_async_copy(spec_hbm.at[at], spec_ref.at[at], sems.at[distance])
+
+    def arrival(distance):
+        return pltpu.make_async_copy(
+            filter_hbm[distance], filter_ref.at[distance], filter_sems.at[distance]
+        )
+
+    top_rows = pl.ds(half_rows, 1)
+    top = pltpu.make_async_copy(
+        spec_hbm.at[top_rows], spec_ref.at[top_rows], sems.at[top_block]
+    )
     matrices = pltpu.make_async_copy(matrices_hbm, matrices_ref, sems.at[top_block + 1])
     matrices.start()
-    fetch(0).start()
-    for distance in range(devices_seq):
-        source = place_ref[0] ^ distance
-        pltpu.make_async_copy(
-            filter_hbm[distance], filter_ref.at[source], filter_sems.at[source]
-        ).start()
-    for block in range(1, top_block):
-        fetch(block).start()
-    fetch(top_block, 1).start()
+    for distance in range(top_block):
+        fetch(distance).start()
+        arrival(distance).start()
+        arrival(devices_seq - 1 - distance).start()
+    top.start()
     matrices.wait()
-
-    def arrival(source):
-        return pltpu.make_async_copy(
-            filter_hbm[0], filter_ref.at[source], filter_sems.at[source]
-        )
-
-    def response_of(low):
-        return filter_ref[low // per_source, pl.ds(low % per_source * width, width), :].astype(F32)
     third_matrix = matrices_ref[: 2 * width]
     last_matrix = matrices_ref[2 * width :]
+
+    def response_of(distance, at):
+        far = devices_seq - 1 - distance
+        row = pl.ds(at * width, width)
+        mirror = pl.ds((per_source - at) * width, width)
+        lower = jnp.where(upper, filter_ref[far, row], filter_ref[distance, row])
+        higher = jnp.where(upper, filter_ref[distance, mirror], filter_ref[far, mirror])
+        return lower.astype(F32) + higher.astype(F32)
 
     def filtered(spec, response):
         turned = pltpu.roll(response, HALF, 1)
@@ -324,27 +338,49 @@
         real, imag = values[:width], values[width:]
         return real * cosine - imag * sine, real * sine + imag * cosine
 
-    for block in range(top_block):
-        fetch(block).wait()
-        arrival(block).wait()
-        arrival(devices_seq - 1 - block).wait()
-        for u in range(0, per_source, 2):
-            pair = []
-            for v in range(u, u + 2):
-                low = per_source * block + v
-                response = response_of(low)
-                if low:
-                    response = response + response_of(2 * half_rows - low)
-                pair.append(filtered(spec_ref[low], response))
-            done = transform(jnp.concatenate(pair, 1))
-            for v in range(2):
-                real, imag = turned_back(done[:, v * LANES : (v + 1) * LANES], block, u + v)
-                at = pl.ds((per_source * block + u + v) * pitch, width)
-                real_ref[at, :] = real
-                imag_ref[at, :] = imag
-    fetch(top_block, 1).wait()
-    done = transform(filtered(spec_ref[half_rows], response_of(half_rows)))
-    imag_ref[pl.ds(0, width), :] = turned_back(done, top_block, 0)[0]
+    def third_stage(slots):
+        values = jnp.concatenate(
+            [filtered(spec_ref[low], response) for low, response, _, _ in slots], 1
+        )
+        done = transform(values)
+        results = []
+        for v, (_, _, block, u) in enumerate(slots):
+            results.append(turned_back(done[:, v * LANES : (v + 1) * LANES], block, u))
+        return results
+
+    def keep(low, values):
+        at = low * pitch if isinstance(low, int) else pl.multiple_of(low * pitch, PAD)
+        real_ref[pl.ds(at, width), :] = values[0]
+        imag_ref[pl.ds(at, width), :] = values[1]
+
+    for distance in range(top_block):
+        block = block_of(distance)
+        far = devices_seq - 1 - distance
+        fetch(distance).wait()
+        arrival(distance).wait()
+        arrival(far).wait()
+        for near in (distance, far):
+            lead_ref[place ^ near] = filter_ref[near, :width].astype(F32)
+        slots = [
+            (per_source * block + v, response_of(distance, v), block, v)
+            for v in range(1, per_source)
+        ]
+        for at in range(0, len(slots), 2):
+            pair = slots[at : at + 2]
+            for slot, values in zip(pair, third_stage(pair)):
+                keep(slot[0], values)
+    top.wait()
+    slots = [(0, lead_ref[0], 0, 0), (half_rows, lead_ref[top_block], top_block, 0)]
+    first, middle = third_stage(slots)
+    keep(0, (first[0], middle[0]))
+    slots = [
+        (per_source * block, lead_ref[block] + lead_ref[devices_seq - block], block, 0)
+        for block in range(1, top_block)
+    ]
+    for at in range(0, len(slots), 2):
+        pair = slots[at : at + 2]
+        for slot, values in zip(pair, third_stage(pair)):
+            keep(slot[0], values)
 
     def last_stage(step, carry):
         for u in range(0, 8, 2):
@@ -389,6 +425,7 @@
         scratch_shapes=[
             pltpu.VMEM(spectrum.shape, F32),
             pltpu.VMEM((devices_seq, *arrived[0].shape), BF16),
+            pltpu.VMEM((devices_seq, width, LANES), F32),
             pltpu.VMEM(matrices.shape, BF16),
         ]
         + [pltpu.VMEM((half_rows * (width + PAD), LANES), F32)] * 3

time: 119 us -> 119 us (level)
  local copies, waits for them, and re-layouts: 4.12 us -> 1.48 us
    unnamed x38 -> x34, local copies, waits for them, and re-layouts: 4.12 us -> 1.48 us
    pallas_call x1, Pallas kernels: 6.7 us -> 8.66 us  [forward(): pl.pallas_call(functools.partial(forward_kernel, devices_seq=devices_seq)...]
    pallas_call x1, Pallas kernels: 7.89 us -> 6.18 us  [inverse(): pl.pallas_call(functools.partial(inverse_kernel, devices_seq=devices_seq)...]
  transfers between devices with their start and end apart: 16 -> 16, of which waited for: 5 -> 5; matrix products, arithmetic and copies ran while one was open for 0% -> 0% of each run, Pallas kernels for 10% -> 12%
where the time goes in v4:
time: 119 us; the launch traced here: 118 us
  blocking collectives  33.8 us (28%)
  starting transfers between devices  30.8 us (26%)
  waiting for transfers between devices  26.9 us (23%)
  Pallas kernels  25.1 us (21%)
  local copies, waits for them, and re-layouts  1.48 us (1%)
    all_to_all x1, blocking collectives, exchange(): return lax.all_to_all(values, axes, split_axis=0, concat_axis=0, tiled=True)  33.8 us
    ppermute x15, waiting for transfers between devices, swap_with(): lax.ppermute(values, 'seq', [(i, i ^ distance) for i in range(count)])  26.9 us
    ppermute x15, starting transfers between devices, swap_with(): lax.ppermute(values, 'seq', [(i, i ^ distance) for i in range(count)])  23.5 us
    pallas_call x1, Pallas kernels, forward(): pl.pallas_call(functools.partial(forward_kernel, devices_seq=devices_seq)...  8.66 us
    all_to_all x1, starting transfers between devices, exchange(): return lax.all_to_all(values, axes, split_axis=0, concat_axis=0, tiled=True)  7.3 us
    pallas_call x1, Pallas kernels, inverse(): pl.pallas_call(functools.partial(inverse_kernel, devices_seq=devices_seq)...  6.18 us
    pallas_call x1, Pallas kernels, pack_filter(): pl.pallas_call(functools.partial(pack_filter_kernel, middle=low * devices...  5.68 us
    pallas_call x1, Pallas kernels, pack_input(): pl.pallas_call(pack_input_kernel, out_shape=jax.ShapeDtypeStruct((devices...  2.63 us
  transfers between devices with their start and end apart: 16, of which 5 were waited for; matrix products, arithmetic and copies ran while one was open for 0% of the time, Pallas kernels for 12%

profile of v4, /device:TPU:0, one launch (start us, length us, event | category | flops | bytes accessed | tf_op | source)
XLA Modules:
  0.0 118.3 jit_solution(18419718599560761444)
XLA Ops:
  0.0 2.6 %pack_input.1 = bf16[16,2,128,128]{3,2,1,0:T(8,128)(2,1)} custom-call(bf16[256,2048]{1,0:T(8,128)(2,1)} %signal_ref.3, bf16[256,2048]{1,0:T(8,128)(2,1)} %gate_ref.3), custom_call_target="tpu_custom_call" | custom-call | flops 524288 | bytes 3145728 | tf_op jit(solution)/shard_map/pack_input/pallas_call | solution.py:89
  2.6 7.3 %all-to-all-start = ((bf16[32,128,128]{2,1,0:T(8,128)(2,1)}), bf16[32,128,128]{2,1,0:T(8,128)(2,1)S(1)}, u32[]{:S(2)}, u32[]{:S(2)}) async-start(bf16[32,128,128]{2,1,0:T(8,128)(2,1)} %bitcast.11), calls=%async_computation | async-start | bytes 2097152 | tf_op jit(solution)/shard_map/all_to_all | solution.py:23
  9.9 0.1 pad_add_fusion.place_ref
  10.0 5.7 %pack_filter.1 = (bf16[512,128]{1,0:T(8,128)(2,1)}, bf16[512,128]{1,0:T(8,128)(2,1)}, bf16[512,128]{1,0:T(8,128)(2,1)}, bf16[512,128]{1,0:T(8,128)(2,1)}, bf16[5...) custom-call(s32[2]{0:T(128)S(1)} %pad_add_fusion.place_ref, ...), custom_call_target="tpu_custom_call" | custom-call | flops 134217728 | bytes 6291456 | tf_op jit(solution)/shard_map/pack_filter/pallas_call | solution.py:143
  15.7 0.3 collective-permute-start
  16.0 1.7 %collective-permute-start.1 = (bf16[512,128]{1,0:T(8,128)(2,1)}, bf16[512,128]{1,0:T(8,128)(2,1)S(1)}, u32[]{:S(2)}, u32[]{:S(2)}) collective-permute-start(bf16[512,128]{1,0:T(8,128)(2,1)} %get-tuple-element.23), channel_id=1, source_target_pairs={{0,2},{1,3},{2,0},{3,1},{4,6},{5,7},{6,4},{7,5},{8,10},{9,11},{10,... | collective-permute-start | bytes 393224 | tf_op jit(solution)/shard_map/ppermute | solution.py:166
  17.7 0.0 collective-permute-start.2
  17.7 1.7 %collective-permute-start.3 = (bf16[512,128]{1,0:T(8,128)(2,1)}, bf16[512,128]{1,0:T(8,128)(2,1)S(1)}, u32[]{:S(2)}, u32[]{:S(2)}) collective-permute-start(bf16[512,128]{1,0:T(8,128)(2,1)} %get-tuple-element.25), channel_id=1, source_target_pairs={{0,4},{1,5},{2,6},{3,7},{4,0},{5,1},{6,2},{7,3},{8,12},{9,13},{10,... | collective-permute-start | bytes 393224 | tf_op jit(solution)/shard_map/ppermute | solution.py:166
  19.4 0.1 collective-permute-start.4
  19.5 2.6 %collective-permute-start.5 = (bf16[512,128]{1,0:T(8,128)(2,1)}, bf16[512,128]{1,0:T(8,128)(2,1)S(1)}, u32[]{:S(2)}, u32[]{:S(2)}) collective-permute-start(bf16[512,128]{1,0:T(8,128)(2,1)} %get-tuple-element.27), channel_id=1, source_target_pairs={{0,6},{1,7},{2,4},{3,5},{4,2},{5,3},{6,0},{7,1},{8,14},{9,15},{10,... | collective-permute-start | bytes 393224 | tf_op jit(solution)/shard_map/ppermute | solution.py:166
  22.1 3.2 %collective-permute-done.1.refs_2_ = bf16[512,128]{1,0:T(8,128)(2,1)S(1)} collective-permute-done((bf16[512,128]{1,0:T(8,128)(2,1)}, bf16[512,128]{1,0:T(8,128)(2,1)S(1)}, u32[]{:S(2)}, u32[]{:S(2)}) %collective-permute-start.1) | collective-permute-done | bytes 131104 | tf_op jit(solution)/shard_map/ppermute | solution.py:166
  25.3 1.8 %collective-permute-start.6 = (bf16[512,128]{1,0:T(8,128)(2,1)}, bf16[512,128]{1,0:T(8,128)(2,1)S(1)}, u32[]{:S(2)}, u32[]{:S(2)}) collective-permute-start(bf16[512,128]{1,0:T(8,128)(2,1)} %get-tuple-element.28), channel_id=1, source_target_pairs={{0,7},{1,6},{2,5},{3,4},{4,3},{5,2},{6,1},{7,0},{8,15},{9,14},{10,... | collective-permute-start | bytes 393224 | tf_op jit(solution)/shard_map/ppermute | solution.py:166
  27.1 1.1 collective-permute-done.2.refs_3_
  28.2 2.7 %collective-permute-start.7 = (bf16[512,128]{1,0:T(8,128)(2,1)}, bf16[512,128]{1,0:T(8,128)(2,1)S(1)}, u32[]{:S(2)}, u32[]{:S(2)}) collective-permute-start(bf16[512,128]{1,0:T(8,128)(2,1)} %get-tuple-element.29), channel_id=1, source_target_pairs={{0,8},{1,9},{2,10},{3,11},{4,12},{5,13},{6,14},{7,15},{8,0},{9,1},... | collective-permute-start | bytes 393224 | tf_op jit(solution)/shard_map/ppermute | solution.py:166
  30.8 3.3 %collective-permute-start.8 = (bf16[512,128]{1,0:T(8,128)(2,1)}, bf16[512,128]{1,0:T(8,128)(2,1)S(1)}, u32[]{:S(2)}, u32[]{:S(2)}) collective-permute-start(bf16[512,128]{1,0:T(8,128)(2,1)} %get-tuple-element.30), channel_id=1, source_target_pairs={{0,9},{1,8},{2,11},{3,10},{4,13},{5,12},{6,15},{7,14},{8,1},{9,0},... | collective-permute-start | bytes 393224 | tf_op jit(solution)/shard_map/ppermute | solution.py:166
  34.1 0.0 collective-permute-done.4.refs_5_
  34.1 4.0 %collective-permute-start.9 = (bf16[512,128]{1,0:T(8,128)(2,1)}, bf16[512,128]{1,0:T(8,128)(2,1)S(1)}, u32[]{:S(2)}, u32[]{:S(2)}) collective-permute-start(bf16[512,128]{1,0:T(8,128)(2,1)} %get-tuple-element.31), channel_id=1, source_target_pairs={{0,10},{1,11},{2,8},{3,9},{4,14},{5,15},{6,12},{7,13},{8,2},{9,3},... | collective-permute-start | bytes 393224 | tf_op jit(solution)/shard_map/ppermute | solution.py:166
  38.1 7.9 %collective-permute-done.5.refs_6_ = bf16[512,128]{1,0:T(8,128)(2,1)S(1)} collective-permute-done((bf16[512,128]{1,0:T(8,128)(2,1)}, bf16[512,128]{1,0:T(8,128)(2,1)S(1)}, u32[]{:S(2)}, u32[]{:S(2)}) %collective-permute-start.5) | collective-permute-done | bytes 131104 | tf_op jit(solution)/shard_map/ppermute | solution.py:166
  46.1 1.9 %collective-permute-done.6.refs_7_ = bf16[512,128]{1,0:T(8,128)(2,1)S(1)} collective-permute-done((bf16[512,128]{1,0:T(8,128)(2,1)}, bf16[512,128]{1,0:T(8,128)(2,1)S(1)}, u32[]{:S(2)}, u32[]{:S(2)}) %collective-permute-start.6) | collective-permute-done | bytes 131104 | tf_op jit(solution)/shard_map/ppermute | solution.py:166
  48.0 1.8 %collective-permute-start.11 = (bf16[512,128]{1,0:T(8,128)(2,1)}, bf16[512,128]{1,0:T(8,128)(2,1)}, u32[]{:S(2)}, u32[]{:S(2)}) collective-permute-start(bf16[512,128]{1,0:T(8,128)(2,1)} %get-tuple-element.33), channel_id=1, source_target_pairs={{0,12},{1,13},{2,14},{3,15},{4,8},{5,9},{6,10},{7,11},{8,4},{9,5},... | collective-permute-start | bytes 393224 | tf_op jit(solution)/shard_map/ppermute | solution.py:166
  49.8 0.0 collective-permute-done.7.refs_8_
  49.8 1.9 %collective-permute-start.12 = (bf16[512,128]{1,0:T(8,128)(2,1)}, bf16[512,128]{1,0:T(8,128)(2,1)}, u32[]{:S(2)}, u32[]{:S(2)}) collective-permute-start(bf16[512,128]{1,0:T(8,128)(2,1)} %get-tuple-element.34), channel_id=1, source_target_pairs={{0,13},{1,12},{2,15},{3,14},{4,9},{5,8},{6,11},{7,10},{8,5},{9,4},... | collective-permute-start | bytes 393224 | tf_op jit(solution)/shard_map/ppermute | solution.py:166
  51.7 1.2 %collective-permute-start.13 = (bf16[512,128]{1,0:T(8,128)(2,1)}, bf16[512,128]{1,0:T(8,128)(2,1)}, u32[]{:S(2)}, u32[]{:S(2)}) collective-permute-start(bf16[512,128]{1,0:T(8,128)(2,1)} %get-tuple-element.35), channel_id=1, source_target_pairs={{0,14},{1,15},{2,12},{3,13},{4,10},{5,11},{6,8},{7,9},{8,6},{9,7},... | collective-permute-start | bytes 393224 | tf_op jit(solution)/shard_map/ppermute | solution.py:166
  52.9 12.8 %collective-permute-done.9.refs_10_ = bf16[512,128]{1,0:T(8,128)(2,1)S(1)} collective-permute-done((bf16[512,128]{1,0:T(8,128)(2,1)}, bf16[512,128]{1,0:T(8,128)(2,1)S(1)}, u32[]{:S(2)}, u32[]{:S(2)}) %collective-permute-start.9) | collective-permute-done | bytes 131104 | tf_op jit(solution)/shard_map/ppermute | solution.py:166
  65.8 0.6 copy-done.16
  66.4 0.4 collective-permute-start.14
  66.8 0.0 copy-start.5
  66.8 0.8 copy-done.5
  67.6 8.7 %forward.1.spec_hbm = f32[65,128,128]{2,1,0:T(8,128)} custom-call(bf16[16,2,128,128]{3,2,1,0:T(8,128)(2,1)S(1)} %bitcast.9, bf16[128,128]{1,0:T(8,128)(2,1)S(1)} %copy-done.5, bf16[128,384]{1,0:T(8,128)(2,1)S(1)} %copy-done.4, f32[9,64,128]{2,1,0:T(8,128)S(1)} %copy-done.2), custom_call_target="tpu_custom_call" | custom-call | flops 1073741824 | bytes 5242880 | tf_op jit(solution)/shard_map/forward/pallas_call | solution.py:249
  76.3 6.2 %inverse.1 = bf16[16,2,128,128]{3,2,1,0:T(8,128)(2,1)S(1)} custom-call(s32[1]{0:T(128)} %bitcast.place_ref, f32[65,128,128]{2,1,0:T(8,128)} %forward.1.spec_hbm, bf16[192,256]{1,0:T(8,128)(2,1)} %constant.20.clone.matrices_hbm, bf16[512,128]{1,0:T(8,128)(2,1)} %get-tuple-element.21.refs_0_, bf16[512,128]{1,0:T(8,128)(2,1)} %copy-done.7, ...), custom_call_target="tpu_custom_call" | custom-call | flops 805306368 | bytes 6356992 | tf_op jit(solution)/shard_map/inverse/pallas_call | solution.py:419
  82.5 33.8 %all_to_all.10 = bf16[32,128,128]{2,1,0:T(8,128)(2,1)S(1)} all-to-all(bf16[32,128,128]{2,1,0:T(8,128)(2,1)S(1)} %bitcast.7), channel_id=1, replica_groups=mesh['groups'=2,'seq'=16] {'seq','groups'}, dimensions={0} | all-to-all | bytes 2097152 | tf_op jit(solution)/shard_map/all_to_all | solution.py:23
  116.3 2.0 %mix.1 = bf16[256,2048]{1,0:T(8,128)(2,1)} custom-call(bf16[16,2,128,128]{3,2,1,0:T(8,128)(2,1)S(1)} %bitcast.8, bf16[256,2048]{1,0:T(8,128)(2,1)S(1)} %copy-done, bf16[256,2048]{1,0:T(8,128)(2,1)S(1)} %copy-done.1, bf16[256,2048]{1,0:T(8,128)(2,1)S(1)} %copy-done.3, f32[1,2048]{1,0:T(1,128)S(1)} %bitcast.10), custom_call_target="tpu_custom_call" | custom-call | flops 2097152 | bytes 5242880 | tf_op jit(solution)/shard_map/mix/pallas_call | solution.py:468
  (41 shorter events, 0.1 us)
Async XLA Ops:
  0.0 66.8 %copy-start.2 = (f32[9,64,128]{2,1,0:T(8,128)S(1)}, f32[9,64,128]{2,1,0:T(8,128)}, u32[]{:S(2)}) copy-start(f32[9,64,128]{2,1,0:T(8,128)} %constant.19.clone.turn_ref.refs_16_) | copy-start | bytes 884740
  0.0 66.8 %copy-start.4 = (bf16[128,384]{1,0:T(8,128)(2,1)S(1)}, bf16[128,384]{1,0:T(8,128)(2,1)}, u32[]{:S(2)}) copy-start(bf16[128,384]{1,0:T(8,128)(2,1)} %constant.18.clone.second_ref) | copy-start | bytes 294916
  2.6 64.1 %all-to-all-start = ((bf16[32,128,128]{2,1,0:T(8,128)(2,1)}), bf16[32,128,128]{2,1,0:T(8,128)(2,1)S(1)}, u32[]{:S(2)}, u32[]{:S(2)}) async-start(bf16[32,128,128]{2,1,0:T(8,128)(2,1)} %bitcast.11), calls=%async_computation | async-start | bytes 2097152 | tf_op jit(solution)/shard_map/all_to_all | solution.py:23
  10.0 106.2 %copy-start.6 = (f32[2048]{0:T(1024)S(1)}, f32[2048]{0:T(1024)}, u32[]{:S(2)}) copy-start(f32[2048]{0:T(1024)} %param.13) | copy-start | bytes 24580
  15.7 100.6 %copy-start = (bf16[256,2048]{1,0:T(8,128)(2,1)S(1)}, bf16[256,2048]{1,0:T(8,128)(2,1)}, u32[]{:S(2)}) copy-start(bf16[256,2048]{1,0:T(8,128)(2,1)} %signal_ref.3) | copy-start | bytes 3145732
  15.7 100.6 %copy-start.1 = (bf16[256,2048]{1,0:T(8,128)(2,1)S(1)}, bf16[256,2048]{1,0:T(8,128)(2,1)}, u32[]{:S(2)}) copy-start(bf16[256,2048]{1,0:T(8,128)(2,1)} %gate_ref.3) | copy-start | bytes 3145732
  15.7 3.8 %collective-permute-start = (bf16[512,128]{1,0:T(8,128)(2,1)}, bf16[512,128]{1,0:T(8,128)(2,1)S(1)}, u32[]{:S(2)}, u32[]{:S(2)}) collective-permute-start(bf16[512,128]{1,0:T(8,128)(2,1)} %get-tuple-element.22), channel_id=1, source_target_pairs={{0,1},{1,0},{2,3},{3,2},{4,5},{5,4},{6,7},{7,6},{8,9},{9,8},{10,11... | collective-permute-start | bytes 393224 | tf_op jit(solution)/shard_map/ppermute | solution.py:166
  16.0 9.3 %collective-permute-start.1 = (bf16[512,128]{1,0:T(8,128)(2,1)}, bf16[512,128]{1,0:T(8,128)(2,1)S(1)}, u32[]{:S(2)}, u32[]{:S(2)}) collective-permute-start(bf16[512,128]{1,0:T(8,128)(2,1)} %get-tuple-element.23), channel_id=1, source_target_pairs={{0,2},{1,3},{2,0},{3,1},{4,6},{5,7},{6,4},{7,5},{8,10},{9,11},{10,... | collective-permute-start | bytes 393224 | tf_op jit(solution)/shard_map/ppermute | solution.py:166
  17.7 10.4 %collective-permute-start.2 = (bf16[512,128]{1,0:T(8,128)(2,1)}, bf16[512,128]{1,0:T(8,128)(2,1)S(1)}, u32[]{:S(2)}, u32[]{:S(2)}) collective-permute-start(bf16[512,128]{1,0:T(8,128)(2,1)} %get-tuple-element.24), channel_id=1, source_target_pairs={{0,3},{1,2},{2,1},{3,0},{4,7},{5,6},{6,5},{7,4},{8,11},{9,10},{10,... | collective-permute-start | bytes 393224 | tf_op jit(solution)/shard_map/ppermute | solution.py:166
  17.7 13.1 %collective-permute-start.3 = (bf16[512,128]{1,0:T(8,128)(2,1)}, bf16[512,128]{1,0:T(8,128)(2,1)S(1)}, u32[]{:S(2)}, u32[]{:S(2)}) collective-permute-start(bf16[512,128]{1,0:T(8,128)(2,1)} %get-tuple-element.25), channel_id=1, source_target_pairs={{0,4},{1,5},{2,6},{3,7},{4,0},{5,1},{6,2},{7,3},{8,12},{9,13},{10,... | collective-permute-start | bytes 393224 | tf_op jit(solution)/shard_map/ppermute | solution.py:166
  19.4 14.7 %collective-permute-start.4 = (bf16[512,128]{1,0:T(8,128)(2,1)}, bf16[512,128]{1,0:T(8,128)(2,1)S(1)}, u32[]{:S(2)}, u32[]{:S(2)}) collective-permute-start(bf16[512,128]{1,0:T(8,128)(2,1)} %get-tuple-element.26), channel_id=1, source_target_pairs={{0,5},{1,4},{2,7},{3,6},{4,1},{5,0},{6,3},{7,2},{8,13},{9,12},{10,... | collective-permute-start | bytes 393224 | tf_op jit(solution)/shard_map/ppermute | solution.py:166
  19.5 46.2 %copy-start.7 = (bf16[512,128]{1,0:T(8,128)(2,1)}, bf16[512,128]{1,0:T(8,128)(2,1)S(1)}, u32[]{:S(2)}) copy-start(bf16[512,128]{1,0:T(8,128)(2,1)S(1)} %collective-permute-done.refs_1_) | copy-start | bytes 393220
  19.5 26.6 %collective-permute-start.5 = (bf16[512,128]{1,0:T(8,128)(2,1)}, bf16[512,128]{1,0:T(8,128)(2,1)S(1)}, u32[]{:S(2)}, u32[]{:S(2)}) collective-permute-start(bf16[512,128]{1,0:T(8,128)(2,1)} %get-tuple-element.27), channel_id=1, source_target_pairs={{0,6},{1,7},{2,4},{3,5},{4,2},{5,3},{6,0},{7,1},{8,14},{9,15},{10,... | collective-permute-start | bytes 393224 | tf_op jit(solution)/shard_map/ppermute | solution.py:166
  25.3 40.4 %copy-start.8 = (bf16[512,128]{1,0:T(8,128)(2,1)}, bf16[512,128]{1,0:T(8,128)(2,1)S(1)}, u32[]{:S(2)}) copy-start(bf16[512,128]{1,0:T(8,128)(2,1)S(1)} %collective-permute-done.1.refs_2_) | copy-start | bytes 393220
  25.3 22.6 %collective-permute-start.6 = (bf16[512,128]{1,0:T(8,128)(2,1)}, bf16[512,128]{1,0:T(8,128)(2,1)S(1)}, u32[]{:S(2)}, u32[]{:S(2)}) collective-permute-start(bf16[512,128]{1,0:T(8,128)(2,1)} %get-tuple-element.28), channel_id=1, source_target_pairs={{0,7},{1,6},{2,5},{3,4},{4,3},{5,2},{6,1},{7,0},{8,15},{9,14},{10,... | collective-permute-start | bytes 393224 | tf_op jit(solution)/shard_map/ppermute | solution.py:166
  28.2 37.5 %copy-start.9 = (bf16[512,128]{1,0:T(8,128)(2,1)}, bf16[512,128]{1,0:T(8,128)(2,1)S(1)}, u32[]{:S(2)}) copy-start(bf16[512,128]{1,0:T(8,128)(2,1)S(1)} %collective-permute-done.2.refs_3_) | copy-start | bytes 393220
  28.2 21.6 %collective-permute-start.7 = (bf16[512,128]{1,0:T(8,128)(2,1)}, bf16[512,128]{1,0:T(8,128)(2,1)S(1)}, u32[]{:S(2)}, u32[]{:S(2)}) collective-permute-start(bf16[512,128]{1,0:T(8,128)(2,1)} %get-tuple-element.29), channel_id=1, source_target_pairs={{0,8},{1,9},{2,10},{3,11},{4,12},{5,13},{6,14},{7,15},{8,0},{9,1},... | collective-permute-start | bytes 393224 | tf_op jit(solution)/shard_map/ppermute | solution.py:166
  30.8 34.9 %copy-start.10 = (bf16[512,128]{1,0:T(8,128)(2,1)}, bf16[512,128]{1,0:T(8,128)(2,1)S(1)}, u32[]{:S(2)}) copy-start(bf16[512,128]{1,0:T(8,128)(2,1)S(1)} %collective-permute-done.3.refs_4_) | copy-start | bytes 393220
  30.8 20.9 %collective-permute-start.8 = (bf16[512,128]{1,0:T(8,128)(2,1)}, bf16[512,128]{1,0:T(8,128)(2,1)S(1)}, u32[]{:S(2)}, u32[]{:S(2)}) collective-permute-start(bf16[512,128]{1,0:T(8,128)(2,1)} %get-tuple-element.30), channel_id=1, source_target_pairs={{0,9},{1,8},{2,11},{3,10},{4,13},{5,12},{6,15},{7,14},{8,1},{9,0},... | collective-permute-start | bytes 393224 | tf_op jit(solution)/shard_map/ppermute | solution.py:166
  34.1 31.6 %copy-start.11 = (bf16[512,128]{1,0:T(8,128)(2,1)}, bf16[512,128]{1,0:T(8,128)(2,1)S(1)}, u32[]{:S(2)}) copy-start(bf16[512,128]{1,0:T(8,128)(2,1)S(1)} %collective-permute-done.4.refs_5_) | copy-start | bytes 393220
  34.1 31.6 %collective-permute-start.9 = (bf16[512,128]{1,0:T(8,128)(2,1)}, bf16[512,128]{1,0:T(8,128)(2,1)S(1)}, u32[]{:S(2)}, u32[]{:S(2)}) collective-permute-start(bf16[512,128]{1,0:T(8,128)(2,1)} %get-tuple-element.31), channel_id=1, source_target_pairs={{0,10},{1,11},{2,8},{3,9},{4,14},{5,15},{6,12},{7,13},{8,2},{9,3},... | collective-permute-start | bytes 393224 | tf_op jit(solution)/shard_map/ppermute | solution.py:166
  46.1 19.6 %copy-start.12 = (bf16[512,128]{1,0:T(8,128)(2,1)}, bf16[512,128]{1,0:T(8,128)(2,1)S(1)}, u32[]{:S(2)}) copy-start(bf16[512,128]{1,0:T(8,128)(2,1)S(1)} %collective-permute-done.5.refs_6_) | copy-start | bytes 393220
  46.1 30.2 %collective-permute-start.10 = (bf16[512,128]{1,0:T(8,128)(2,1)}, bf16[512,128]{1,0:T(8,128)(2,1)}, u32[]{:S(2)}, u32[]{:S(2)}) collective-permute-start(bf16[512,128]{1,0:T(8,128)(2,1)} %get-tuple-element.32), channel_id=1, source_target_pairs={{0,11},{1,10},{2,9},{3,8},{4,15},{5,14},{6,13},{7,12},{8,3},{9,2},... | collective-permute-start | bytes 393224 | tf_op jit(solution)/shard_map/ppermute | solution.py:166
  48.0 17.8 %copy-start.13 = (bf16[512,128]{1,0:T(8,128)(2,1)}, bf16[512,128]{1,0:T(8,128)(2,1)S(1)}, u32[]{:S(2)}) copy-start(bf16[512,128]{1,0:T(8,128)(2,1)S(1)} %collective-permute-done.6.refs_7_) | copy-start | bytes 393220
  48.0 28.3 %collective-permute-start.11 = (bf16[512,128]{1,0:T(8,128)(2,1)}, bf16[512,128]{1,0:T(8,128)(2,1)}, u32[]{:S(2)}, u32[]{:S(2)}) collective-permute-start(bf16[512,128]{1,0:T(8,128)(2,1)} %get-tuple-element.33), channel_id=1, source_target_pairs={{0,12},{1,13},{2,14},{3,15},{4,8},{5,9},{6,10},{7,11},{8,4},{9,5},... | collective-permute-start | bytes 393224 | tf_op jit(solution)/shard_map/ppermute | solution.py:166
  49.8 16.0 %copy-start.14 = (bf16[512,128]{1,0:T(8,128)(2,1)}, bf16[512,128]{1,0:T(8,128)(2,1)S(1)}, u32[]{:S(2)}) copy-start(bf16[512,128]{1,0:T(8,128)(2,1)S(1)} %collective-permute-done.7.refs_8_) | copy-start | bytes 393220
  49.8 26.5 %collective-permute-start.12 = (bf16[512,128]{1,0:T(8,128)(2,1)}, bf16[512,128]{1,0:T(8,128)(2,1)}, u32[]{:S(2)}, u32[]{:S(2)}) collective-permute-start(bf16[512,128]{1,0:T(8,128)(2,1)} %get-tuple-element.34), channel_id=1, source_target_pairs={{0,13},{1,12},{2,15},{3,14},{4,9},{5,8},{6,11},{7,10},{8,5},{9,4},... | collective-permute-start | bytes 393224 | tf_op jit(solution)/shard_map/ppermute | solution.py:166
  51.7 14.1 %copy-start.15 = (bf16[512,128]{1,0:T(8,128)(2,1)}, bf16[512,128]{1,0:T(8,128)(2,1)S(1)}, u32[]{:S(2)}) copy-start(bf16[512,128]{1,0:T(8,128)(2,1)S(1)} %collective-permute-done.8.refs_9_) | copy-start | bytes 393220
  51.7 24.6 %collective-permute-start.13 = (bf16[512,128]{1,0:T(8,128)(2,1)}, bf16[512,128]{1,0:T(8,128)(2,1)}, u32[]{:S(2)}, u32[]{:S(2)}) collective-permute-start(bf16[512,128]{1,0:T(8,128)(2,1)} %get-tuple-element.35), channel_id=1, source_target_pairs={{0,14},{1,15},{2,12},{3,13},{4,10},{5,11},{6,8},{7,9},{8,6},{9,7},... | collective-permute-start | bytes 393224 | tf_op jit(solution)/shard_map/ppermute | solution.py:166
  66.4 9.9 %collective-permute-start.14 = (bf16[512,128]{1,0:T(8,128)(2,1)}, bf16[512,128]{1,0:T(8,128)(2,1)}, u32[]{:S(2)}, u32[]{:S(2)}) collective-permute-start(bf16[512,128]{1,0:T(8,128)(2,1)} %get-tuple-element.36), channel_id=1, source_target_pairs={{0,15},{1,14},{2,13},{3,12},{4,11},{5,10},{6,9},{7,8},{8,7},{9,6},... | collective-permute-start | bytes 393224 | tf_op jit(solution)/shard_map/ppermute | solution.py:166
  66.7 49.5 %copy-start.3 = (bf16[256,2048]{1,0:T(8,128)(2,1)S(1)}, bf16[256,2048]{1,0:T(8,128)(2,1)}, u32[]{:S(2)}) copy-start(bf16[256,2048]{1,0:T(8,128)(2,1)} %out_gate_ref.1) | copy-start | bytes 3145732
  66.8 0.8 copy-start.5
  (1 other events, 0.7 us)

commit v5 on v4

--- a/solution.py
+++ b/solution.py
@@ -15,6 +15,8 @@
 LANES = 128
 HALF = LANES // 2
 PAD = 8
+PIECES = 4
+JOINED = (8, 10)
 BF16 = jnp.bfloat16
 F32 = jnp.float32
 
@@ -121,12 +123,13 @@
             for half in range(2):
                 near = (2 * block + half) ^ (seq % chunks)
                 chunks_ref[near, rows, :] = halves[half].astype(BF16)
-    for step in range(len(out_refs) // chunks):
+    views = [ref.at[at] for ref in out_refs for at in range(ref.shape[0])]
+    for step in range(len(views) // chunks):
 
         @pl.when(pl.program_id(0) == step)
         def _():
             for near in range(chunks):
-                out_refs[chunks * step + near][...] = chunks_ref[near]
+                views[chunks * step + near][...] = chunks_ref[near]
 
 
 def pack_filter(filter_spectrum, devices_seq):
@@ -136,18 +139,21 @@
     steps = devices_seq // chunks
     size = low * width * channels // 2
     block = (low * width, LANES)
+    shapes = [
+        (1 + (d in JOINED), *block) for d in range(devices_seq) if d - 1 not in JOINED
+    ]
 
     def lanes_of(step, place):
         return (0, 0, 0, place[0] * steps + ((place[1] // chunks) ^ step))
 
     return pl.pallas_call(
         functools.partial(pack_filter_kernel, middle=low * devices_seq // 2),
-        out_shape=[pltpu.HBM(block, BF16)] * devices_seq,
+        out_shape=[pltpu.HBM(shape, BF16) for shape in shapes],
         grid_spec=pltpu.PrefetchScalarGridSpec(
             num_scalar_prefetch=1,
             grid=(steps,),
             in_specs=[pl.BlockSpec((2, low, width, wide), lanes_of)],
-            out_specs=[pl.BlockSpec(block, lambda step, place: (0, 0))] * devices_seq,
+            out_specs=[pl.BlockSpec(shape, lambda step, place: (0, 0, 0)) for shape in shapes],
             scratch_shapes=[pltpu.VMEM((chunks, *block), BF16)],
         ),
         compiler_params=pltpu.CompilerParams(vmem_limit_bytes=16 << 20),
@@ -248,7 +254,7 @@
     first, second, _, turn = tables(half_rows, width)
     return pl.pallas_call(
         functools.partial(forward_kernel, devices_seq=devices_seq),
-        out_shape=pltpu.HBM((half_rows + 1, 2 * width, LANES), F32),
+        out_shape=pltpu.VMEM((half_rows + 1, 2 * width, LANES), F32),
         scratch_shapes=[
             pltpu.VMEM((half_rows * (width + PAD), LANES), F32),
             pltpu.VMEM((width * (2 * half_rows + PAD), LANES), F32),
@@ -264,13 +270,11 @@
 
 
 def inverse_kernel(
-    place_ref, spec_hbm, matrices_hbm, *refs, devices_seq
+    place_ref, spec_ref, matrices_hbm, *refs, devices_seq
 ):
     filter_hbm = refs[:devices_seq]
-    turn_ref, out_ref, spec_ref, filter_ref, lead_ref, matrices_ref = refs[
-        devices_seq : devices_seq + 6
-    ]
-    real_ref, imag_ref, rows_ref, sems, filter_sems = refs[devices_seq + 6 :]
+    turn_ref, out_ref, filter_ref, lead_ref, matrices_ref = refs[devices_seq : devices_seq + 5]
+    real_ref, imag_ref, rows_ref, matrices_sem, filter_sems = refs[devices_seq + 5 :]
     width = turn_ref.shape[1]
     half_rows = spec_ref.shape[0] - 1
     pitch = width + PAD
@@ -286,26 +290,18 @@
         source = place ^ distance
         return jnp.where(upper, devices_seq - 1 - source, source)
 
-    def fetch(distance):
-        at = pl.ds(per_source * block_of(distance), per_source)
-        return pltpu.make_async_copy(spec_hbm.at[at], spec_ref.at[at], sems.at[distance])
-
     def arrival(distance):
         return pltpu.make_async_copy(
-            filter_hbm[distance], filter_ref.at[distance], filter_sems.at[distance]
+            filter_hbm[distance].at[int(distance - 1 in JOINED)],
+            filter_ref.at[distance],
+            filter_sems.at[distance],
         )
 
-    top_rows = pl.ds(half_rows, 1)
-    top = pltpu.make_async_copy(
-        spec_hbm.at[top_rows], spec_ref.at[top_rows], sems.at[top_block]
-    )
-    matrices = pltpu.make_async_copy(matrices_hbm, matrices_ref, sems.at[top_block + 1])
+    matrices = pltpu.make_async_copy(matrices_hbm, matrices_ref, matrices_sem)
     matrices.start()
     for distance in range(top_block):
-        fetch(distance).start()
         arrival(distance).start()
         arrival(devices_seq - 1 - distance).start()
-    top.start()
     matrices.wait()
     third_matrix = matrices_ref[: 2 * width]
     last_matrix = matrices_ref[2 * width :]
@@ -356,7 +352,6 @@
     for distance in range(top_block):
         block = block_of(distance)
         far = devices_seq - 1 - distance
-        fetch(distance).wait()
         arrival(distance).wait()
         arrival(far).wait()
         for near in (distance, far):
@@ -369,7 +364,6 @@
             pair = slots[at : at + 2]
             for slot, values in zip(pair, third_stage(pair)):
                 keep(slot[0], values)
-    top.wait()
     slots = [(0, lead_ref[0], 0, 0), (half_rows, lead_ref[top_block], top_block, 0)]
     first, middle = third_stage(slots)
     keep(0, (first[0], middle[0]))
@@ -419,17 +413,16 @@
     return pl.pallas_call(
         functools.partial(inverse_kernel, devices_seq=devices_seq),
         out_shape=jax.ShapeDtypeStruct((devices_seq, 2, piece, LANES), BF16),
-        in_specs=[pl.BlockSpec(memory_space=pltpu.SMEM)]
-        + [pl.BlockSpec(memory_space=pltpu.HBM)] * (2 + devices_seq)
+        in_specs=[pl.BlockSpec(memory_space=pltpu.SMEM), pl.BlockSpec(memory_space=pltpu.VMEM)]
+        + [pl.BlockSpec(memory_space=pltpu.HBM)] * (1 + devices_seq)
         + [pl.BlockSpec(memory_space=pltpu.VMEM)],
         scratch_shapes=[
-            pltpu.VMEM(spectrum.shape, F32),
-            pltpu.VMEM((devices_seq, *arrived[0].shape), BF16),
+            pltpu.VMEM((devices_seq, *arrived[0].shape[1:]), BF16),
             pltpu.VMEM((devices_seq, width, LANES), F32),
             pltpu.VMEM(matrices.shape, BF16),
         ]
         + [pltpu.VMEM((half_rows * (width + PAD), LANES), F32)] * 3
-        + [pltpu.SemaphoreType.DMA((half_rows // 8 + 2,)), pltpu.SemaphoreType.DMA((devices_seq,))],
+        + [pltpu.SemaphoreType.DMA, pltpu.SemaphoreType.DMA((devices_seq,))],
         compiler_params=pltpu.CompilerParams(vmem_limit_bytes=20 << 20),
         cost_estimate=pl.CostEstimate(
             flops=2 * LANES * matrices.size * width,
@@ -439,29 +432,41 @@
         name="inverse",
     )(
         lax.axis_index("seq").reshape(1),
+        pltpu.with_memory_space_constraint(spectrum, pltpu.VMEM),
         *(
             pltpu.with_memory_space_constraint(operand, pltpu.HBM)
-            for operand in (spectrum, jnp.asarray(matrices), *arrived)
+            for operand in (jnp.asarray(matrices), *arrived)
         ),
         turn,
     )
 
 
-def mix_kernel(conv_ref, signal_ref, gate_ref, out_gate_ref, gain_ref, out_ref):
+def mix_kernel(conv_ref, signal_ref, gate_ref, out_gate_ref, gain_ref, out_hbm, out_ref, sems):
     rows = signal_ref.shape[0] // 2
-    for block in range(signal_ref.shape[1] // LANES):
-        lanes = pl.ds(block * LANES, LANES)
-        gain = gain_ref[:, lanes]
-        place = divmod(2 * block, conv_ref.shape[0])
-        halves = swap_halves(
-            conv_ref[place[1], place[0]].astype(F32), conv_ref[place[1] + 1, place[0]].astype(F32)
-        )
-        for half, convolved in enumerate(halves):
-            at = pl.ds(half * rows, rows)
-            gated = signal_ref[at, lanes].astype(F32) * gate_ref[at, lanes].astype(F32)
-            gated = gated.astype(BF16).astype(F32)
-            mixed = out_gate_ref[at, lanes].astype(F32) * (convolved + gain * gated)
-            out_ref[at, lanes] = mixed.astype(BF16)
+    pieces = sems.shape[0]
+    wide = signal_ref.shape[1] // pieces
+
+    def leave(piece):
+        lanes = pl.ds(piece * wide, wide)
+        return pltpu.make_async_copy(out_ref.at[:, lanes], out_hbm.at[:, lanes], sems.at[piece])
+
+    for piece in range(pieces):
+        for start in range(piece * wide, (piece + 1) * wide, LANES):
+            lanes = pl.ds(start, LANES)
+            gain = gain_ref[:, lanes]
+            group, seq = divmod(start // HALF, conv_ref.shape[0])
+            halves = swap_halves(
+                conv_ref[seq, group].astype(F32), conv_ref[seq + 1, group].astype(F32)
+            )
+            for half, convolved in enumerate(halves):
+                at = pl.ds(half * rows, rows)
+                gated = signal_ref[at, lanes].astype(F32) * gate_ref[at, lanes].astype(F32)
+                gated = gated.astype(BF16).astype(F32)
+                mixed = out_gate_ref[at, lanes].astype(F32) * (convolved + gain * gated)
+                out_ref[at, lanes] = mixed.astype(BF16)
+        leave(piece).start()
+    for piece in range(pieces):
+        leave(piece).wait()
 
 
 def mix(conv, signal, input_gate, output_gate, skip_gain):
@@ -469,6 +474,8 @@
         mix_kernel,
         out_shape=jax.ShapeDtypeStruct(signal.shape, BF16),
         in_specs=[pl.BlockSpec(memory_space=pltpu.VMEM)] * 5,
+        out_specs=pl.BlockSpec(memory_space=pltpu.HBM),
+        scratch_shapes=[pltpu.VMEM(signal.shape, BF16), pltpu.SemaphoreType.DMA((PIECES,))],
         compiler_params=pltpu.CompilerParams(vmem_limit_bytes=16 << 20),
         cost_estimate=pl.CostEstimate(
             flops=4 * signal.size, bytes_accessed=10 * signal.size, transcendentals=0
@@ -486,7 +493,13 @@
 
     got = pairs(pack_input(signal, input_gate, devices_seq))
     packed = pack_filter(filter_spectrum, devices_seq)
-    arrived = [packed[0]] + [swap_with(packed[d], d) for d in range(1, devices_seq)]
+    packed = iter(packed)
+    arrived = [next(packed)]
+    for distance in range(1, devices_seq):
+        if distance - 1 in JOINED:
+            arrived.append(swap_with(arrived[-1], 1))
+        else:
+            arrived.append(swap_with(next(packed), distance))
     spectrum = forward(got, devices_seq, width)
     conv = inverse(spectrum, arrived, devices_seq, signal.shape[0] // 2)
     return mix(pairs(conv), signal, input_gate, output_gate, skip_gain)

time: 119 us -> 118 us (level)
  waiting for transfers between devices: 26.9 us -> 31.5 us
  starting transfers between devices: 30.8 us -> 28.4 us
  Pallas kernels: 25.1 us -> 23.1 us
    ppermute x15, waiting for transfers between devices: 26.9 us -> 31.5 us  [swap_with(): lax.ppermute(values, 'seq', [(i, i ^ distance) for i in range(count)])]
    ppermute x15, starting transfers between devices: 23.5 us -> 21.1 us  [swap_with(): lax.ppermute(values, 'seq', [(i, i ^ distance) for i in range(count)])]
    pallas_call x1, Pallas kernels: 8.66 us -> 6.71 us  [forward(): pl.pallas_call(functools.partial(forward_kernel, devices_seq=devices_seq)...]
  transfers between devices with their start and end apart: 16 -> 16, of which waited for: 5 -> 6; matrix products, arithmetic and copies ran while one was open for 0% -> 0% of each run, Pallas kernels for 12% -> 11%
where the time goes in v5:
time: 118 us
  blocking collectives  33 us (28%)
  waiting for transfers between devices  31.5 us (27%)
  starting transfers between devices  28.4 us (24%)
  Pallas kernels  23.1 us (20%)
  local copies, waits for them, and re-layouts  1.48 us (1%)
    all_to_all x1, blocking collectives, exchange(): return lax.all_to_all(values, axes, split_axis=0, concat_axis=0, tiled=True)  33 us
    ppermute x15, waiting for transfers between devices, swap_with(): lax.ppermute(values, 'seq', [(i, i ^ distance) for i in range(count)])  31.5 us
    ppermute x15, starting transfers between devices, swap_with(): lax.ppermute(values, 'seq', [(i, i ^ distance) for i in range(count)])  21.1 us
    all_to_all x1, starting transfers between devices, exchange(): return lax.all_to_all(values, axes, split_axis=0, concat_axis=0, tiled=True)  7.3 us
    pallas_call x1, Pallas kernels, forward(): pl.pallas_call(functools.partial(forward_kernel, devices_seq=devices_seq)...  6.71 us
    pallas_call x1, Pallas kernels, inverse(): pl.pallas_call(functools.partial(inverse_kernel, devices_seq=devices_seq)...  6.3 us
    pallas_call x1, Pallas kernels, pack_filter(): pl.pallas_call(functools.partial(pack_filter_kernel, middle=low * devices...  5.71 us
    pallas_call x1, Pallas kernels, pack_input(): pl.pallas_call(pack_input_kernel, out_shape=jax.ShapeDtypeStruct((devices...  2.63 us
  transfers between devices with their start and end apart: 16, of which 6 were waited for; matrix products, arithmetic and copies ran while one was open for 0% of the time, Pallas kernels for 11%

profile of v5, /device:TPU:0, one launch (start us, length us, event | category | flops | bytes accessed | tf_op | source)
XLA Modules:
  0.0 117.7 jit_solution(10092320327098677182)
XLA Ops:
  0.0 2.6 %pack_input.1 = bf16[16,2,128,128]{3,2,1,0:T(8,128)(2,1)} custom-call(bf16[256,2048]{1,0:T(8,128)(2,1)} %signal_ref.3, bf16[256,2048]{1,0:T(8,128)(2,1)} %gate_ref.3), custom_call_target="tpu_custom_call" | custom-call | flops 524288 | bytes 3145728 | tf_op jit(solution)/shard_map/pack_input/pallas_call | solution.py:91
  2.6 7.3 %all-to-all-start = ((bf16[32,128,128]{2,1,0:T(8,128)(2,1)}), bf16[32,128,128]{2,1,0:T(8,128)(2,1)S(1)}, u32[]{:S(2)}, u32[]{:S(2)}) async-start(bf16[32,128,128]{2,1,0:T(8,128)(2,1)} %bitcast.11), calls=%async_computation | async-start | bytes 2097152 | tf_op jit(solution)/shard_map/all_to_all | solution.py:25
  9.9 0.1 pad_add_fusion.place_ref
  10.0 5.7 %pack_filter.1 = (bf16[1,512,128]{2,1,0:T(8,128)(2,1)}, bf16[1,512,128]{2,1,0:T(8,128)(2,1)}, bf16[1,512,128]{2,1,0:T(8,128)(2,1)}, bf16[1,512,128]{2,1,0:T(8,12...) custom-call(s32[2]{0:T(128)S(1)} %pad_add_fusion.place_ref, ...), custom_call_target="tpu_custom_call" | custom-call | flops 134217728 | bytes 6291456 | tf_op jit(solution)/shard_map/pack_filter/pallas_call | solution.py:149
  15.7 0.3 collective-permute-start
  16.1 1.7 %collective-permute-start.1 = (bf16[1,512,128]{2,1,0:T(8,128)(2,1)}, bf16[1,512,128]{2,1,0:T(8,128)(2,1)S(1)}, u32[]{:S(2)}, u32[]{:S(2)}) collective-permute-start(bf16[1,512,128]{2,1,0:T(8,128)(2,1)} %get-tuple-element.21), channel_id=1, source_target_pairs={{0,2},{1,3},{2,0},{3,1},{4,6},{5,7},{6,4},{7,5},{8,10},{9,11},{10,... | collective-permute-start | bytes 393224 | tf_op jit(solution)/shard_map/ppermute | solution.py:172
  17.7 2.4 %collective-permute-start.7 = (bf16[2,512,128]{2,1,0:T(8,128)(2,1)}, bf16[2,512,128]{2,1,0:T(8,128)(2,1)}, u32[]{:S(2)}, u32[]{:S(2)}) collective-permute-start(bf16[2,512,128]{2,1,0:T(8,128)(2,1)} %get-tuple-element.27), channel_id=1, source_target_pairs={{0,8},{1,9},{2,10},{3,11},{4,12},{5,13},{6,14},{7,15},{8,0},{9,1},... | collective-permute-start | bytes 786440 | tf_op jit(solution)/shard_map/ppermute | solution.py:172
  20.1 0.3 collective-permute-start.9
  20.4 0.8 collective-permute-start.2
  21.2 0.0 collective-permute-done.refs_1_
  21.2 1.5 %collective-permute-start.3 = (bf16[1,512,128]{2,1,0:T(8,128)(2,1)}, bf16[1,512,128]{2,1,0:T(8,128)(2,1)S(1)}, u32[]{:S(2)}, u32[]{:S(2)}) collective-permute-start(bf16[1,512,128]{2,1,0:T(8,128)(2,1)} %get-tuple-element.23), channel_id=1, source_target_pairs={{0,4},{1,5},{2,6},{3,7},{4,0},{5,1},{6,2},{7,3},{8,12},{9,13},{10,... | collective-permute-start | bytes 393224 | tf_op jit(solution)/shard_map/ppermute | solution.py:172
  22.7 2.7 %collective-permute-done.1.refs_2_ = bf16[1,512,128]{2,1,0:T(8,128)(2,1)S(1)} collective-permute-done((bf16[1,512,128]{2,1,0:T(8,128)(2,1)}, bf16[1,512,128]{2,1,0:T(8,128)(2,1)S(1)}, u32[]{:S(2)}, u32[]{:S(2)}) %collective-permute-start.1) | collective-permute-done | bytes 131104 | tf_op jit(solution)/shard_map/ppermute | solution.py:172
  25.4 0.0 collective-permute-start.4
  25.4 2.8 %collective-permute-done.2.refs_3_ = bf16[1,512,128]{2,1,0:T(8,128)(2,1)S(1)} collective-permute-done((bf16[1,512,128]{2,1,0:T(8,128)(2,1)}, bf16[1,512,128]{2,1,0:T(8,128)(2,1)S(1)}, u32[]{:S(2)}, u32[]{:S(2)}) %collective-permute-start.2) | collective-permute-done | bytes 131104 | tf_op jit(solution)/shard_map/ppermute | solution.py:172
  28.2 2.8 %collective-permute-start.5 = (bf16[1,512,128]{2,1,0:T(8,128)(2,1)}, bf16[1,512,128]{2,1,0:T(8,128)(2,1)S(1)}, u32[]{:S(2)}, u32[]{:S(2)}) collective-permute-start(bf16[1,512,128]{2,1,0:T(8,128)(2,1)} %get-tuple-element.25), channel_id=1, source_target_pairs={{0,6},{1,7},{2,4},{3,5},{4,2},{5,3},{6,0},{7,1},{8,14},{9,15},{10,... | collective-permute-start | bytes 393224 | tf_op jit(solution)/shard_map/ppermute | solution.py:172
  31.0 11.1 %collective-permute-done.3.refs_4_ = bf16[1,512,128]{2,1,0:T(8,128)(2,1)S(1)} collective-permute-done((bf16[1,512,128]{2,1,0:T(8,128)(2,1)}, bf16[1,512,128]{2,1,0:T(8,128)(2,1)S(1)}, u32[]{:S(2)}, u32[]{:S(2)}) %collective-permute-start.3) | collective-permute-done | bytes 131104 | tf_op jit(solution)/shard_map/ppermute | solution.py:172
  42.1 2.4 %collective-permute-start.6 = (bf16[1,512,128]{2,1,0:T(8,128)(2,1)}, bf16[1,512,128]{2,1,0:T(8,128)(2,1)S(1)}, u32[]{:S(2)}, u32[]{:S(2)}) collective-permute-start(bf16[1,512,128]{2,1,0:T(8,128)(2,1)} %get-tuple-element.26), channel_id=1, source_target_pairs={{0,7},{1,6},{2,5},{3,4},{4,3},{5,2},{6,1},{7,0},{8,15},{9,14},{10,... | collective-permute-start | bytes 393224 | tf_op jit(solution)/shard_map/ppermute | solution.py:172
  44.5 0.4 collective-permute-done.4.refs_5_
  44.9 3.6 %collective-permute-start.11 = (bf16[1,512,128]{2,1,0:T(8,128)(2,1)}, bf16[1,512,128]{2,1,0:T(8,128)(2,1)S(1)}, u32[]{:S(2)}, u32[]{:S(2)}) collective-permute-start(bf16[1,512,128]{2,1,0:T(8,128)(2,1)} %get-tuple-element.29), channel_id=1, source_target_pairs={{0,12},{1,13},{2,14},{3,15},{4,8},{5,9},{6,10},{7,11},{8,4},{9,5},... | collective-permute-start | bytes 393224 | tf_op jit(solution)/shard_map/ppermute | solution.py:172
  48.5 5.3 %collective-permute-done.7.refs_8_ = bf16[2,512,128]{2,1,0:T(8,128)(2,1)} collective-permute-done((bf16[2,512,128]{2,1,0:T(8,128)(2,1)}, bf16[2,512,128]{2,1,0:T(8,128)(2,1)}, u32[]{:S(2)}, u32[]{:S(2)}) %collective-permute-start.7) | collective-permute-done | bytes 262176 | tf_op jit(solution)/shard_map/ppermute | solution.py:172
  53.8 9.2 %collective-permute-done.9.refs_10_ = bf16[2,512,128]{2,1,0:T(8,128)(2,1)} collective-permute-done((bf16[2,512,128]{2,1,0:T(8,128)(2,1)}, bf16[2,512,128]{2,1,0:T(8,128)(2,1)}, u32[]{:S(2)}, u32[]{:S(2)}) %collective-permute-start.9) | collective-permute-done | bytes 262176 | tf_op jit(solution)/shard_map/ppermute | solution.py:172
  63.0 0.0 collective-permute-start.10
  63.0 1.2 collective-permute-start.12
  64.2 2.8 %collective-permute-start.13 = (bf16[1,512,128]{2,1,0:T(8,128)(2,1)}, bf16[1,512,128]{2,1,0:T(8,128)(2,1)}, u32[]{:S(2)}, u32[]{:S(2)}) collective-permute-start(bf16[1,512,128]{2,1,0:T(8,128)(2,1)} %get-tuple-element.31), channel_id=1, source_target_pairs={{0,14},{1,15},{2,12},{3,13},{4,10},{5,11},{6,8},{7,9},{8,6},{9,7},... | collective-permute-start | bytes 393224 | tf_op jit(solution)/shard_map/ppermute | solution.py:172
  67.0 0.6 copy-done.14
  67.6 1.4 %collective-permute-start.14 = (bf16[1,512,128]{2,1,0:T(8,128)(2,1)}, bf16[1,512,128]{2,1,0:T(8,128)(2,1)}, u32[]{:S(2)}, u32[]{:S(2)}) collective-permute-start(bf16[1,512,128]{2,1,0:T(8,128)(2,1)} %get-tuple-element.32), channel_id=1, source_target_pairs={{0,15},{1,14},{2,13},{3,12},{4,11},{5,10},{6,9},{7,8},{8,7},{9,6},... | collective-permute-start | bytes 393224 | tf_op jit(solution)/shard_map/ppermute | solution.py:172
  69.0 0.0 copy-start.5
  69.0 0.8 copy-done.5
  69.8 6.7 %forward.1.spec_ref = f32[65,128,128]{2,1,0:T(8,128)S(1)} custom-call(bf16[16,2,128,128]{3,2,1,0:T(8,128)(2,1)S(1)} %bitcast.8, bf16[128,128]{1,0:T(8,128)(2,1)S(1)} %copy-done.5, bf16[128,384]{1,0:T(8,128)(2,1)S(1)} %copy-done.4, f32[9,64,128]{2,1,0:T(8,128)S(1)} %copy-done.2), custom_call_target="tpu_custom_call" | custom-call | flops 1073741824 | bytes 5242880 | tf_op jit(solution)/shard_map/forward/pallas_call | solution.py:255
  76.6 6.3 %inverse.1 = bf16[16,2,128,128]{3,2,1,0:T(8,128)(2,1)S(1)} custom-call(s32[1]{0:T(128)} %bitcast.place_ref, f32[65,128,128]{2,1,0:T(8,128)S(1)} %forward.1.spec_ref, bf16[192,256]{1,0:T(8,128)(2,1)} %constant.20.clone.matrices_hbm, bf16[1,512,128]{2,1,0:T(8,128)(2,1)} %get-tuple-element.19.refs_0_, bf16[1,512,128]{2,1,0:T(8,128)(2,1)} %copy-done.7, ...), custom_call_target="tpu_custom_call" | custom-call | flops 805306368 | bytes 6356992 | tf_op jit(solution)/shard_map/inverse/pallas_call | solution.py:413
  82.9 33.0 %all_to_all.10 = bf16[32,128,128]{2,1,0:T(8,128)(2,1)S(1)} all-to-all(bf16[32,128,128]{2,1,0:T(8,128)(2,1)S(1)} %bitcast.9), channel_id=1, replica_groups=mesh['groups'=2,'seq'=16] {'seq','groups'}, dimensions={0} | all-to-all | bytes 2097152 | tf_op jit(solution)/shard_map/all_to_all | solution.py:25
  115.9 1.8 %mix.1 = bf16[256,2048]{1,0:T(8,128)(2,1)} custom-call(bf16[16,2,128,128]{3,2,1,0:T(8,128)(2,1)S(1)} %bitcast.7, bf16[256,2048]{1,0:T(8,128)(2,1)S(1)} %copy-done, bf16[256,2048]{1,0:T(8,128)(2,1)S(1)} %copy-done.1, bf16[256,2048]{1,0:T(8,128)(2,1)S(1)} %copy-done.3, f32[1,2048]{1,0:T(1,128)S(1)} %bitcast.10), custom_call_target="tpu_custom_call" | custom-call | flops 2097152 | bytes 5242880 | tf_op jit(solution)/shard_map/mix/pallas_call | solution.py:473
  (37 shorter events, 0.1 us)
Async XLA Ops:
  0.0 69.0 %copy-start.2 = (f32[9,64,128]{2,1,0:T(8,128)S(1)}, f32[9,64,128]{2,1,0:T(8,128)}, u32[]{:S(2)}) copy-start(f32[9,64,128]{2,1,0:T(8,128)} %constant.19.clone.turn_ref.refs_16_) | copy-start | bytes 884740
  0.0 69.0 %copy-start.4 = (bf16[128,384]{1,0:T(8,128)(2,1)S(1)}, bf16[128,384]{1,0:T(8,128)(2,1)}, u32[]{:S(2)}) copy-start(bf16[128,384]{1,0:T(8,128)(2,1)} %constant.18.clone.second_ref) | copy-start | bytes 294916
  2.6 66.3 %all-to-all-start = ((bf16[32,128,128]{2,1,0:T(8,128)(2,1)}), bf16[32,128,128]{2,1,0:T(8,128)(2,1)S(1)}, u32[]{:S(2)}, u32[]{:S(2)}) async-start(bf16[32,128,128]{2,1,0:T(8,128)(2,1)} %bitcast.11), calls=%async_computation | async-start | bytes 2097152 | tf_op jit(solution)/shard_map/all_to_all | solution.py:25
  10.0 105.9 %copy-start.6 = (f32[2048]{0:T(1024)S(1)}, f32[2048]{0:T(1024)}, u32[]{:S(2)}) copy-start(f32[2048]{0:T(1024)} %param.13) | copy-start | bytes 24580
  15.7 100.2 %copy-start = (bf16[256,2048]{1,0:T(8,128)(2,1)S(1)}, bf16[256,2048]{1,0:T(8,128)(2,1)}, u32[]{:S(2)}) copy-start(bf16[256,2048]{1,0:T(8,128)(2,1)} %signal_ref.3) | copy-start | bytes 3145732
  15.7 100.2 %copy-start.1 = (bf16[256,2048]{1,0:T(8,128)(2,1)S(1)}, bf16[256,2048]{1,0:T(8,128)(2,1)}, u32[]{:S(2)}) copy-start(bf16[256,2048]{1,0:T(8,128)(2,1)} %gate_ref.3) | copy-start | bytes 3145732
  15.7 5.5 %collective-permute-start = (bf16[1,512,128]{2,1,0:T(8,128)(2,1)}, bf16[1,512,128]{2,1,0:T(8,128)(2,1)S(1)}, u32[]{:S(2)}, u32[]{:S(2)}) collective-permute-start(bf16[1,512,128]{2,1,0:T(8,128)(2,1)} %get-tuple-element.20), channel_id=1, source_target_pairs={{0,1},{1,0},{2,3},{3,2},{4,5},{5,4},{6,7},{7,6},{8,9},{9,8},{10,11... | collective-permute-start | bytes 393224 | tf_op jit(solution)/shard_map/ppermute | solution.py:172
  16.1 9.3 %collective-permute-start.1 = (bf16[1,512,128]{2,1,0:T(8,128)(2,1)}, bf16[1,512,128]{2,1,0:T(8,128)(2,1)S(1)}, u32[]{:S(2)}, u32[]{:S(2)}) collective-permute-start(bf16[1,512,128]{2,1,0:T(8,128)(2,1)} %get-tuple-element.21), channel_id=1, source_target_pairs={{0,2},{1,3},{2,0},{3,1},{4,6},{5,7},{6,4},{7,5},{8,10},{9,11},{10,... | collective-permute-start | bytes 393224 | tf_op jit(solution)/shard_map/ppermute | solution.py:172
  17.7 36.0 %collective-permute-start.7 = (bf16[2,512,128]{2,1,0:T(8,128)(2,1)}, bf16[2,512,128]{2,1,0:T(8,128)(2,1)}, u32[]{:S(2)}, u32[]{:S(2)}) collective-permute-start(bf16[2,512,128]{2,1,0:T(8,128)(2,1)} %get-tuple-element.27), channel_id=1, source_target_pairs={{0,8},{1,9},{2,10},{3,11},{4,12},{5,13},{6,14},{7,15},{8,0},{9,1},... | collective-permute-start | bytes 786440 | tf_op jit(solution)/shard_map/ppermute | solution.py:172
  20.1 42.9 %collective-permute-start.9 = (bf16[2,512,128]{2,1,0:T(8,128)(2,1)}, bf16[2,512,128]{2,1,0:T(8,128)(2,1)}, u32[]{:S(2)}, u32[]{:S(2)}) collective-permute-start(bf16[2,512,128]{2,1,0:T(8,128)(2,1)} %get-tuple-element.28), channel_id=1, source_target_pairs={{0,10},{1,11},{2,8},{3,9},{4,14},{5,15},{6,12},{7,13},{8,2},{9,3},... | collective-permute-start | bytes 786440 | tf_op jit(solution)/shard_map/ppermute | solution.py:172
  20.4 7.7 %collective-permute-start.2 = (bf16[1,512,128]{2,1,0:T(8,128)(2,1)}, bf16[1,512,128]{2,1,0:T(8,128)(2,1)S(1)}, u32[]{:S(2)}, u32[]{:S(2)}) collective-permute-start(bf16[1,512,128]{2,1,0:T(8,128)(2,1)} %get-tuple-element.22), channel_id=1, source_target_pairs={{0,3},{1,2},{2,1},{3,0},{4,7},{5,6},{6,5},{7,4},{8,11},{9,10},{10,... | collective-permute-start | bytes 393224 | tf_op jit(solution)/shard_map/ppermute | solution.py:172
  21.2 45.7 %copy-start.7 = (bf16[1,512,128]{2,1,0:T(8,128)(2,1)}, bf16[1,512,128]{2,1,0:T(8,128)(2,1)S(1)}, u32[]{:S(2)}) copy-start(bf16[1,512,128]{2,1,0:T(8,128)(2,1)S(1)} %collective-permute-done.refs_1_) | copy-start | bytes 393220
  21.2 20.8 %collective-permute-start.3 = (bf16[1,512,128]{2,1,0:T(8,128)(2,1)}, bf16[1,512,128]{2,1,0:T(8,128)(2,1)S(1)}, u32[]{:S(2)}, u32[]{:S(2)}) collective-permute-start(bf16[1,512,128]{2,1,0:T(8,128)(2,1)} %get-tuple-element.23), channel_id=1, source_target_pairs={{0,4},{1,5},{2,6},{3,7},{4,0},{5,1},{6,2},{7,3},{8,12},{9,13},{10,... | collective-permute-start | bytes 393224 | tf_op jit(solution)/shard_map/ppermute | solution.py:172
  25.4 41.6 %copy-start.8 = (bf16[1,512,128]{2,1,0:T(8,128)(2,1)}, bf16[1,512,128]{2,1,0:T(8,128)(2,1)S(1)}, u32[]{:S(2)}) copy-start(bf16[1,512,128]{2,1,0:T(8,128)(2,1)S(1)} %collective-permute-done.1.refs_2_) | copy-start | bytes 393220
  25.4 19.5 %collective-permute-start.4 = (bf16[1,512,128]{2,1,0:T(8,128)(2,1)}, bf16[1,512,128]{2,1,0:T(8,128)(2,1)S(1)}, u32[]{:S(2)}, u32[]{:S(2)}) collective-permute-start(bf16[1,512,128]{2,1,0:T(8,128)(2,1)} %get-tuple-element.24), channel_id=1, source_target_pairs={{0,5},{1,4},{2,7},{3,6},{4,1},{5,0},{6,3},{7,2},{8,13},{9,12},{10,... | collective-permute-start | bytes 393224 | tf_op jit(solution)/shard_map/ppermute | solution.py:172
  28.2 38.8 %copy-start.9 = (bf16[1,512,128]{2,1,0:T(8,128)(2,1)}, bf16[1,512,128]{2,1,0:T(8,128)(2,1)S(1)}, u32[]{:S(2)}) copy-start(bf16[1,512,128]{2,1,0:T(8,128)(2,1)S(1)} %collective-permute-done.2.refs_3_) | copy-start | bytes 393220
  28.2 34.8 %collective-permute-start.5 = (bf16[1,512,128]{2,1,0:T(8,128)(2,1)}, bf16[1,512,128]{2,1,0:T(8,128)(2,1)S(1)}, u32[]{:S(2)}, u32[]{:S(2)}) collective-permute-start(bf16[1,512,128]{2,1,0:T(8,128)(2,1)} %get-tuple-element.25), channel_id=1, source_target_pairs={{0,6},{1,7},{2,4},{3,5},{4,2},{5,3},{6,0},{7,1},{8,14},{9,15},{10,... | collective-permute-start | bytes 393224 | tf_op jit(solution)/shard_map/ppermute | solution.py:172
  42.1 24.9 %copy-start.10 = (bf16[1,512,128]{2,1,0:T(8,128)(2,1)}, bf16[1,512,128]{2,1,0:T(8,128)(2,1)S(1)}, u32[]{:S(2)}) copy-start(bf16[1,512,128]{2,1,0:T(8,128)(2,1)S(1)} %collective-permute-done.3.refs_4_) | copy-start | bytes 393220
  42.1 22.1 %collective-permute-start.6 = (bf16[1,512,128]{2,1,0:T(8,128)(2,1)}, bf16[1,512,128]{2,1,0:T(8,128)(2,1)S(1)}, u32[]{:S(2)}, u32[]{:S(2)}) collective-permute-start(bf16[1,512,128]{2,1,0:T(8,128)(2,1)} %get-tuple-element.26), channel_id=1, source_target_pairs={{0,7},{1,6},{2,5},{3,4},{4,3},{5,2},{6,1},{7,0},{8,15},{9,14},{10,... | collective-permute-start | bytes 393224 | tf_op jit(solution)/shard_map/ppermute | solution.py:172
  44.9 22.1 %copy-start.11 = (bf16[1,512,128]{2,1,0:T(8,128)(2,1)}, bf16[1,512,128]{2,1,0:T(8,128)(2,1)S(1)}, u32[]{:S(2)}) copy-start(bf16[1,512,128]{2,1,0:T(8,128)(2,1)S(1)} %collective-permute-done.4.refs_5_) | copy-start | bytes 393220
  44.9 22.0 %collective-permute-start.11 = (bf16[1,512,128]{2,1,0:T(8,128)(2,1)}, bf16[1,512,128]{2,1,0:T(8,128)(2,1)S(1)}, u32[]{:S(2)}, u32[]{:S(2)}) collective-permute-start(bf16[1,512,128]{2,1,0:T(8,128)(2,1)} %get-tuple-element.29), channel_id=1, source_target_pairs={{0,12},{1,13},{2,14},{3,15},{4,8},{5,9},{6,10},{7,11},{8,4},{9,5},... | collective-permute-start | bytes 393224 | tf_op jit(solution)/shard_map/ppermute | solution.py:172
  53.8 22.8 %collective-permute-start.8 = (bf16[2,512,128]{2,1,0:T(8,128)(2,1)}, bf16[2,512,128]{2,1,0:T(8,128)(2,1)}, u32[]{:S(2)}, u32[]{:S(2)}) collective-permute-start(bf16[2,512,128]{2,1,0:T(8,128)(2,1)} %collective-permute-done.7.refs_8_), channel_id=1, source_target_pairs={{0,1},{1,0},{2,3},{3,2},{4,5},{5,4},{6,7},{7,6},{8,9},{9,8},{10,11... | collective-permute-start | bytes 786440 | tf_op jit(solution)/shard_map/ppermute | solution.py:172
  63.0 13.6 %collective-permute-start.10 = (bf16[2,512,128]{2,1,0:T(8,128)(2,1)}, bf16[2,512,128]{2,1,0:T(8,128)(2,1)}, u32[]{:S(2)}, u32[]{:S(2)}) collective-permute-start(bf16[2,512,128]{2,1,0:T(8,128)(2,1)} %collective-permute-done.9.refs_10_), channel_id=1, source_target_pairs={{0,1},{1,0},{2,3},{3,2},{4,5},{5,4},{6,7},{7,6},{8,9},{9,8},{10,11... | collective-permute-start | bytes 786440 | tf_op jit(solution)/shard_map/ppermute | solution.py:172
  63.0 4.0 %copy-start.12 = (bf16[1,512,128]{2,1,0:T(8,128)(2,1)}, bf16[1,512,128]{2,1,0:T(8,128)(2,1)S(1)}, u32[]{:S(2)}) copy-start(bf16[1,512,128]{2,1,0:T(8,128)(2,1)S(1)} %collective-permute-done.5.refs_6_) | copy-start | bytes 393220
  63.0 13.5 %collective-permute-start.12 = (bf16[1,512,128]{2,1,0:T(8,128)(2,1)}, bf16[1,512,128]{2,1,0:T(8,128)(2,1)}, u32[]{:S(2)}, u32[]{:S(2)}) collective-permute-start(bf16[1,512,128]{2,1,0:T(8,128)(2,1)} %get-tuple-element.30), channel_id=1, source_target_pairs={{0,13},{1,12},{2,15},{3,14},{4,9},{5,8},{6,11},{7,10},{8,5},{9,4},... | collective-permute-start | bytes 393224 | tf_op jit(solution)/shard_map/ppermute | solution.py:172
  64.2 2.8 %copy-start.13 = (bf16[1,512,128]{2,1,0:T(8,128)(2,1)}, bf16[1,512,128]{2,1,0:T(8,128)(2,1)S(1)}, u32[]{:S(2)}) copy-start(bf16[1,512,128]{2,1,0:T(8,128)(2,1)S(1)} %collective-permute-done.6.refs_7_) | copy-start | bytes 393220
  64.2 12.4 %collective-permute-start.13 = (bf16[1,512,128]{2,1,0:T(8,128)(2,1)}, bf16[1,512,128]{2,1,0:T(8,128)(2,1)}, u32[]{:S(2)}, u32[]{:S(2)}) collective-permute-start(bf16[1,512,128]{2,1,0:T(8,128)(2,1)} %get-tuple-element.31), channel_id=1, source_target_pairs={{0,14},{1,15},{2,12},{3,13},{4,10},{5,11},{6,8},{7,9},{8,6},{9,7},... | collective-permute-start | bytes 393224 | tf_op jit(solution)/shard_map/ppermute | solution.py:172
  66.9 0.7 copy-start.14
  67.6 9.0 %collective-permute-start.14 = (bf16[1,512,128]{2,1,0:T(8,128)(2,1)}, bf16[1,512,128]{2,1,0:T(8,128)(2,1)}, u32[]{:S(2)}, u32[]{:S(2)}) collective-permute-start(bf16[1,512,128]{2,1,0:T(8,128)(2,1)} %get-tuple-element.32), channel_id=1, source_target_pairs={{0,15},{1,14},{2,13},{3,12},{4,11},{5,10},{6,9},{7,8},{8,7},{9,6},... | collective-permute-start | bytes 393224 | tf_op jit(solution)/shard_map/ppermute | solution.py:172
  69.0 47.0 %copy-start.3 = (bf16[256,2048]{1,0:T(8,128)(2,1)S(1)}, bf16[256,2048]{1,0:T(8,128)(2,1)}, u32[]{:S(2)}) copy-start(bf16[256,2048]{1,0:T(8,128)(2,1)} %out_gate_ref.1) | copy-start | bytes 3145732
  69.0 0.8 copy-start.5

commit v6 on v5

--- a/solution.py
+++ b/solution.py
@@ -16,7 +16,8 @@
 HALF = LANES // 2
 PAD = 8
 PIECES = 4
-JOINED = (8, 10)
+JOINED = ()
+EARLY = (7, 6, 5, 4)
 BF16 = jnp.bfloat16
 F32 = jnp.float32
 
@@ -269,18 +270,19 @@
     )(got, first, second, turn)
 
 
-def inverse_kernel(
-    place_ref, spec_ref, matrices_hbm, *refs, devices_seq
-):
-    filter_hbm = refs[:devices_seq]
-    turn_ref, out_ref, filter_ref, lead_ref, matrices_ref = refs[devices_seq : devices_seq + 5]
-    real_ref, imag_ref, rows_ref, matrices_sem, filter_sems = refs[devices_seq + 5 :]
+def inverse_kernel(place_ref, spec_ref, turn_ref, matrices_hbm, *refs, devices_seq, early):
+    distances = EARLY if early else [d for d in range(devices_seq // 2) if d not in EARLY]
+    filter_hbm, refs = refs[:devices_seq], refs[devices_seq:]
+    if early:
+        real_ref, imag_ref, filter_ref, matrices_ref, matrices_sem, filter_sems = refs
+    else:
+        (_, _, out_ref, real_ref, imag_ref) = refs[:5]
+        filter_ref, matrices_ref, matrices_sem, filter_sems, lead_ref, rows_ref = refs[5:]
     width = turn_ref.shape[1]
     half_rows = spec_ref.shape[0] - 1
     pitch = width + PAD
     per_source = 8
     left = left_lanes(width)
-
     top_block = half_rows // per_source
 
     place = place_ref[0]
@@ -290,18 +292,26 @@
         source = place ^ distance
         return jnp.where(upper, devices_seq - 1 - source, source)
 
-    def arrival(distance):
+    def arrival(distance, count=None):
+        rows = pl.ds(0, count or filter_ref.shape[1])
         return pltpu.make_async_copy(
-            filter_hbm[distance].at[int(distance - 1 in JOINED)],
-            filter_ref.at[distance],
+            filter_hbm[distance].at[int(distance - 1 in JOINED), rows],
+            filter_ref.at[distance, rows],
             filter_sems.at[distance],
         )
 
+    def pair_of(distance):
+        return distance, devices_seq - 1 - distance
+
     matrices = pltpu.make_async_copy(matrices_hbm, matrices_ref, matrices_sem)
     matrices.start()
-    for distance in range(top_block):
-        arrival(distance).start()
-        arrival(devices_seq - 1 - distance).start()
+    for distance in distances:
+        for near in pair_of(distance):
+            arrival(near).start()
+    if not early:
+        for distance in EARLY:
+            for near in pair_of(distance):
+                arrival(near, width).start()
     matrices.wait()
     third_matrix = matrices_ref[: 2 * width]
     last_matrix = matrices_ref[2 * width :]
@@ -349,13 +359,10 @@
         real_ref[pl.ds(at, width), :] = values[0]
         imag_ref[pl.ds(at, width), :] = values[1]
 
-    for distance in range(top_block):
+    for distance in distances:
         block = block_of(distance)
-        far = devices_seq - 1 - distance
-        arrival(distance).wait()
-        arrival(far).wait()
-        for near in (distance, far):
-            lead_ref[place ^ near] = filter_ref[near, :width].astype(F32)
+        for near in pair_of(distance):
+            arrival(near).wait()
         slots = [
             (per_source * block + v, response_of(distance, v), block, v)
             for v in range(1, per_source)
@@ -364,6 +371,13 @@
             pair = slots[at : at + 2]
             for slot, values in zip(pair, third_stage(pair)):
                 keep(slot[0], values)
+    if early:
+        return
+    for distance in EARLY:
+        for near in pair_of(distance):
+            arrival(near, width).wait()
+    for distance in range(devices_seq):
+        lead_ref[place ^ distance] = filter_ref[distance, :width].astype(F32)
     slots = [(0, lead_ref[0], 0, 0), (half_rows, lead_ref[top_block], top_block, 0)]
     first, middle = third_stage(slots)
     keep(0, (first[0], middle[0]))
@@ -410,35 +424,60 @@
     width = spectrum.shape[1] // 2
     half_rows = spectrum.shape[0] - 1
     _, _, matrices, turn = tables(half_rows, width)
-    return pl.pallas_call(
-        functools.partial(inverse_kernel, devices_seq=devices_seq),
-        out_shape=jax.ShapeDtypeStruct((devices_seq, 2, piece, LANES), BF16),
-        in_specs=[pl.BlockSpec(memory_space=pltpu.SMEM), pl.BlockSpec(memory_space=pltpu.VMEM)]
-        + [pl.BlockSpec(memory_space=pltpu.HBM)] * (1 + devices_seq)
-        + [pl.BlockSpec(memory_space=pltpu.VMEM)],
-        scratch_shapes=[
-            pltpu.VMEM((devices_seq, *arrived[0].shape[1:]), BF16),
-            pltpu.VMEM((devices_seq, width, LANES), F32),
-            pltpu.VMEM(matrices.shape, BF16),
+    stage = pltpu.VMEM((half_rows * (width + PAD), LANES), F32)
+    block = arrived[0].shape[1:]
+
+    def in_hbm(operand):
+        return pltpu.with_memory_space_constraint(jnp.asarray(operand), pltpu.HBM)
+
+    def in_vmem(operand):
+        return pltpu.with_memory_space_constraint(operand, pltpu.VMEM)
+
+    vmem = pl.BlockSpec(memory_space=pltpu.VMEM)
+    specs = [pl.BlockSpec(memory_space=pltpu.SMEM), vmem, vmem] + [
+        pl.BlockSpec(memory_space=pltpu.HBM)
+    ] * (1 + devices_seq)
+    scratch = [
+        pltpu.VMEM((devices_seq, *block), BF16),
+        pltpu.VMEM(matrices.shape, BF16),
+        pltpu.SemaphoreType.DMA,
+        pltpu.SemaphoreType.DMA((devices_seq,)),
+    ]
+
+    def call(early, more_in, out_shape, more_scratch, aliases):
+        used = [d for e in EARLY for d in (e, devices_seq - 1 - e)]
+        rows = [
+            in_hbm(arrived[d] if d in used or not early else arrived[used[0]])
+            for d in range(devices_seq)
         ]
-        + [pltpu.VMEM((half_rows * (width + PAD), LANES), F32)] * 3
-        + [pltpu.SemaphoreType.DMA, pltpu.SemaphoreType.DMA((devices_seq,))],
-        compiler_params=pltpu.CompilerParams(vmem_limit_bytes=20 << 20),
-        cost_estimate=pl.CostEstimate(
-            flops=2 * LANES * matrices.size * width,
-            bytes_accessed=4 * spectrum.size + 2 * devices_seq * arrived[0].size,
-            transcendentals=0,
-        ),
-        name="inverse",
-    )(
-        lax.axis_index("seq").reshape(1),
-        pltpu.with_memory_space_constraint(spectrum, pltpu.VMEM),
-        *(
-            pltpu.with_memory_space_constraint(operand, pltpu.HBM)
-            for operand in (jnp.asarray(matrices), *arrived)
-        ),
-        turn,
-    )
+        operands = [lax.axis_index("seq").reshape(1), in_vmem(spectrum), turn, in_hbm(matrices)]
+        operands += rows + more_in
+        return pl.pallas_call(
+            functools.partial(inverse_kernel, devices_seq=devices_seq, early=early),
+            out_shape=out_shape,
+            in_specs=specs + [vmem] * len(more_in),
+            out_specs=[vmem] * len(out_shape),
+            scratch_shapes=scratch + more_scratch,
+            input_output_aliases={
+                len(specs) + at: to for at, to in enumerate(aliases)
+            },
+            compiler_params=pltpu.CompilerParams(vmem_limit_bytes=20 << 20),
+            cost_estimate=pl.CostEstimate(
+                flops=LANES * matrices.size * width,
+                bytes_accessed=2 * devices_seq * block[0] * block[1],
+                transcendentals=0,
+            ),
+            name="inverse_early" if early else "inverse_late",
+        )(*operands)
+
+    real, imag = call(True, [], [stage, stage], [], [])
+    return call(
+        False,
+        [in_vmem(real), in_vmem(imag)],
+        [jax.ShapeDtypeStruct((devices_seq, 2, piece, LANES), BF16), stage, stage],
+        [pltpu.VMEM((devices_seq, width, LANES), F32), stage],
+        [1, 2],
+    )[0]
 
 
 def mix_kernel(conv_ref, signal_ref, gate_ref, out_gate_ref, gain_ref, out_hbm, out_ref, sems):

time: 118 us -> 117 us (level)
  waiting for transfers between devices: 31.5 us -> 28.5 us
  Pallas kernels: 23.1 us -> 24.3 us
    ppermute x15, waiting for transfers between devices: 31.5 us -> 28.5 us  [swap_with(): lax.ppermute(values, 'seq', [(i, i ^ distance) for i in range(count)])]
    pallas_call x1 -> x2, Pallas kernels: 6.3 us -> 7.55 us  [call(): pl.pallas_call(functools.partial(inverse_kernel, devices_seq=devices_seq,...]
  transfers between devices with their start and end apart: 16 -> 16, of which waited for: 6 -> 6; matrix products, arithmetic and copies ran while one was open for 0% -> 0% of each run, Pallas kernels for 11% -> 13%
where the time goes in v6:
time: 117 us
  blocking collectives  34 us (29%)
  starting transfers between devices  29.1 us (25%)
  waiting for transfers between devices  28.5 us (24%)
  Pallas kernels  24.3 us (21%)
    all_to_all x1, blocking collectives, exchange(): return lax.all_to_all(values, axes, split_axis=0, concat_axis=0, tiled=True)  34 us
    ppermute x15, waiting for transfers between devices, swap_with(): lax.ppermute(values, 'seq', [(i, i ^ distance) for i in range(count)])  28.5 us
    ppermute x15, starting transfers between devices, swap_with(): lax.ppermute(values, 'seq', [(i, i ^ distance) for i in range(count)])  21.8 us
    pallas_call x2, Pallas kernels, call(): pl.pallas_call(functools.partial(inverse_kernel, devices_seq=devices_seq,...  7.55 us
    all_to_all x1, starting transfers between devices, exchange(): return lax.all_to_all(values, axes, split_axis=0, concat_axis=0, tiled=True)  7.3 us
    pallas_call x1, Pallas kernels, forward(): pl.pallas_call(functools.partial(forward_kernel, devices_seq=devices_seq)...  6.69 us
    pallas_call x1, Pallas kernels, pack_filter(): pl.pallas_call(functools.partial(pack_filter_kernel, middle=low * devices...  5.76 us
    pallas_call x1, Pallas kernels, pack_input(): pl.pallas_call(pack_input_kernel, out_shape=jax.ShapeDtypeStruct((devices...  2.58 us
  transfers between devices with their start and end apart: 16, of which 6 were waited for; matrix products, arithmetic and copies ran while one was open for 0% of the time, Pallas kernels for 13%

profile of v6, /device:TPU:0, one launch (start us, length us, event | category | flops | bytes accessed | tf_op | source)
XLA Modules:
  0.0 117.1 jit_solution(7419971343608585089)
XLA Ops:
  0.0 2.6 %pack_input.1 = bf16[16,2,128,128]{3,2,1,0:T(8,128)(2,1)} custom-call(bf16[256,2048]{1,0:T(8,128)(2,1)} %signal_ref.3, bf16[256,2048]{1,0:T(8,128)(2,1)} %gate_ref.3), custom_call_target="tpu_custom_call" | custom-call | flops 524288 | bytes 3145728 | tf_op jit(solution)/shard_map/pack_input/pallas_call | solution.py:92
  2.6 7.3 %all-to-all-start = ((bf16[32,128,128]{2,1,0:T(8,128)(2,1)}), bf16[32,128,128]{2,1,0:T(8,128)(2,1)S(1)}, u32[]{:S(2)}, u32[]{:S(2)}) async-start(bf16[32,128,128]{2,1,0:T(8,128)(2,1)} %bitcast.11), calls=%async_computation | async-start | bytes 2097152 | tf_op jit(solution)/shard_map/all_to_all | solution.py:26
  9.9 0.1 pad_add_fusion.place_ref
  10.0 5.8 %pack_filter.1 = (bf16[1,512,128]{2,1,0:T(8,128)(2,1)}, bf16[1,512,128]{2,1,0:T(8,128)(2,1)}, bf16[1,512,128]{2,1,0:T(8,128)(2,1)}, bf16[1,512,128]{2,1,0:T(8,12...) custom-call(s32[2]{0:T(128)S(1)} %pad_add_fusion.place_ref, ...), custom_call_target="tpu_custom_call" | custom-call | flops 134217728 | bytes 6291456 | tf_op jit(solution)/shard_map/pack_filter/pallas_call | solution.py:150
  15.7 0.3 collective-permute-start
  16.0 1.7 %collective-permute-start.1 = (bf16[1,512,128]{2,1,0:T(8,128)(2,1)}, bf16[1,512,128]{2,1,0:T(8,128)(2,1)S(1)}, u32[]{:S(2)}, u32[]{:S(2)}) collective-permute-start(bf16[1,512,128]{2,1,0:T(8,128)(2,1)} %get-tuple-element.26), channel_id=1, source_target_pairs={{0,2},{1,3},{2,0},{3,1},{4,6},{5,7},{6,4},{7,5},{8,10},{9,11},{10,... | collective-permute-start | bytes 393224 | tf_op jit(solution)/shard_map/ppermute | solution.py:173
  17.7 1.5 %collective-permute-start.3 = (bf16[1,512,128]{2,1,0:T(8,128)(2,1)}, bf16[1,512,128]{2,1,0:T(8,128)(2,1)S(1)}, u32[]{:S(2)}, u32[]{:S(2)}) collective-permute-start(bf16[1,512,128]{2,1,0:T(8,128)(2,1)} %get-tuple-element.28), channel_id=1, source_target_pairs={{0,4},{1,5},{2,6},{3,7},{4,0},{5,1},{6,2},{7,3},{8,12},{9,13},{10,... | collective-permute-start | bytes 393224 | tf_op jit(solution)/shard_map/ppermute | solution.py:173
  19.1 1.4 %collective-permute-start.5 = (bf16[1,512,128]{2,1,0:T(8,128)(2,1)}, bf16[1,512,128]{2,1,0:T(8,128)(2,1)S(1)}, u32[]{:S(2)}, u32[]{:S(2)}) collective-permute-start(bf16[1,512,128]{2,1,0:T(8,128)(2,1)} %get-tuple-element.30), channel_id=1, source_target_pairs={{0,6},{1,7},{2,4},{3,5},{4,2},{5,3},{6,0},{7,1},{8,14},{9,15},{10,... | collective-permute-start | bytes 393224 | tf_op jit(solution)/shard_map/ppermute | solution.py:173
  20.6 1.5 %collective-permute-start.6 = (bf16[1,512,128]{2,1,0:T(8,128)(2,1)}, bf16[1,512,128]{2,1,0:T(8,128)(2,1)S(1)}, u32[]{:S(2)}, u32[]{:S(2)}) collective-permute-start(bf16[1,512,128]{2,1,0:T(8,128)(2,1)} %get-tuple-element.31), channel_id=1, source_target_pairs={{0,7},{1,6},{2,5},{3,4},{4,3},{5,2},{6,1},{7,0},{8,15},{9,14},{10,... | collective-permute-start | bytes 393224 | tf_op jit(solution)/shard_map/ppermute | solution.py:173
  22.1 3.0 %collective-permute-done.1.refs_2_ = bf16[1,512,128]{2,1,0:T(8,128)(2,1)S(1)} collective-permute-done((bf16[1,512,128]{2,1,0:T(8,128)(2,1)}, bf16[1,512,128]{2,1,0:T(8,128)(2,1)S(1)}, u32[]{:S(2)}, u32[]{:S(2)}) %collective-permute-start.1) | collective-permute-done | bytes 131104 | tf_op jit(solution)/shard_map/ppermute | solution.py:173
  25.1 2.4 %collective-permute-start.7 = (bf16[1,512,128]{2,1,0:T(8,128)(2,1)}, bf16[1,512,128]{2,1,0:T(8,128)(2,1)S(1)}, u32[]{:S(2)}, u32[]{:S(2)}) collective-permute-start(bf16[1,512,128]{2,1,0:T(8,128)(2,1)} %get-tuple-element.32), channel_id=1, source_target_pairs={{0,8},{1,9},{2,10},{3,11},{4,12},{5,13},{6,14},{7,15},{8,0},{9,1},... | collective-permute-start | bytes 393224 | tf_op jit(solution)/shard_map/ppermute | solution.py:173
  27.4 3.4 %collective-permute-done.3.refs_4_ = bf16[1,512,128]{2,1,0:T(8,128)(2,1)S(1)} collective-permute-done((bf16[1,512,128]{2,1,0:T(8,128)(2,1)}, bf16[1,512,128]{2,1,0:T(8,128)(2,1)S(1)}, u32[]{:S(2)}, u32[]{:S(2)}) %collective-permute-start.3) | collective-permute-done | bytes 131104 | tf_op jit(solution)/shard_map/ppermute | solution.py:173
  30.8 3.3 %collective-permute-start.8 = (bf16[1,512,128]{2,1,0:T(8,128)(2,1)}, bf16[1,512,128]{2,1,0:T(8,128)(2,1)S(1)}, u32[]{:S(2)}, u32[]{:S(2)}) collective-permute-start(bf16[1,512,128]{2,1,0:T(8,128)(2,1)} %get-tuple-element.33), channel_id=1, source_target_pairs={{0,9},{1,8},{2,11},{3,10},{4,13},{5,12},{6,15},{7,14},{8,1},{9,0},... | collective-permute-start | bytes 393224 | tf_op jit(solution)/shard_map/ppermute | solution.py:173
  34.1 4.0 %collective-permute-start.9 = (bf16[1,512,128]{2,1,0:T(8,128)(2,1)}, bf16[1,512,128]{2,1,0:T(8,128)(2,1)S(1)}, u32[]{:S(2)}, u32[]{:S(2)}) collective-permute-start(bf16[1,512,128]{2,1,0:T(8,128)(2,1)} %get-tuple-element.34), channel_id=1, source_target_pairs={{0,10},{1,11},{2,8},{3,9},{4,14},{5,15},{6,12},{7,13},{8,2},{9,3},... | collective-permute-start | bytes 393224 | tf_op jit(solution)/shard_map/ppermute | solution.py:173
  38.1 7.9 %collective-permute-done.5.refs_6_ = bf16[1,512,128]{2,1,0:T(8,128)(2,1)S(1)} collective-permute-done((bf16[1,512,128]{2,1,0:T(8,128)(2,1)}, bf16[1,512,128]{2,1,0:T(8,128)(2,1)S(1)}, u32[]{:S(2)}, u32[]{:S(2)}) %collective-permute-start.5) | collective-permute-done | bytes 131104 | tf_op jit(solution)/shard_map/ppermute | solution.py:173
  46.0 1.9 %collective-permute-done.6.refs_0_.refs_1_.refs_2_.refs_3_.refs_7_.refs_12_.refs_13_.refs_14_.refs_15_ = bf16[1,512,128]{2,1,0:T(8,128)(2,1)S(1)} collective-permute-done((bf16[1,512,128]{2,1,0:T(8,128)(2,1)}, bf16[1,512,128]{2,1,0:T(8,128)(2,1)S(1)}, u32[]{:S(2)}, u32[]{:S(2)}) %collective-permute-start.6) | collective-permute-done | bytes 131104 | tf_op jit(solution)/shard_map/ppermute | solution.py:173
  47.9 0.7 collective-permute-start.2
  48.6 1.3 %collective-permute-start.11 = (bf16[1,512,128]{2,1,0:T(8,128)(2,1)}, bf16[1,512,128]{2,1,0:T(8,128)(2,1)S(1)}, u32[]{:S(2)}, u32[]{:S(2)}) collective-permute-start(bf16[1,512,128]{2,1,0:T(8,128)(2,1)} %get-tuple-element.36), channel_id=1, source_target_pairs={{0,12},{1,13},{2,14},{3,15},{4,8},{5,9},{6,10},{7,11},{8,4},{9,5},... | collective-permute-start | bytes 393224 | tf_op jit(solution)/shard_map/ppermute | solution.py:173
  49.9 1.8 %collective-permute-start.12 = (bf16[1,512,128]{2,1,0:T(8,128)(2,1)}, bf16[1,512,128]{2,1,0:T(8,128)(2,1)S(1)}, u32[]{:S(2)}, u32[]{:S(2)}) collective-permute-start(bf16[1,512,128]{2,1,0:T(8,128)(2,1)} %get-tuple-element.37), channel_id=1, source_target_pairs={{0,13},{1,12},{2,15},{3,14},{4,9},{5,8},{6,11},{7,10},{8,5},{9,4},... | collective-permute-start | bytes 393224 | tf_op jit(solution)/shard_map/ppermute | solution.py:173
  51.7 11.1 %collective-permute-done.9.refs_10_ = bf16[1,512,128]{2,1,0:T(8,128)(2,1)S(1)} collective-permute-done((bf16[1,512,128]{2,1,0:T(8,128)(2,1)}, bf16[1,512,128]{2,1,0:T(8,128)(2,1)S(1)}, u32[]{:S(2)}, u32[]{:S(2)}) %collective-permute-start.9) | collective-permute-done | bytes 131104 | tf_op jit(solution)/shard_map/ppermute | solution.py:173
  62.8 0.6 collective-permute-start.13
  63.5 1.2 %collective-permute-done.10.refs_11_ = bf16[1,512,128]{2,1,0:T(8,128)(2,1)S(1)} collective-permute-done((bf16[1,512,128]{2,1,0:T(8,128)(2,1)}, bf16[1,512,128]{2,1,0:T(8,128)(2,1)S(1)}, u32[]{:S(2)}, u32[]{:S(2)}) %collective-permute-start.10) | collective-permute-done | bytes 131104 | tf_op jit(solution)/shard_map/ppermute | solution.py:173
  64.7 1.4 %collective-permute-start.14 = (bf16[1,512,128]{2,1,0:T(8,128)(2,1)}, bf16[1,512,128]{2,1,0:T(8,128)(2,1)S(1)}, u32[]{:S(2)}, u32[]{:S(2)}) collective-permute-start(bf16[1,512,128]{2,1,0:T(8,128)(2,1)} %get-tuple-element.39), channel_id=1, source_target_pairs={{0,15},{1,14},{2,13},{3,12},{4,11},{5,10},{6,9},{7,8},{8,7},{9,6},... | collective-permute-start | bytes 393224 | tf_op jit(solution)/shard_map/ppermute | solution.py:173
  66.1 6.7 %forward.1.spec_ref = f32[65,128,128]{2,1,0:T(8,128)S(1)} custom-call(bf16[16,2,128,128]{3,2,1,0:T(8,128)(2,1)S(1)} %bitcast.8, bf16[128,128]{1,0:T(8,128)(2,1)S(1)} %copy-done.5, bf16[128,384]{1,0:T(8,128)(2,1)S(1)} %copy-done.4, f32[9,64,128]{2,1,0:T(8,128)S(1)} %copy-done.2), custom_call_target="tpu_custom_call" | custom-call | flops 1073741824 | bytes 5242880 | tf_op jit(solution)/shard_map/forward/pallas_call | solution.py:256
  72.9 2.8 %inverse_early.1 = (f32[4608,128]{1,0:T(8,128)S(1)}, f32[4608,128]{1,0:T(8,128)S(1)}) custom-call(s32[1]{0:T(128)} %bitcast.place_ref, f32[65,128,128]{2,1,0:T(8,128)S(1)} %forward.1.spec_ref, f32[9,64,128]{2,1,0:T(8,128)S(1)} %copy-done.2, bf16[192,256]{1,0:T(8,128)(2,1)} %constant.20.clone.matrices_hbm, bf16[1,512,128]{2,1,0:T(8,128)(2,1)} %copy-done.7, ...), custom_call_target="tpu_custom_call" | custom-call | flops 402653184 | bytes 2097152 | tf_op jit(solution)/shard_map/inverse_early/pallas_call | solution.py:455
  75.8 0.6 copy-done.17
  76.4 0.0 copy-done.18
  76.5 0.1 copy-done.20
  76.5 0.0 copy-done.21
  76.5 4.7 %inverse_late.1 = (bf16[16,2,128,128]{3,2,1,0:T(8,128)(2,1)S(1)}, f32[4608,128]{1,0:T(8,128)S(1)}, f32[4608,128]{1,0:T(8,128)S(1)}) custom-call(s32[1]{0:T(128)} %bitcast.place_ref, f32[65,128,128]{2,1,0:T(8,128)S(1)} %forward.1.spec_ref, f32[9,64,128]{2,1,0:T(8,128)S(1)} %copy-done.2, ...), custom_call_target="tpu_custom_call", output_to_operand_aliasing={{1}: (20, {}), {2}: (21, {})} | custom-call | flops 402653184 | bytes 2097152 | tf_op jit(solution)/shard_map/inverse_late/pallas_call | solution.py:455
  81.3 34.0 %all_to_all.10 = bf16[32,128,128]{2,1,0:T(8,128)(2,1)S(1)} all-to-all(bf16[32,128,128]{2,1,0:T(8,128)(2,1)S(1)} %bitcast.9), channel_id=1, replica_groups=mesh['groups'=2,'seq'=16] {'seq','groups'}, dimensions={0} | all-to-all | bytes 2097152 | tf_op jit(solution)/shard_map/all_to_all | solution.py:26
  115.4 1.7 %mix.1 = bf16[256,2048]{1,0:T(8,128)(2,1)} custom-call(bf16[16,2,128,128]{3,2,1,0:T(8,128)(2,1)S(1)} %bitcast.7, bf16[256,2048]{1,0:T(8,128)(2,1)S(1)} %copy-done, bf16[256,2048]{1,0:T(8,128)(2,1)S(1)} %copy-done.1, bf16[256,2048]{1,0:T(8,128)(2,1)S(1)} %copy-done.3, f32[1,2048]{1,0:T(1,128)S(1)} %bitcast.10), custom_call_target="tpu_custom_call" | custom-call | flops 2097152 | bytes 5242880 | tf_op jit(solution)/shard_map/mix/pallas_call | solution.py:512
  (52 shorter events, 0.1 us)
Async XLA Ops:
  2.6 63.5 %all-to-all-start = ((bf16[32,128,128]{2,1,0:T(8,128)(2,1)}), bf16[32,128,128]{2,1,0:T(8,128)(2,1)S(1)}, u32[]{:S(2)}, u32[]{:S(2)}) async-start(bf16[32,128,128]{2,1,0:T(8,128)(2,1)} %bitcast.11), calls=%async_computation | async-start | bytes 2097152 | tf_op jit(solution)/shard_map/all_to_all | solution.py:26
  10.0 56.1 %copy-start.2 = (f32[9,64,128]{2,1,0:T(8,128)S(1)}, f32[9,64,128]{2,1,0:T(8,128)}, u32[]{:S(2)}) copy-start(f32[9,64,128]{2,1,0:T(8,128)} %constant.19.clone.turn_ref) | copy-start | bytes 884740
  10.0 56.1 %copy-start.4 = (bf16[128,384]{1,0:T(8,128)(2,1)S(1)}, bf16[128,384]{1,0:T(8,128)(2,1)}, u32[]{:S(2)}) copy-start(bf16[128,384]{1,0:T(8,128)(2,1)} %constant.18.clone.second_ref) | copy-start | bytes 294916
  10.0 56.1 %copy-start.5 = (bf16[128,128]{1,0:T(8,128)(2,1)S(1)}, bf16[128,128]{1,0:T(8,128)(2,1)}, u32[]{:S(2)}) copy-start(bf16[128,128]{1,0:T(8,128)(2,1)} %constant.17.clone.first_ref) | copy-start | bytes 98308
  15.7 4.8 %collective-permute-start = (bf16[1,512,128]{2,1,0:T(8,128)(2,1)}, bf16[1,512,128]{2,1,0:T(8,128)(2,1)S(1)}, u32[]{:S(2)}, u32[]{:S(2)}) collective-permute-start(bf16[1,512,128]{2,1,0:T(8,128)(2,1)} %get-tuple-element.25), channel_id=1, source_target_pairs={{0,1},{1,0},{2,3},{3,2},{4,5},{5,4},{6,7},{7,6},{8,9},{9,8},{10,11... | collective-permute-start | bytes 393224 | tf_op jit(solution)/shard_map/ppermute | solution.py:173
  16.0 9.1 %collective-permute-start.1 = (bf16[1,512,128]{2,1,0:T(8,128)(2,1)}, bf16[1,512,128]{2,1,0:T(8,128)(2,1)S(1)}, u32[]{:S(2)}, u32[]{:S(2)}) collective-permute-start(bf16[1,512,128]{2,1,0:T(8,128)(2,1)} %get-tuple-element.26), channel_id=1, source_target_pairs={{0,2},{1,3},{2,0},{3,1},{4,6},{5,7},{6,4},{7,5},{8,10},{9,11},{10,... | collective-permute-start | bytes 393224 | tf_op jit(solution)/shard_map/ppermute | solution.py:173
  17.7 13.1 %collective-permute-start.3 = (bf16[1,512,128]{2,1,0:T(8,128)(2,1)}, bf16[1,512,128]{2,1,0:T(8,128)(2,1)S(1)}, u32[]{:S(2)}, u32[]{:S(2)}) collective-permute-start(bf16[1,512,128]{2,1,0:T(8,128)(2,1)} %get-tuple-element.28), channel_id=1, source_target_pairs={{0,4},{1,5},{2,6},{3,7},{4,0},{5,1},{6,2},{7,3},{8,12},{9,13},{10,... | collective-permute-start | bytes 393224 | tf_op jit(solution)/shard_map/ppermute | solution.py:173
  19.1 14.9 %collective-permute-start.4 = (bf16[1,512,128]{2,1,0:T(8,128)(2,1)}, bf16[1,512,128]{2,1,0:T(8,128)(2,1)S(1)}, u32[]{:S(2)}, u32[]{:S(2)}) collective-permute-start(bf16[1,512,128]{2,1,0:T(8,128)(2,1)} %get-tuple-element.29), channel_id=1, source_target_pairs={{0,5},{1,4},{2,7},{3,6},{4,1},{5,0},{6,3},{7,2},{8,13},{9,12},{10,... | collective-permute-start | bytes 393224 | tf_op jit(solution)/shard_map/ppermute | solution.py:173
  19.1 26.9 %collective-permute-start.5 = (bf16[1,512,128]{2,1,0:T(8,128)(2,1)}, bf16[1,512,128]{2,1,0:T(8,128)(2,1)S(1)}, u32[]{:S(2)}, u32[]{:S(2)}) collective-permute-start(bf16[1,512,128]{2,1,0:T(8,128)(2,1)} %get-tuple-element.30), channel_id=1, source_target_pairs={{0,6},{1,7},{2,4},{3,5},{4,2},{5,3},{6,0},{7,1},{8,14},{9,15},{10,... | collective-permute-start | bytes 393224 | tf_op jit(solution)/shard_map/ppermute | solution.py:173
  20.6 52.2 %copy-start.15 = (bf16[1,512,128]{2,1,0:T(8,128)(2,1)}, bf16[1,512,128]{2,1,0:T(8,128)(2,1)S(1)}, u32[]{:S(2)}) copy-start(bf16[1,512,128]{2,1,0:T(8,128)(2,1)S(1)} %collective-permute-done.refs_1_) | copy-start | bytes 393220
  20.6 27.3 %collective-permute-start.6 = (bf16[1,512,128]{2,1,0:T(8,128)(2,1)}, bf16[1,512,128]{2,1,0:T(8,128)(2,1)S(1)}, u32[]{:S(2)}, u32[]{:S(2)}) collective-permute-start(bf16[1,512,128]{2,1,0:T(8,128)(2,1)} %get-tuple-element.31), channel_id=1, source_target_pairs={{0,7},{1,6},{2,5},{3,4},{4,3},{5,2},{6,1},{7,0},{8,15},{9,14},{10,... | collective-permute-start | bytes 393224 | tf_op jit(solution)/shard_map/ppermute | solution.py:173
  25.1 47.7 %copy-start.16 = (bf16[1,512,128]{2,1,0:T(8,128)(2,1)}, bf16[1,512,128]{2,1,0:T(8,128)(2,1)S(1)}, u32[]{:S(2)}) copy-start(bf16[1,512,128]{2,1,0:T(8,128)(2,1)S(1)} %collective-permute-done.1.refs_2_) | copy-start | bytes 393220
  25.1 23.6 %collective-permute-start.7 = (bf16[1,512,128]{2,1,0:T(8,128)(2,1)}, bf16[1,512,128]{2,1,0:T(8,128)(2,1)S(1)}, u32[]{:S(2)}, u32[]{:S(2)}) collective-permute-start(bf16[1,512,128]{2,1,0:T(8,128)(2,1)} %get-tuple-element.32), channel_id=1, source_target_pairs={{0,8},{1,9},{2,10},{3,11},{4,12},{5,13},{6,14},{7,15},{8,0},{9,1},... | collective-permute-start | bytes 393224 | tf_op jit(solution)/shard_map/ppermute | solution.py:173
  30.8 42.0 %copy-start.8 = (bf16[1,512,128]{2,1,0:T(8,128)(2,1)}, bf16[1,512,128]{2,1,0:T(8,128)(2,1)S(1)}, u32[]{:S(2)}) copy-start(bf16[1,512,128]{2,1,0:T(8,128)(2,1)S(1)} %collective-permute-done.3.refs_4_) | copy-start | bytes 393220
  30.8 19.1 %collective-permute-start.8 = (bf16[1,512,128]{2,1,0:T(8,128)(2,1)}, bf16[1,512,128]{2,1,0:T(8,128)(2,1)S(1)}, u32[]{:S(2)}, u32[]{:S(2)}) collective-permute-start(bf16[1,512,128]{2,1,0:T(8,128)(2,1)} %get-tuple-element.33), channel_id=1, source_target_pairs={{0,9},{1,8},{2,11},{3,10},{4,13},{5,12},{6,15},{7,14},{8,1},{9,0},... | collective-permute-start | bytes 393224 | tf_op jit(solution)/shard_map/ppermute | solution.py:173
  34.1 38.7 %copy-start.9 = (bf16[1,512,128]{2,1,0:T(8,128)(2,1)}, bf16[1,512,128]{2,1,0:T(8,128)(2,1)S(1)}, u32[]{:S(2)}) copy-start(bf16[1,512,128]{2,1,0:T(8,128)(2,1)S(1)} %collective-permute-done.4.refs_5_) | copy-start | bytes 393220
  34.1 28.8 %collective-permute-start.9 = (bf16[1,512,128]{2,1,0:T(8,128)(2,1)}, bf16[1,512,128]{2,1,0:T(8,128)(2,1)S(1)}, u32[]{:S(2)}, u32[]{:S(2)}) collective-permute-start(bf16[1,512,128]{2,1,0:T(8,128)(2,1)} %get-tuple-element.34), channel_id=1, source_target_pairs={{0,10},{1,11},{2,8},{3,9},{4,14},{5,15},{6,12},{7,13},{8,2},{9,3},... | collective-permute-start | bytes 393224 | tf_op jit(solution)/shard_map/ppermute | solution.py:173
  46.0 26.8 %copy-start.10 = (bf16[1,512,128]{2,1,0:T(8,128)(2,1)}, bf16[1,512,128]{2,1,0:T(8,128)(2,1)S(1)}, u32[]{:S(2)}) copy-start(bf16[1,512,128]{2,1,0:T(8,128)(2,1)S(1)} %collective-permute-done.5.refs_6_) | copy-start | bytes 393220
  46.0 18.6 %collective-permute-start.10 = (bf16[1,512,128]{2,1,0:T(8,128)(2,1)}, bf16[1,512,128]{2,1,0:T(8,128)(2,1)S(1)}, u32[]{:S(2)}, u32[]{:S(2)}) collective-permute-start(bf16[1,512,128]{2,1,0:T(8,128)(2,1)} %get-tuple-element.35), channel_id=1, source_target_pairs={{0,11},{1,10},{2,9},{3,8},{4,15},{5,14},{6,13},{7,12},{8,3},{9,2},... | collective-permute-start | bytes 393224 | tf_op jit(solution)/shard_map/ppermute | solution.py:173
  47.9 24.9 %copy-start.7 = (bf16[1,512,128]{2,1,0:T(8,128)(2,1)}, bf16[1,512,128]{2,1,0:T(8,128)(2,1)S(1)}, u32[]{:S(2)}) copy-start(bf16[1,512,128]{2,1,0:T(8,128)(2,1)S(1)} %collective-permute-done.6.refs_0_.refs_1_.refs_2_.refs_3_.refs_7_.refs_12_.refs_13_.refs_14_.refs_15_) | copy-start | bytes 393220
  47.9 27.8 %collective-permute-start.2 = (bf16[1,512,128]{2,1,0:T(8,128)(2,1)}, bf16[1,512,128]{2,1,0:T(8,128)(2,1)S(1)}, u32[]{:S(2)}, u32[]{:S(2)}) collective-permute-start(bf16[1,512,128]{2,1,0:T(8,128)(2,1)} %get-tuple-element.27), channel_id=1, source_target_pairs={{0,3},{1,2},{2,1},{3,0},{4,7},{5,6},{6,5},{7,4},{8,11},{9,10},{10,... | collective-permute-start | bytes 393224 | tf_op jit(solution)/shard_map/ppermute | solution.py:173
  48.6 24.2 %copy-start.11 = (bf16[1,512,128]{2,1,0:T(8,128)(2,1)}, bf16[1,512,128]{2,1,0:T(8,128)(2,1)S(1)}, u32[]{:S(2)}) copy-start(bf16[1,512,128]{2,1,0:T(8,128)(2,1)S(1)} %collective-permute-done.7.refs_8_) | copy-start | bytes 393220
  48.6 27.1 %collective-permute-start.11 = (bf16[1,512,128]{2,1,0:T(8,128)(2,1)}, bf16[1,512,128]{2,1,0:T(8,128)(2,1)S(1)}, u32[]{:S(2)}, u32[]{:S(2)}) collective-permute-start(bf16[1,512,128]{2,1,0:T(8,128)(2,1)} %get-tuple-element.36), channel_id=1, source_target_pairs={{0,12},{1,13},{2,14},{3,15},{4,8},{5,9},{6,10},{7,11},{8,4},{9,5},... | collective-permute-start | bytes 393224 | tf_op jit(solution)/shard_map/ppermute | solution.py:173
  49.9 22.9 %copy-start.12 = (bf16[1,512,128]{2,1,0:T(8,128)(2,1)}, bf16[1,512,128]{2,1,0:T(8,128)(2,1)S(1)}, u32[]{:S(2)}) copy-start(bf16[1,512,128]{2,1,0:T(8,128)(2,1)S(1)} %collective-permute-done.8.refs_9_) | copy-start | bytes 393220
  49.9 25.8 %collective-permute-start.12 = (bf16[1,512,128]{2,1,0:T(8,128)(2,1)}, bf16[1,512,128]{2,1,0:T(8,128)(2,1)S(1)}, u32[]{:S(2)}, u32[]{:S(2)}) collective-permute-start(bf16[1,512,128]{2,1,0:T(8,128)(2,1)} %get-tuple-element.37), channel_id=1, source_target_pairs={{0,13},{1,12},{2,15},{3,14},{4,9},{5,8},{6,11},{7,10},{8,5},{9,4},... | collective-permute-start | bytes 393224 | tf_op jit(solution)/shard_map/ppermute | solution.py:173
  62.8 10.0 %copy-start.13 = (bf16[1,512,128]{2,1,0:T(8,128)(2,1)}, bf16[1,512,128]{2,1,0:T(8,128)(2,1)S(1)}, u32[]{:S(2)}) copy-start(bf16[1,512,128]{2,1,0:T(8,128)(2,1)S(1)} %collective-permute-done.9.refs_10_) | copy-start | bytes 393220
  62.8 12.9 %collective-permute-start.13 = (bf16[1,512,128]{2,1,0:T(8,128)(2,1)}, bf16[1,512,128]{2,1,0:T(8,128)(2,1)S(1)}, u32[]{:S(2)}, u32[]{:S(2)}) collective-permute-start(bf16[1,512,128]{2,1,0:T(8,128)(2,1)} %get-tuple-element.38), channel_id=1, source_target_pairs={{0,14},{1,15},{2,12},{3,13},{4,10},{5,11},{6,8},{7,9},{8,6},{9,7},... | collective-permute-start | bytes 393224 | tf_op jit(solution)/shard_map/ppermute | solution.py:173
  64.7 11.1 %collective-permute-start.14 = (bf16[1,512,128]{2,1,0:T(8,128)(2,1)}, bf16[1,512,128]{2,1,0:T(8,128)(2,1)S(1)}, u32[]{:S(2)}, u32[]{:S(2)}) collective-permute-start(bf16[1,512,128]{2,1,0:T(8,128)(2,1)} %get-tuple-element.39), channel_id=1, source_target_pairs={{0,15},{1,14},{2,13},{3,12},{4,11},{5,10},{6,9},{7,8},{8,7},{9,6},... | collective-permute-start | bytes 393224 | tf_op jit(solution)/shard_map/ppermute | solution.py:173
  76.5 38.8 %copy-start.3 = (bf16[256,2048]{1,0:T(8,128)(2,1)S(1)}, bf16[256,2048]{1,0:T(8,128)(2,1)}, u32[]{:S(2)}) copy-start(bf16[256,2048]{1,0:T(8,128)(2,1)} %out_gate_ref.1) | copy-start | bytes 3145732
  76.5 38.8 %copy-start.6 = (f32[2048]{0:T(1024)S(1)}, f32[2048]{0:T(1024)}, u32[]{:S(2)}) copy-start(f32[2048]{0:T(1024)} %param.13) | copy-start | bytes 24580
  81.3 34.1 %copy-start = (bf16[256,2048]{1,0:T(8,128)(2,1)S(1)}, bf16[256,2048]{1,0:T(8,128)(2,1)}, u32[]{:S(2)}) copy-start(bf16[256,2048]{1,0:T(8,128)(2,1)} %signal_ref.3) | copy-start | bytes 3145732
  81.3 34.1 %copy-start.1 = (bf16[256,2048]{1,0:T(8,128)(2,1)S(1)}, bf16[256,2048]{1,0:T(8,128)(2,1)}, u32[]{:S(2)}) copy-start(bf16[256,2048]{1,0:T(8,128)(2,1)} %gate_ref.3) | copy-start | bytes 3145732
  (6 other events, 11.7 us)

commit v7 on v6

--- a/solution.py
+++ b/solution.py
@@ -16,8 +16,6 @@
 HALF = LANES // 2
 PAD = 8
 PIECES = 4
-JOINED = ()
-EARLY = (7, 6, 5, 4)
 BF16 = jnp.bfloat16
 F32 = jnp.float32
 
@@ -124,13 +122,12 @@
             for half in range(2):
                 near = (2 * block + half) ^ (seq % chunks)
                 chunks_ref[near, rows, :] = halves[half].astype(BF16)
-    views = [ref.at[at] for ref in out_refs for at in range(ref.shape[0])]
-    for step in range(len(views) // chunks):
+    for step in range(len(out_refs) // chunks):
 
         @pl.when(pl.program_id(0) == step)
         def _():
             for near in range(chunks):
-                views[chunks * step + near][...] = chunks_ref[near]
+                out_refs[chunks * step + near][...] = chunks_ref[near]
 
 
 def pack_filter(filter_spectrum, devices_seq):
@@ -140,21 +137,18 @@
     steps = devices_seq // chunks
     size = low * width * channels // 2
     block = (low * width, LANES)
-    shapes = [
-        (1 + (d in JOINED), *block) for d in range(devices_seq) if d - 1 not in JOINED
-    ]
 
     def lanes_of(step, place):
         return (0, 0, 0, place[0] * steps + ((place[1] // chunks) ^ step))
 
     return pl.pallas_call(
         functools.partial(pack_filter_kernel, middle=low * devices_seq // 2),
-        out_shape=[pltpu.HBM(shape, BF16) for shape in shapes],
+        out_shape=[pltpu.HBM(block, BF16)] * devices_seq,
         grid_spec=pltpu.PrefetchScalarGridSpec(
             num_scalar_prefetch=1,
             grid=(steps,),
             in_specs=[pl.BlockSpec((2, low, width, wide), lanes_of)],
-            out_specs=[pl.BlockSpec(shape, lambda step, place: (0, 0, 0)) for shape in shapes],
+            out_specs=[pl.BlockSpec(block, lambda step, place: (0, 0))] * devices_seq,
             scratch_shapes=[pltpu.VMEM((chunks, *block), BF16)],
         ),
         compiler_params=pltpu.CompilerParams(vmem_limit_bytes=16 << 20),
@@ -166,6 +160,10 @@
         jnp.stack([lax.axis_index("groups"), lax.axis_index("seq")]),
         pltpu.with_memory_space_constraint(filter_spectrum, pltpu.HBM),
     )
+
+
+def early_distances(devices_seq):
+    return list(reversed(range(devices_seq // 4, devices_seq // 2)))
 
 
 def swap_with(values, distance):
@@ -271,7 +269,9 @@
 
 
 def inverse_kernel(place_ref, spec_ref, turn_ref, matrices_hbm, *refs, devices_seq, early):
-    distances = EARLY if early else [d for d in range(devices_seq // 2) if d not in EARLY]
+    distances = first = early_distances(devices_seq)
+    if not early:
+        distances = [d for d in range(devices_seq // 2) if d not in first]
     filter_hbm, refs = refs[:devices_seq], refs[devices_seq:]
     if early:
         real_ref, imag_ref, filter_ref, matrices_ref, matrices_sem, filter_sems = refs
@@ -295,7 +295,7 @@
     def arrival(distance, count=None):
         rows = pl.ds(0, count or filter_ref.shape[1])
         return pltpu.make_async_copy(
-            filter_hbm[distance].at[int(distance - 1 in JOINED), rows],
+            filter_hbm[distance].at[rows],
             filter_ref.at[distance, rows],
             filter_sems.at[distance],
         )
@@ -309,7 +309,7 @@
         for near in pair_of(distance):
             arrival(near).start()
     if not early:
-        for distance in EARLY:
+        for distance in first:
             for near in pair_of(distance):
                 arrival(near, width).start()
     matrices.wait()
@@ -373,7 +373,7 @@
                 keep(slot[0], values)
     if early:
         return
-    for distance in EARLY:
+    for distance in first:
         for near in pair_of(distance):
             arrival(near, width).wait()
     for distance in range(devices_seq):
@@ -425,7 +425,7 @@
     half_rows = spectrum.shape[0] - 1
     _, _, matrices, turn = tables(half_rows, width)
     stage = pltpu.VMEM((half_rows * (width + PAD), LANES), F32)
-    block = arrived[0].shape[1:]
+    block = arrived[0].shape
 
     def in_hbm(operand):
         return pltpu.with_memory_space_constraint(jnp.asarray(operand), pltpu.HBM)
@@ -445,7 +445,7 @@
     ]
 
     def call(early, more_in, out_shape, more_scratch, aliases):
-        used = [d for e in EARLY for d in (e, devices_seq - 1 - e)]
+        used = [d for e in early_distances(devices_seq) for d in (e, devices_seq - 1 - e)]
         rows = [
             in_hbm(arrived[d] if d in used or not early else arrived[used[0]])
             for d in range(devices_seq)
@@ -532,13 +532,7 @@
 
     got = pairs(pack_input(signal, input_gate, devices_seq))
     packed = pack_filter(filter_spectrum, devices_seq)
-    packed = iter(packed)
-    arrived = [next(packed)]
-    for distance in range(1, devices_seq):
-        if distance - 1 in JOINED:
-            arrived.append(swap_with(arrived[-1], 1))
-        else:
-            arrived.append(swap_with(next(packed), distance))
+    arrived = [packed[0]] + [swap_with(packed[d], d) for d in range(1, devices_seq)]
     spectrum = forward(got, devices_seq, width)
     conv = inverse(spectrum, arrived, devices_seq, signal.shape[0] // 2)
     return mix(pairs(conv), signal, input_gate, output_gate, skip_gain)

time: 117 us -> 117 us (level)
  no operation moved by 1% of the time
where the time goes in v7:
time: 117 us
  blocking collectives  34 us (29%)
  starting transfers between devices  29.1 us (25%)
  waiting for transfers between devices  28.5 us (24%)
  Pallas kernels  24.3 us (21%)
    all_to_all x1, blocking collectives, exchange(): return lax.all_to_all(values, axes, split_axis=0, concat_axis=0, tiled=True)  34 us
    ppermute x15, waiting for transfers between devices, swap_with(): lax.ppermute(values, 'seq', [(i, i ^ distance) for i in range(count)])  28.5 us
    ppermute x15, starting transfers between devices, swap_with(): lax.ppermute(values, 'seq', [(i, i ^ distance) for i in range(count)])  21.8 us
    pallas_call x2, Pallas kernels, call(): pl.pallas_call(functools.partial(inverse_kernel, devices_seq=devices_seq,...  7.55 us
    all_to_all x1, starting transfers between devices, exchange(): return lax.all_to_all(values, axes, split_axis=0, concat_axis=0, tiled=True)  7.3 us
    pallas_call x1, Pallas kernels, forward(): pl.pallas_call(functools.partial(forward_kernel, devices_seq=devices_seq)...  6.69 us
    pallas_call x1, Pallas kernels, pack_filter(): pl.pallas_call(functools.partial(pack_filter_kernel, middle=low * devices...  5.76 us
    pallas_call x1, Pallas kernels, pack_input(): pl.pallas_call(pack_input_kernel, out_shape=jax.ShapeDtypeStruct((devices...  2.58 us
  transfers between devices with their start and end apart: 16, of which 6 were waited for; matrix products, arithmetic and copies ran while one was open for 0% of the time, Pallas kernels for 13%

profile of v7, /device:TPU:0, one launch (start us, length us, event | category | flops | bytes accessed | tf_op | source)
XLA Modules:
  0.0 117.1 jit_solution(7419971343608585089)
XLA Ops:
  0.0 2.6 %pack_input.1 = bf16[16,2,128,128]{3,2,1,0:T(8,128)(2,1)} custom-call(bf16[256,2048]{1,0:T(8,128)(2,1)} %signal_ref.3, bf16[256,2048]{1,0:T(8,128)(2,1)} %gate_ref.3), custom_call_target="tpu_custom_call" | custom-call | flops 524288 | bytes 3145728 | tf_op jit(solution)/shard_map/pack_input/pallas_call | solution.py:90
  2.6 7.3 %all-to-all-start = ((bf16[32,128,128]{2,1,0:T(8,128)(2,1)}), bf16[32,128,128]{2,1,0:T(8,128)(2,1)S(1)}, u32[]{:S(2)}, u32[]{:S(2)}) async-start(bf16[32,128,128]{2,1,0:T(8,128)(2,1)} %bitcast.11), calls=%async_computation | async-start | bytes 2097152 | tf_op jit(solution)/shard_map/all_to_all | solution.py:24
  9.9 0.1 pad_add_fusion.place_ref
  10.0 5.8 %pack_filter.1 = (bf16[512,128]{1,0:T(8,128)(2,1)}, bf16[512,128]{1,0:T(8,128)(2,1)}, bf16[512,128]{1,0:T(8,128)(2,1)}, bf16[512,128]{1,0:T(8,128)(2,1)}, bf16[5...) custom-call(s32[2]{0:T(128)S(1)} %pad_add_fusion.place_ref, ...), custom_call_target="tpu_custom_call" | custom-call | flops 134217728 | bytes 6291456 | tf_op jit(solution)/shard_map/pack_filter/pallas_call | solution.py:144
  15.7 0.3 collective-permute-start
  16.0 1.7 %collective-permute-start.1 = (bf16[512,128]{1,0:T(8,128)(2,1)}, bf16[512,128]{1,0:T(8,128)(2,1)S(1)}, u32[]{:S(2)}, u32[]{:S(2)}) collective-permute-start(bf16[512,128]{1,0:T(8,128)(2,1)} %get-tuple-element.26), channel_id=1, source_target_pairs={{0,2},{1,3},{2,0},{3,1},{4,6},{5,7},{6,4},{7,5},{8,10},{9,11},{10,... | collective-permute-start | bytes 393224 | tf_op jit(solution)/shard_map/ppermute | solution.py:171
  17.7 1.5 %collective-permute-start.3 = (bf16[512,128]{1,0:T(8,128)(2,1)}, bf16[512,128]{1,0:T(8,128)(2,1)S(1)}, u32[]{:S(2)}, u32[]{:S(2)}) collective-permute-start(bf16[512,128]{1,0:T(8,128)(2,1)} %get-tuple-element.28), channel_id=1, source_target_pairs={{0,4},{1,5},{2,6},{3,7},{4,0},{5,1},{6,2},{7,3},{8,12},{9,13},{10,... | collective-permute-start | bytes 393224 | tf_op jit(solution)/shard_map/ppermute | solution.py:171
  19.1 1.4 %collective-permute-start.5 = (bf16[512,128]{1,0:T(8,128)(2,1)}, bf16[512,128]{1,0:T(8,128)(2,1)S(1)}, u32[]{:S(2)}, u32[]{:S(2)}) collective-permute-start(bf16[512,128]{1,0:T(8,128)(2,1)} %get-tuple-element.30), channel_id=1, source_target_pairs={{0,6},{1,7},{2,4},{3,5},{4,2},{5,3},{6,0},{7,1},{8,14},{9,15},{10,... | collective-permute-start | bytes 393224 | tf_op jit(solution)/shard_map/ppermute | solution.py:171
  20.6 1.5 %collective-permute-start.6 = (bf16[512,128]{1,0:T(8,128)(2,1)}, bf16[512,128]{1,0:T(8,128)(2,1)S(1)}, u32[]{:S(2)}, u32[]{:S(2)}) collective-permute-start(bf16[512,128]{1,0:T(8,128)(2,1)} %get-tuple-element.31), channel_id=1, source_target_pairs={{0,7},{1,6},{2,5},{3,4},{4,3},{5,2},{6,1},{7,0},{8,15},{9,14},{10,... | collective-permute-start | bytes 393224 | tf_op jit(solution)/shard_map/ppermute | solution.py:171
  22.1 3.0 %collective-permute-done.1.refs_2_ = bf16[512,128]{1,0:T(8,128)(2,1)S(1)} collective-permute-done((bf16[512,128]{1,0:T(8,128)(2,1)}, bf16[512,128]{1,0:T(8,128)(2,1)S(1)}, u32[]{:S(2)}, u32[]{:S(2)}) %collective-permute-start.1) | collective-permute-done | bytes 131104 | tf_op jit(solution)/shard_map/ppermute | solution.py:171
  25.1 2.4 %collective-permute-start.7 = (bf16[512,128]{1,0:T(8,128)(2,1)}, bf16[512,128]{1,0:T(8,128)(2,1)S(1)}, u32[]{:S(2)}, u32[]{:S(2)}) collective-permute-start(bf16[512,128]{1,0:T(8,128)(2,1)} %get-tuple-element.32), channel_id=1, source_target_pairs={{0,8},{1,9},{2,10},{3,11},{4,12},{5,13},{6,14},{7,15},{8,0},{9,1},... | collective-permute-start | bytes 393224 | tf_op jit(solution)/shard_map/ppermute | solution.py:171
  27.4 3.4 %collective-permute-done.3.refs_4_ = bf16[512,128]{1,0:T(8,128)(2,1)S(1)} collective-permute-done((bf16[512,128]{1,0:T(8,128)(2,1)}, bf16[512,128]{1,0:T(8,128)(2,1)S(1)}, u32[]{:S(2)}, u32[]{:S(2)}) %collective-permute-start.3) | collective-permute-done | bytes 131104 | tf_op jit(solution)/shard_map/ppermute | solution.py:171
  30.8 3.3 %collective-permute-start.8 = (bf16[512,128]{1,0:T(8,128)(2,1)}, bf16[512,128]{1,0:T(8,128)(2,1)S(1)}, u32[]{:S(2)}, u32[]{:S(2)}) collective-permute-start(bf16[512,128]{1,0:T(8,128)(2,1)} %get-tuple-element.33), channel_id=1, source_target_pairs={{0,9},{1,8},{2,11},{3,10},{4,13},{5,12},{6,15},{7,14},{8,1},{9,0},... | collective-permute-start | bytes 393224 | tf_op jit(solution)/shard_map/ppermute | solution.py:171
  34.1 4.0 %collective-permute-start.9 = (bf16[512,128]{1,0:T(8,128)(2,1)}, bf16[512,128]{1,0:T(8,128)(2,1)S(1)}, u32[]{:S(2)}, u32[]{:S(2)}) collective-permute-start(bf16[512,128]{1,0:T(8,128)(2,1)} %get-tuple-element.34), channel_id=1, source_target_pairs={{0,10},{1,11},{2,8},{3,9},{4,14},{5,15},{6,12},{7,13},{8,2},{9,3},... | collective-permute-start | bytes 393224 | tf_op jit(solution)/shard_map/ppermute | solution.py:171
  38.1 7.9 %collective-permute-done.5.refs_6_ = bf16[512,128]{1,0:T(8,128)(2,1)S(1)} collective-permute-done((bf16[512,128]{1,0:T(8,128)(2,1)}, bf16[512,128]{1,0:T(8,128)(2,1)S(1)}, u32[]{:S(2)}, u32[]{:S(2)}) %collective-permute-start.5) | collective-permute-done | bytes 131104 | tf_op jit(solution)/shard_map/ppermute | solution.py:171
  46.0 1.9 %collective-permute-done.6.refs_0_.refs_1_.refs_2_.refs_3_.refs_7_.refs_12_.refs_13_.refs_14_.refs_15_ = bf16[512,128]{1,0:T(8,128)(2,1)S(1)} collective-permute-done((bf16[512,128]{1,0:T(8,128)(2,1)}, bf16[512,128]{1,0:T(8,128)(2,1)S(1)}, u32[]{:S(2)}, u32[]{:S(2)}) %collective-permute-start.6) | collective-permute-done | bytes 131104 | tf_op jit(solution)/shard_map/ppermute | solution.py:171
  47.9 0.7 collective-permute-start.2
  48.6 1.3 %collective-permute-start.11 = (bf16[512,128]{1,0:T(8,128)(2,1)}, bf16[512,128]{1,0:T(8,128)(2,1)S(1)}, u32[]{:S(2)}, u32[]{:S(2)}) collective-permute-start(bf16[512,128]{1,0:T(8,128)(2,1)} %get-tuple-element.36), channel_id=1, source_target_pairs={{0,12},{1,13},{2,14},{3,15},{4,8},{5,9},{6,10},{7,11},{8,4},{9,5},... | collective-permute-start | bytes 393224 | tf_op jit(solution)/shard_map/ppermute | solution.py:171
  49.9 1.8 %collective-permute-start.12 = (bf16[512,128]{1,0:T(8,128)(2,1)}, bf16[512,128]{1,0:T(8,128)(2,1)S(1)}, u32[]{:S(2)}, u32[]{:S(2)}) collective-permute-start(bf16[512,128]{1,0:T(8,128)(2,1)} %get-tuple-element.37), channel_id=1, source_target_pairs={{0,13},{1,12},{2,15},{3,14},{4,9},{5,8},{6,11},{7,10},{8,5},{9,4},... | collective-permute-start | bytes 393224 | tf_op jit(solution)/shard_map/ppermute | solution.py:171
  51.7 11.1 %collective-permute-done.9.refs_10_ = bf16[512,128]{1,0:T(8,128)(2,1)S(1)} collective-permute-done((bf16[512,128]{1,0:T(8,128)(2,1)}, bf16[512,128]{1,0:T(8,128)(2,1)S(1)}, u32[]{:S(2)}, u32[]{:S(2)}) %collective-permute-start.9) | collective-permute-done | bytes 131104 | tf_op jit(solution)/shard_map/ppermute | solution.py:171
  62.8 0.6 collective-permute-start.13
  63.5 1.2 %collective-permute-done.10.refs_11_ = bf16[512,128]{1,0:T(8,128)(2,1)S(1)} collective-permute-done((bf16[512,128]{1,0:T(8,128)(2,1)}, bf16[512,128]{1,0:T(8,128)(2,1)S(1)}, u32[]{:S(2)}, u32[]{:S(2)}) %collective-permute-start.10) | collective-permute-done | bytes 131104 | tf_op jit(solution)/shard_map/ppermute | solution.py:171
  64.7 1.4 %collective-permute-start.14 = (bf16[512,128]{1,0:T(8,128)(2,1)}, bf16[512,128]{1,0:T(8,128)(2,1)S(1)}, u32[]{:S(2)}, u32[]{:S(2)}) collective-permute-start(bf16[512,128]{1,0:T(8,128)(2,1)} %get-tuple-element.39), channel_id=1, source_target_pairs={{0,15},{1,14},{2,13},{3,12},{4,11},{5,10},{6,9},{7,8},{8,7},{9,6},... | collective-permute-start | bytes 393224 | tf_op jit(solution)/shard_map/ppermute | solution.py:171
  66.1 6.7 %forward.1.spec_ref = f32[65,128,128]{2,1,0:T(8,128)S(1)} custom-call(bf16[16,2,128,128]{3,2,1,0:T(8,128)(2,1)S(1)} %bitcast.8, bf16[128,128]{1,0:T(8,128)(2,1)S(1)} %copy-done.5, bf16[128,384]{1,0:T(8,128)(2,1)S(1)} %copy-done.4, f32[9,64,128]{2,1,0:T(8,128)S(1)} %copy-done.2), custom_call_target="tpu_custom_call" | custom-call | flops 1073741824 | bytes 5242880 | tf_op jit(solution)/shard_map/forward/pallas_call | solution.py:254
  72.9 2.8 %inverse_early.1 = (f32[4608,128]{1,0:T(8,128)S(1)}, f32[4608,128]{1,0:T(8,128)S(1)}) custom-call(s32[1]{0:T(128)} %bitcast.place_ref, f32[65,128,128]{2,1,0:T(8,128)S(1)} %forward.1.spec_ref, f32[9,64,128]{2,1,0:T(8,128)S(1)} %copy-done.2, bf16[192,256]{1,0:T(8,128)(2,1)} %constant.20.clone.matrices_hbm, bf16[512,128]{1,0:T(8,128)(2,1)} %copy-done.7, ...), custom_call_target="tpu_custom_call" | custom-call | flops 402653184 | bytes 2097152 | tf_op jit(solution)/shard_map/inverse_early/pallas_call | solution.py:455
  75.8 0.6 copy-done.17
  76.4 0.0 copy-done.18
  76.5 0.1 copy-done.20
  76.5 0.0 copy-done.21
  76.5 4.7 %inverse_late.1 = (bf16[16,2,128,128]{3,2,1,0:T(8,128)(2,1)S(1)}, f32[4608,128]{1,0:T(8,128)S(1)}, f32[4608,128]{1,0:T(8,128)S(1)}) custom-call(s32[1]{0:T(128)} %bitcast.place_ref, f32[65,128,128]{2,1,0:T(8,128)S(1)} %forward.1.spec_ref, f32[9,64,128]{2,1,0:T(8,128)S(1)} %copy-done.2, ...), custom_call_target="tpu_custom_call", output_to_operand_aliasing={{1}: (20, {}), {2}: (21, {})} | custom-call | flops 402653184 | bytes 2097152 | tf_op jit(solution)/shard_map/inverse_late/pallas_call | solution.py:455
  81.3 34.0 %all_to_all.10 = bf16[32,128,128]{2,1,0:T(8,128)(2,1)S(1)} all-to-all(bf16[32,128,128]{2,1,0:T(8,128)(2,1)S(1)} %bitcast.9), channel_id=1, replica_groups=mesh['groups'=2,'seq'=16] {'seq','groups'}, dimensions={0} | all-to-all | bytes 2097152 | tf_op jit(solution)/shard_map/all_to_all | solution.py:24
  115.4 1.7 %mix.1 = bf16[256,2048]{1,0:T(8,128)(2,1)} custom-call(bf16[16,2,128,128]{3,2,1,0:T(8,128)(2,1)S(1)} %bitcast.7, bf16[256,2048]{1,0:T(8,128)(2,1)S(1)} %copy-done, bf16[256,2048]{1,0:T(8,128)(2,1)S(1)} %copy-done.1, bf16[256,2048]{1,0:T(8,128)(2,1)S(1)} %copy-done.3, f32[1,2048]{1,0:T(1,128)S(1)} %bitcast.10), custom_call_target="tpu_custom_call" | custom-call | flops 2097152 | bytes 5242880 | tf_op jit(solution)/shard_map/mix/pallas_call | solution.py:512
  (52 shorter events, 0.1 us)
Async XLA Ops:
  2.6 63.5 %all-to-all-start = ((bf16[32,128,128]{2,1,0:T(8,128)(2,1)}), bf16[32,128,128]{2,1,0:T(8,128)(2,1)S(1)}, u32[]{:S(2)}, u32[]{:S(2)}) async-start(bf16[32,128,128]{2,1,0:T(8,128)(2,1)} %bitcast.11), calls=%async_computation | async-start | bytes 2097152 | tf_op jit(solution)/shard_map/all_to_all | solution.py:24
  10.0 56.1 %copy-start.2 = (f32[9,64,128]{2,1,0:T(8,128)S(1)}, f32[9,64,128]{2,1,0:T(8,128)}, u32[]{:S(2)}) copy-start(f32[9,64,128]{2,1,0:T(8,128)} %constant.19.clone.turn_ref) | copy-start | bytes 884740
  10.0 56.1 %copy-start.4 = (bf16[128,384]{1,0:T(8,128)(2,1)S(1)}, bf16[128,384]{1,0:T(8,128)(2,1)}, u32[]{:S(2)}) copy-start(bf16[128,384]{1,0:T(8,128)(2,1)} %constant.18.clone.second_ref) | copy-start | bytes 294916
  10.0 56.1 %copy-start.5 = (bf16[128,128]{1,0:T(8,128)(2,1)S(1)}, bf16[128,128]{1,0:T(8,128)(2,1)}, u32[]{:S(2)}) copy-start(bf16[128,128]{1,0:T(8,128)(2,1)} %constant.17.clone.first_ref) | copy-start | bytes 98308
  15.7 4.8 %collective-permute-start = (bf16[512,128]{1,0:T(8,128)(2,1)}, bf16[512,128]{1,0:T(8,128)(2,1)S(1)}, u32[]{:S(2)}, u32[]{:S(2)}) collective-permute-start(bf16[512,128]{1,0:T(8,128)(2,1)} %get-tuple-element.25), channel_id=1, source_target_pairs={{0,1},{1,0},{2,3},{3,2},{4,5},{5,4},{6,7},{7,6},{8,9},{9,8},{10,11... | collective-permute-start | bytes 393224 | tf_op jit(solution)/shard_map/ppermute | solution.py:171
  16.0 9.1 %collective-permute-start.1 = (bf16[512,128]{1,0:T(8,128)(2,1)}, bf16[512,128]{1,0:T(8,128)(2,1)S(1)}, u32[]{:S(2)}, u32[]{:S(2)}) collective-permute-start(bf16[512,128]{1,0:T(8,128)(2,1)} %get-tuple-element.26), channel_id=1, source_target_pairs={{0,2},{1,3},{2,0},{3,1},{4,6},{5,7},{6,4},{7,5},{8,10},{9,11},{10,... | collective-permute-start | bytes 393224 | tf_op jit(solution)/shard_map/ppermute | solution.py:171
  17.7 13.1 %collective-permute-start.3 = (bf16[512,128]{1,0:T(8,128)(2,1)}, bf16[512,128]{1,0:T(8,128)(2,1)S(1)}, u32[]{:S(2)}, u32[]{:S(2)}) collective-permute-start(bf16[512,128]{1,0:T(8,128)(2,1)} %get-tuple-element.28), channel_id=1, source_target_pairs={{0,4},{1,5},{2,6},{3,7},{4,0},{5,1},{6,2},{7,3},{8,12},{9,13},{10,... | collective-permute-start | bytes 393224 | tf_op jit(solution)/shard_map/ppermute | solution.py:171
  19.1 14.9 %collective-permute-start.4 = (bf16[512,128]{1,0:T(8,128)(2,1)}, bf16[512,128]{1,0:T(8,128)(2,1)S(1)}, u32[]{:S(2)}, u32[]{:S(2)}) collective-permute-start(bf16[512,128]{1,0:T(8,128)(2,1)} %get-tuple-element.29), channel_id=1, source_target_pairs={{0,5},{1,4},{2,7},{3,6},{4,1},{5,0},{6,3},{7,2},{8,13},{9,12},{10,... | collective-permute-start | bytes 393224 | tf_op jit(solution)/shard_map/ppermute | solution.py:171
  19.1 26.9 %collective-permute-start.5 = (bf16[512,128]{1,0:T(8,128)(2,1)}, bf16[512,128]{1,0:T(8,128)(2,1)S(1)}, u32[]{:S(2)}, u32[]{:S(2)}) collective-permute-start(bf16[512,128]{1,0:T(8,128)(2,1)} %get-tuple-element.30), channel_id=1, source_target_pairs={{0,6},{1,7},{2,4},{3,5},{4,2},{5,3},{6,0},{7,1},{8,14},{9,15},{10,... | collective-permute-start | bytes 393224 | tf_op jit(solution)/shard_map/ppermute | solution.py:171
  20.6 52.2 %copy-start.15 = (bf16[512,128]{1,0:T(8,128)(2,1)}, bf16[512,128]{1,0:T(8,128)(2,1)S(1)}, u32[]{:S(2)}) copy-start(bf16[512,128]{1,0:T(8,128)(2,1)S(1)} %collective-permute-done.refs_1_) | copy-start | bytes 393220
  20.6 27.3 %collective-permute-start.6 = (bf16[512,128]{1,0:T(8,128)(2,1)}, bf16[512,128]{1,0:T(8,128)(2,1)S(1)}, u32[]{:S(2)}, u32[]{:S(2)}) collective-permute-start(bf16[512,128]{1,0:T(8,128)(2,1)} %get-tuple-element.31), channel_id=1, source_target_pairs={{0,7},{1,6},{2,5},{3,4},{4,3},{5,2},{6,1},{7,0},{8,15},{9,14},{10,... | collective-permute-start | bytes 393224 | tf_op jit(solution)/shard_map/ppermute | solution.py:171
  25.1 47.7 %copy-start.16 = (bf16[512,128]{1,0:T(8,128)(2,1)}, bf16[512,128]{1,0:T(8,128)(2,1)S(1)}, u32[]{:S(2)}) copy-start(bf16[512,128]{1,0:T(8,128)(2,1)S(1)} %collective-permute-done.1.refs_2_) | copy-start | bytes 393220
  25.1 23.6 %collective-permute-start.7 = (bf16[512,128]{1,0:T(8,128)(2,1)}, bf16[512,128]{1,0:T(8,128)(2,1)S(1)}, u32[]{:S(2)}, u32[]{:S(2)}) collective-permute-start(bf16[512,128]{1,0:T(8,128)(2,1)} %get-tuple-element.32), channel_id=1, source_target_pairs={{0,8},{1,9},{2,10},{3,11},{4,12},{5,13},{6,14},{7,15},{8,0},{9,1},... | collective-permute-start | bytes 393224 | tf_op jit(solution)/shard_map/ppermute | solution.py:171
  30.8 42.0 %copy-start.8 = (bf16[512,128]{1,0:T(8,128)(2,1)}, bf16[512,128]{1,0:T(8,128)(2,1)S(1)}, u32[]{:S(2)}) copy-start(bf16[512,128]{1,0:T(8,128)(2,1)S(1)} %collective-permute-done.3.refs_4_) | copy-start | bytes 393220
  30.8 19.1 %collective-permute-start.8 = (bf16[512,128]{1,0:T(8,128)(2,1)}, bf16[512,128]{1,0:T(8,128)(2,1)S(1)}, u32[]{:S(2)}, u32[]{:S(2)}) collective-permute-start(bf16[512,128]{1,0:T(8,128)(2,1)} %get-tuple-element.33), channel_id=1, source_target_pairs={{0,9},{1,8},{2,11},{3,10},{4,13},{5,12},{6,15},{7,14},{8,1},{9,0},... | collective-permute-start | bytes 393224 | tf_op jit(solution)/shard_map/ppermute | solution.py:171
  34.1 38.7 %copy-start.9 = (bf16[512,128]{1,0:T(8,128)(2,1)}, bf16[512,128]{1,0:T(8,128)(2,1)S(1)}, u32[]{:S(2)}) copy-start(bf16[512,128]{1,0:T(8,128)(2,1)S(1)} %collective-permute-done.4.refs_5_) | copy-start | bytes 393220
  34.1 28.8 %collective-permute-start.9 = (bf16[512,128]{1,0:T(8,128)(2,1)}, bf16[512,128]{1,0:T(8,128)(2,1)S(1)}, u32[]{:S(2)}, u32[]{:S(2)}) collective-permute-start(bf16[512,128]{1,0:T(8,128)(2,1)} %get-tuple-element.34), channel_id=1, source_target_pairs={{0,10},{1,11},{2,8},{3,9},{4,14},{5,15},{6,12},{7,13},{8,2},{9,3},... | collective-permute-start | bytes 393224 | tf_op jit(solution)/shard_map/ppermute | solution.py:171
  46.0 26.8 %copy-start.10 = (bf16[512,128]{1,0:T(8,128)(2,1)}, bf16[512,128]{1,0:T(8,128)(2,1)S(1)}, u32[]{:S(2)}) copy-start(bf16[512,128]{1,0:T(8,128)(2,1)S(1)} %collective-permute-done.5.refs_6_) | copy-start | bytes 393220
  46.0 18.6 %collective-permute-start.10 = (bf16[512,128]{1,0:T(8,128)(2,1)}, bf16[512,128]{1,0:T(8,128)(2,1)S(1)}, u32[]{:S(2)}, u32[]{:S(2)}) collective-permute-start(bf16[512,128]{1,0:T(8,128)(2,1)} %get-tuple-element.35), channel_id=1, source_target_pairs={{0,11},{1,10},{2,9},{3,8},{4,15},{5,14},{6,13},{7,12},{8,3},{9,2},... | collective-permute-start | bytes 393224 | tf_op jit(solution)/shard_map/ppermute | solution.py:171
  47.9 24.9 %copy-start.7 = (bf16[512,128]{1,0:T(8,128)(2,1)}, bf16[512,128]{1,0:T(8,128)(2,1)S(1)}, u32[]{:S(2)}) copy-start(bf16[512,128]{1,0:T(8,128)(2,1)S(1)} %collective-permute-done.6.refs_0_.refs_1_.refs_2_.refs_3_.refs_7_.refs_12_.refs_13_.refs_14_.refs_15_) | copy-start | bytes 393220
  47.9 27.8 %collective-permute-start.2 = (bf16[512,128]{1,0:T(8,128)(2,1)}, bf16[512,128]{1,0:T(8,128)(2,1)S(1)}, u32[]{:S(2)}, u32[]{:S(2)}) collective-permute-start(bf16[512,128]{1,0:T(8,128)(2,1)} %get-tuple-element.27), channel_id=1, source_target_pairs={{0,3},{1,2},{2,1},{3,0},{4,7},{5,6},{6,5},{7,4},{8,11},{9,10},{10,... | collective-permute-start | bytes 393224 | tf_op jit(solution)/shard_map/ppermute | solution.py:171
  48.6 24.2 %copy-start.11 = (bf16[512,128]{1,0:T(8,128)(2,1)}, bf16[512,128]{1,0:T(8,128)(2,1)S(1)}, u32[]{:S(2)}) copy-start(bf16[512,128]{1,0:T(8,128)(2,1)S(1)} %collective-permute-done.7.refs_8_) | copy-start | bytes 393220
  48.6 27.1 %collective-permute-start.11 = (bf16[512,128]{1,0:T(8,128)(2,1)}, bf16[512,128]{1,0:T(8,128)(2,1)S(1)}, u32[]{:S(2)}, u32[]{:S(2)}) collective-permute-start(bf16[512,128]{1,0:T(8,128)(2,1)} %get-tuple-element.36), channel_id=1, source_target_pairs={{0,12},{1,13},{2,14},{3,15},{4,8},{5,9},{6,10},{7,11},{8,4},{9,5},... | collective-permute-start | bytes 393224 | tf_op jit(solution)/shard_map/ppermute | solution.py:171
  49.9 22.9 %copy-start.12 = (bf16[512,128]{1,0:T(8,128)(2,1)}, bf16[512,128]{1,0:T(8,128)(2,1)S(1)}, u32[]{:S(2)}) copy-start(bf16[512,128]{1,0:T(8,128)(2,1)S(1)} %collective-permute-done.8.refs_9_) | copy-start | bytes 393220
  49.9 25.8 %collective-permute-start.12 = (bf16[512,128]{1,0:T(8,128)(2,1)}, bf16[512,128]{1,0:T(8,128)(2,1)S(1)}, u32[]{:S(2)}, u32[]{:S(2)}) collective-permute-start(bf16[512,128]{1,0:T(8,128)(2,1)} %get-tuple-element.37), channel_id=1, source_target_pairs={{0,13},{1,12},{2,15},{3,14},{4,9},{5,8},{6,11},{7,10},{8,5},{9,4},... | collective-permute-start | bytes 393224 | tf_op jit(solution)/shard_map/ppermute | solution.py:171
  62.8 10.0 %copy-start.13 = (bf16[512,128]{1,0:T(8,128)(2,1)}, bf16[512,128]{1,0:T(8,128)(2,1)S(1)}, u32[]{:S(2)}) copy-start(bf16[512,128]{1,0:T(8,128)(2,1)S(1)} %collective-permute-done.9.refs_10_) | copy-start | bytes 393220
  62.8 12.9 %collective-permute-start.13 = (bf16[512,128]{1,0:T(8,128)(2,1)}, bf16[512,128]{1,0:T(8,128)(2,1)S(1)}, u32[]{:S(2)}, u32[]{:S(2)}) collective-permute-start(bf16[512,128]{1,0:T(8,128)(2,1)} %get-tuple-element.38), channel_id=1, source_target_pairs={{0,14},{1,15},{2,12},{3,13},{4,10},{5,11},{6,8},{7,9},{8,6},{9,7},... | collective-permute-start | bytes 393224 | tf_op jit(solution)/shard_map/ppermute | solution.py:171
  64.7 11.1 %collective-permute-start.14 = (bf16[512,128]{1,0:T(8,128)(2,1)}, bf16[512,128]{1,0:T(8,128)(2,1)S(1)}, u32[]{:S(2)}, u32[]{:S(2)}) collective-permute-start(bf16[512,128]{1,0:T(8,128)(2,1)} %get-tuple-element.39), channel_id=1, source_target_pairs={{0,15},{1,14},{2,13},{3,12},{4,11},{5,10},{6,9},{7,8},{8,7},{9,6},... | collective-permute-start | bytes 393224 | tf_op jit(solution)/shard_map/ppermute | solution.py:171
  76.5 38.8 %copy-start.3 = (bf16[256,2048]{1,0:T(8,128)(2,1)S(1)}, bf16[256,2048]{1,0:T(8,128)(2,1)}, u32[]{:S(2)}) copy-start(bf16[256,2048]{1,0:T(8,128)(2,1)} %out_gate_ref.1) | copy-start | bytes 3145732
  76.5 38.8 %copy-start.6 = (f32[2048]{0:T(1024)S(1)}, f32[2048]{0:T(1024)}, u32[]{:S(2)}) copy-start(f32[2048]{0:T(1024)} %param.13) | copy-start | bytes 24580
  81.3 34.1 %copy-start = (bf16[256,2048]{1,0:T(8,128)(2,1)S(1)}, bf16[256,2048]{1,0:T(8,128)(2,1)}, u32[]{:S(2)}) copy-start(bf16[256,2048]{1,0:T(8,128)(2,1)} %signal_ref.3) | copy-start | bytes 3145732
  81.3 34.1 %copy-start.1 = (bf16[256,2048]{1,0:T(8,128)(2,1)S(1)}, bf16[256,2048]{1,0:T(8,128)(2,1)}, u32[]{:S(2)}) copy-start(bf16[256,2048]{1,0:T(8,128)(2,1)} %gate_ref.3) | copy-start | bytes 3145732
  (6 other events, 11.7 us)

commit v8 on v7

--- a/solution.py
+++ b/solution.py
@@ -359,16 +359,18 @@
         real_ref[pl.ds(at, width), :] = values[0]
         imag_ref[pl.ds(at, width), :] = values[1]
 
-    for distance in distances:
-        block = block_of(distance)
-        for near in pair_of(distance):
-            arrival(near).wait()
-        slots = [
-            (per_source * block + v, response_of(distance, v), block, v)
-            for v in range(1, per_source)
-        ]
-        for at in range(0, len(slots), 2):
-            pair = slots[at : at + 2]
+    for at in range(0, len(distances), 2):
+        slots = []
+        for distance in distances[at : at + 2]:
+            block = block_of(distance)
+            for near in pair_of(distance):
+                arrival(near).wait()
+            slots += [
+                (per_source * block + v, response_of(distance, v), block, v)
+                for v in range(1, per_source)
+            ]
+        for first_slot in range(0, len(slots), 2):
+            pair = slots[first_slot : first_slot + 2]
             for slot, values in zip(pair, third_stage(pair)):
                 keep(slot[0], values)
     if early:

time: 117 us -> 117 us (level)
  no operation moved by 1% of the time
where the time goes in v8:
time: 117 us
  blocking collectives  34.1 us (29%)
  starting transfers between devices  29.1 us (25%)
  waiting for transfers between devices  28.5 us (24%)
  Pallas kernels  24.2 us (21%)
    all_to_all x1, blocking collectives, exchange(): return lax.all_to_all(values, axes, split_axis=0, concat_axis=0, tiled=True)  34.1 us
    ppermute x15, waiting for transfers between devices, swap_with(): lax.ppermute(values, 'seq', [(i, i ^ distance) for i in range(count)])  28.5 us
    ppermute x15, starting transfers between devices, swap_with(): lax.ppermute(values, 'seq', [(i, i ^ distance) for i in range(count)])  21.8 us
    pallas_call x2, Pallas kernels, call(): pl.pallas_call(functools.partial(inverse_kernel, devices_seq=devices_seq,...  7.4 us
    all_to_all x1, starting transfers between devices, exchange(): return lax.all_to_all(values, axes, split_axis=0, concat_axis=0, tiled=True)  7.3 us
    pallas_call x1, Pallas kernels, forward(): pl.pallas_call(functools.partial(forward_kernel, devices_seq=devices_seq)...  6.69 us
    pallas_call x1, Pallas kernels, pack_filter(): pl.pallas_call(functools.partial(pack_filter_kernel, middle=low * devices...  5.76 us
    pallas_call x1, Pallas kernels, pack_input(): pl.pallas_call(pack_input_kernel, out_shape=jax.ShapeDtypeStruct((devices...  2.58 us
  transfers between devices with their start and end apart: 16, of which 6 were waited for; matrix products, arithmetic and copies ran while one was open for 0% of the time, Pallas kernels for 13%

profile of v8, /device:TPU:0, one launch (start us, length us, event | category | flops | bytes accessed | tf_op | source)
XLA Modules:
  0.0 117.0 jit_solution(6159123183796945997)
XLA Ops:
  0.0 2.6 %pack_input.1 = bf16[16,2,128,128]{3,2,1,0:T(8,128)(2,1)} custom-call(bf16[256,2048]{1,0:T(8,128)(2,1)} %signal_ref.3, bf16[256,2048]{1,0:T(8,128)(2,1)} %gate_ref.3), custom_call_target="tpu_custom_call" | custom-call | flops 524288 | bytes 3145728 | tf_op jit(solution)/shard_map/pack_input/pallas_call | solution.py:90
  2.6 7.3 %all-to-all-start = ((bf16[32,128,128]{2,1,0:T(8,128)(2,1)}), bf16[32,128,128]{2,1,0:T(8,128)(2,1)S(1)}, u32[]{:S(2)}, u32[]{:S(2)}) async-start(bf16[32,128,128]{2,1,0:T(8,128)(2,1)} %bitcast.11), calls=%async_computation | async-start | bytes 2097152 | tf_op jit(solution)/shard_map/all_to_all | solution.py:24
  9.9 0.1 pad_add_fusion.place_ref
  10.0 5.8 %pack_filter.1 = (bf16[512,128]{1,0:T(8,128)(2,1)}, bf16[512,128]{1,0:T(8,128)(2,1)}, bf16[512,128]{1,0:T(8,128)(2,1)}, bf16[512,128]{1,0:T(8,128)(2,1)}, bf16[5...) custom-call(s32[2]{0:T(128)S(1)} %pad_add_fusion.place_ref, ...), custom_call_target="tpu_custom_call" | custom-call | flops 134217728 | bytes 6291456 | tf_op jit(solution)/shard_map/pack_filter/pallas_call | solution.py:144
  15.7 0.3 collective-permute-start
  16.0 1.7 %collective-permute-start.1 = (bf16[512,128]{1,0:T(8,128)(2,1)}, bf16[512,128]{1,0:T(8,128)(2,1)S(1)}, u32[]{:S(2)}, u32[]{:S(2)}) collective-permute-start(bf16[512,128]{1,0:T(8,128)(2,1)} %get-tuple-element.26), channel_id=1, source_target_pairs={{0,2},{1,3},{2,0},{3,1},{4,6},{5,7},{6,4},{7,5},{8,10},{9,11},{10,... | collective-permute-start | bytes 393224 | tf_op jit(solution)/shard_map/ppermute | solution.py:171
  17.7 1.5 %collective-permute-start.3 = (bf16[512,128]{1,0:T(8,128)(2,1)}, bf16[512,128]{1,0:T(8,128)(2,1)S(1)}, u32[]{:S(2)}, u32[]{:S(2)}) collective-permute-start(bf16[512,128]{1,0:T(8,128)(2,1)} %get-tuple-element.28), channel_id=1, source_target_pairs={{0,4},{1,5},{2,6},{3,7},{4,0},{5,1},{6,2},{7,3},{8,12},{9,13},{10,... | collective-permute-start | bytes 393224 | tf_op jit(solution)/shard_map/ppermute | solution.py:171
  19.1 1.4 %collective-permute-start.5 = (bf16[512,128]{1,0:T(8,128)(2,1)}, bf16[512,128]{1,0:T(8,128)(2,1)S(1)}, u32[]{:S(2)}, u32[]{:S(2)}) collective-permute-start(bf16[512,128]{1,0:T(8,128)(2,1)} %get-tuple-element.30), channel_id=1, source_target_pairs={{0,6},{1,7},{2,4},{3,5},{4,2},{5,3},{6,0},{7,1},{8,14},{9,15},{10,... | collective-permute-start | bytes 393224 | tf_op jit(solution)/shard_map/ppermute | solution.py:171
  20.6 1.5 %collective-permute-start.6 = (bf16[512,128]{1,0:T(8,128)(2,1)}, bf16[512,128]{1,0:T(8,128)(2,1)S(1)}, u32[]{:S(2)}, u32[]{:S(2)}) collective-permute-start(bf16[512,128]{1,0:T(8,128)(2,1)} %get-tuple-element.31), channel_id=1, source_target_pairs={{0,7},{1,6},{2,5},{3,4},{4,3},{5,2},{6,1},{7,0},{8,15},{9,14},{10,... | collective-permute-start | bytes 393224 | tf_op jit(solution)/shard_map/ppermute | solution.py:171
  22.1 3.0 %collective-permute-done.1.refs_2_ = bf16[512,128]{1,0:T(8,128)(2,1)S(1)} collective-permute-done((bf16[512,128]{1,0:T(8,128)(2,1)}, bf16[512,128]{1,0:T(8,128)(2,1)S(1)}, u32[]{:S(2)}, u32[]{:S(2)}) %collective-permute-start.1) | collective-permute-done | bytes 131104 | tf_op jit(solution)/shard_map/ppermute | solution.py:171
  25.1 2.4 %collective-permute-start.7 = (bf16[512,128]{1,0:T(8,128)(2,1)}, bf16[512,128]{1,0:T(8,128)(2,1)S(1)}, u32[]{:S(2)}, u32[]{:S(2)}) collective-permute-start(bf16[512,128]{1,0:T(8,128)(2,1)} %get-tuple-element.32), channel_id=1, source_target_pairs={{0,8},{1,9},{2,10},{3,11},{4,12},{5,13},{6,14},{7,15},{8,0},{9,1},... | collective-permute-start | bytes 393224 | tf_op jit(solution)/shard_map/ppermute | solution.py:171
  27.4 3.4 %collective-permute-done.3.refs_4_ = bf16[512,128]{1,0:T(8,128)(2,1)S(1)} collective-permute-done((bf16[512,128]{1,0:T(8,128)(2,1)}, bf16[512,128]{1,0:T(8,128)(2,1)S(1)}, u32[]{:S(2)}, u32[]{:S(2)}) %collective-permute-start.3) | collective-permute-done | bytes 131104 | tf_op jit(solution)/shard_map/ppermute | solution.py:171
  30.8 3.3 %collective-permute-start.8 = (bf16[512,128]{1,0:T(8,128)(2,1)}, bf16[512,128]{1,0:T(8,128)(2,1)S(1)}, u32[]{:S(2)}, u32[]{:S(2)}) collective-permute-start(bf16[512,128]{1,0:T(8,128)(2,1)} %get-tuple-element.33), channel_id=1, source_target_pairs={{0,9},{1,8},{2,11},{3,10},{4,13},{5,12},{6,15},{7,14},{8,1},{9,0},... | collective-permute-start | bytes 393224 | tf_op jit(solution)/shard_map/ppermute | solution.py:171
  34.1 4.0 %collective-permute-start.9 = (bf16[512,128]{1,0:T(8,128)(2,1)}, bf16[512,128]{1,0:T(8,128)(2,1)S(1)}, u32[]{:S(2)}, u32[]{:S(2)}) collective-permute-start(bf16[512,128]{1,0:T(8,128)(2,1)} %get-tuple-element.34), channel_id=1, source_target_pairs={{0,10},{1,11},{2,8},{3,9},{4,14},{5,15},{6,12},{7,13},{8,2},{9,3},... | collective-permute-start | bytes 393224 | tf_op jit(solution)/shard_map/ppermute | solution.py:171
  38.1 7.9 %collective-permute-done.5.refs_6_ = bf16[512,128]{1,0:T(8,128)(2,1)S(1)} collective-permute-done((bf16[512,128]{1,0:T(8,128)(2,1)}, bf16[512,128]{1,0:T(8,128)(2,1)S(1)}, u32[]{:S(2)}, u32[]{:S(2)}) %collective-permute-start.5) | collective-permute-done | bytes 131104 | tf_op jit(solution)/shard_map/ppermute | solution.py:171
  46.0 1.9 %collective-permute-done.6.refs_0_.refs_1_.refs_2_.refs_3_.refs_7_.refs_12_.refs_13_.refs_14_.refs_15_ = bf16[512,128]{1,0:T(8,128)(2,1)S(1)} collective-permute-done((bf16[512,128]{1,0:T(8,128)(2,1)}, bf16[512,128]{1,0:T(8,128)(2,1)S(1)}, u32[]{:S(2)}, u32[]{:S(2)}) %collective-permute-start.6) | collective-permute-done | bytes 131104 | tf_op jit(solution)/shard_map/ppermute | solution.py:171
  47.9 0.7 collective-permute-start.2
  48.6 1.3 %collective-permute-start.11 = (bf16[512,128]{1,0:T(8,128)(2,1)}, bf16[512,128]{1,0:T(8,128)(2,1)S(1)}, u32[]{:S(2)}, u32[]{:S(2)}) collective-permute-start(bf16[512,128]{1,0:T(8,128)(2,1)} %get-tuple-element.36), channel_id=1, source_target_pairs={{0,12},{1,13},{2,14},{3,15},{4,8},{5,9},{6,10},{7,11},{8,4},{9,5},... | collective-permute-start | bytes 393224 | tf_op jit(solution)/shard_map/ppermute | solution.py:171
  49.9 1.8 %collective-permute-start.12 = (bf16[512,128]{1,0:T(8,128)(2,1)}, bf16[512,128]{1,0:T(8,128)(2,1)S(1)}, u32[]{:S(2)}, u32[]{:S(2)}) collective-permute-start(bf16[512,128]{1,0:T(8,128)(2,1)} %get-tuple-element.37), channel_id=1, source_target_pairs={{0,13},{1,12},{2,15},{3,14},{4,9},{5,8},{6,11},{7,10},{8,5},{9,4},... | collective-permute-start | bytes 393224 | tf_op jit(solution)/shard_map/ppermute | solution.py:171
  51.7 11.1 %collective-permute-done.9.refs_10_ = bf16[512,128]{1,0:T(8,128)(2,1)S(1)} collective-permute-done((bf16[512,128]{1,0:T(8,128)(2,1)}, bf16[512,128]{1,0:T(8,128)(2,1)S(1)}, u32[]{:S(2)}, u32[]{:S(2)}) %collective-permute-start.9) | collective-permute-done | bytes 131104 | tf_op jit(solution)/shard_map/ppermute | solution.py:171
  62.8 0.6 collective-permute-start.13
  63.5 1.2 %collective-permute-done.10.refs_11_ = bf16[512,128]{1,0:T(8,128)(2,1)S(1)} collective-permute-done((bf16[512,128]{1,0:T(8,128)(2,1)}, bf16[512,128]{1,0:T(8,128)(2,1)S(1)}, u32[]{:S(2)}, u32[]{:S(2)}) %collective-permute-start.10) | collective-permute-done | bytes 131104 | tf_op jit(solution)/shard_map/ppermute | solution.py:171
  64.7 1.4 %collective-permute-start.14 = (bf16[512,128]{1,0:T(8,128)(2,1)}, bf16[512,128]{1,0:T(8,128)(2,1)S(1)}, u32[]{:S(2)}, u32[]{:S(2)}) collective-permute-start(bf16[512,128]{1,0:T(8,128)(2,1)} %get-tuple-element.39), channel_id=1, source_target_pairs={{0,15},{1,14},{2,13},{3,12},{4,11},{5,10},{6,9},{7,8},{8,7},{9,6},... | collective-permute-start | bytes 393224 | tf_op jit(solution)/shard_map/ppermute | solution.py:171
  66.1 6.7 %forward.1.spec_ref = f32[65,128,128]{2,1,0:T(8,128)S(1)} custom-call(bf16[16,2,128,128]{3,2,1,0:T(8,128)(2,1)S(1)} %bitcast.8, bf16[128,128]{1,0:T(8,128)(2,1)S(1)} %copy-done.5, bf16[128,384]{1,0:T(8,128)(2,1)S(1)} %copy-done.4, f32[9,64,128]{2,1,0:T(8,128)S(1)} %copy-done.2), custom_call_target="tpu_custom_call" | custom-call | flops 1073741824 | bytes 5242880 | tf_op jit(solution)/shard_map/forward/pallas_call | solution.py:254
  72.9 2.7 %inverse_early.1 = (f32[4608,128]{1,0:T(8,128)S(1)}, f32[4608,128]{1,0:T(8,128)S(1)}) custom-call(s32[1]{0:T(128)} %bitcast.place_ref, f32[65,128,128]{2,1,0:T(8,128)S(1)} %forward.1.spec_ref, f32[9,64,128]{2,1,0:T(8,128)S(1)} %copy-done.2, bf16[192,256]{1,0:T(8,128)(2,1)} %constant.20.clone.matrices_hbm, bf16[512,128]{1,0:T(8,128)(2,1)} %copy-done.7, ...), custom_call_target="tpu_custom_call" | custom-call | flops 402653184 | bytes 2097152 | tf_op jit(solution)/shard_map/inverse_early/pallas_call | solution.py:457
  75.7 0.6 copy-done.17
  76.3 0.0 copy-done.18
  76.4 0.1 copy-done.20
  76.4 0.0 copy-done.21
  76.5 4.7 %inverse_late.1 = (bf16[16,2,128,128]{3,2,1,0:T(8,128)(2,1)S(1)}, f32[4608,128]{1,0:T(8,128)S(1)}, f32[4608,128]{1,0:T(8,128)S(1)}) custom-call(s32[1]{0:T(128)} %bitcast.place_ref, f32[65,128,128]{2,1,0:T(8,128)S(1)} %forward.1.spec_ref, f32[9,64,128]{2,1,0:T(8,128)S(1)} %copy-done.2, ...), custom_call_target="tpu_custom_call", output_to_operand_aliasing={{1}: (20, {}), {2}: (21, {})} | custom-call | flops 402653184 | bytes 2097152 | tf_op jit(solution)/shard_map/inverse_late/pallas_call | solution.py:457
  81.2 34.1 %all_to_all.10 = bf16[32,128,128]{2,1,0:T(8,128)(2,1)S(1)} all-to-all(bf16[32,128,128]{2,1,0:T(8,128)(2,1)S(1)} %bitcast.9), channel_id=1, replica_groups=mesh['groups'=2,'seq'=16] {'seq','groups'}, dimensions={0} | all-to-all | bytes 2097152 | tf_op jit(solution)/shard_map/all_to_all | solution.py:24
  115.3 1.7 %mix.1 = bf16[256,2048]{1,0:T(8,128)(2,1)} custom-call(bf16[16,2,128,128]{3,2,1,0:T(8,128)(2,1)S(1)} %bitcast.7, bf16[256,2048]{1,0:T(8,128)(2,1)S(1)} %copy-done, bf16[256,2048]{1,0:T(8,128)(2,1)S(1)} %copy-done.1, bf16[256,2048]{1,0:T(8,128)(2,1)S(1)} %copy-done.3, f32[1,2048]{1,0:T(1,128)S(1)} %bitcast.10), custom_call_target="tpu_custom_call" | custom-call | flops 2097152 | bytes 5242880 | tf_op jit(solution)/shard_map/mix/pallas_call | solution.py:514
  (52 shorter events, 0.1 us)
Async XLA Ops:
  2.6 63.5 %all-to-all-start = ((bf16[32,128,128]{2,1,0:T(8,128)(2,1)}), bf16[32,128,128]{2,1,0:T(8,128)(2,1)S(1)}, u32[]{:S(2)}, u32[]{:S(2)}) async-start(bf16[32,128,128]{2,1,0:T(8,128)(2,1)} %bitcast.11), calls=%async_computation | async-start | bytes 2097152 | tf_op jit(solution)/shard_map/all_to_all | solution.py:24
  10.0 56.1 %copy-start.2 = (f32[9,64,128]{2,1,0:T(8,128)S(1)}, f32[9,64,128]{2,1,0:T(8,128)}, u32[]{:S(2)}) copy-start(f32[9,64,128]{2,1,0:T(8,128)} %constant.19.clone.turn_ref) | copy-start | bytes 884740
  10.0 56.1 %copy-start.4 = (bf16[128,384]{1,0:T(8,128)(2,1)S(1)}, bf16[128,384]{1,0:T(8,128)(2,1)}, u32[]{:S(2)}) copy-start(bf16[128,384]{1,0:T(8,128)(2,1)} %constant.18.clone.second_ref) | copy-start | bytes 294916
  10.0 56.1 %copy-start.5 = (bf16[128,128]{1,0:T(8,128)(2,1)S(1)}, bf16[128,128]{1,0:T(8,128)(2,1)}, u32[]{:S(2)}) copy-start(bf16[128,128]{1,0:T(8,128)(2,1)} %constant.17.clone.first_ref) | copy-start | bytes 98308
  15.7 4.8 %collective-permute-start = (bf16[512,128]{1,0:T(8,128)(2,1)}, bf16[512,128]{1,0:T(8,128)(2,1)S(1)}, u32[]{:S(2)}, u32[]{:S(2)}) collective-permute-start(bf16[512,128]{1,0:T(8,128)(2,1)} %get-tuple-element.25), channel_id=1, source_target_pairs={{0,1},{1,0},{2,3},{3,2},{4,5},{5,4},{6,7},{7,6},{8,9},{9,8},{10,11... | collective-permute-start | bytes 393224 | tf_op jit(solution)/shard_map/ppermute | solution.py:171
  16.0 9.1 %collective-permute-start.1 = (bf16[512,128]{1,0:T(8,128)(2,1)}, bf16[512,128]{1,0:T(8,128)(2,1)S(1)}, u32[]{:S(2)}, u32[]{:S(2)}) collective-permute-start(bf16[512,128]{1,0:T(8,128)(2,1)} %get-tuple-element.26), channel_id=1, source_target_pairs={{0,2},{1,3},{2,0},{3,1},{4,6},{5,7},{6,4},{7,5},{8,10},{9,11},{10,... | collective-permute-start | bytes 393224 | tf_op jit(solution)/shard_map/ppermute | solution.py:171
  17.7 13.1 %collective-permute-start.3 = (bf16[512,128]{1,0:T(8,128)(2,1)}, bf16[512,128]{1,0:T(8,128)(2,1)S(1)}, u32[]{:S(2)}, u32[]{:S(2)}) collective-permute-start(bf16[512,128]{1,0:T(8,128)(2,1)} %get-tuple-element.28), channel_id=1, source_target_pairs={{0,4},{1,5},{2,6},{3,7},{4,0},{5,1},{6,2},{7,3},{8,12},{9,13},{10,... | collective-permute-start | bytes 393224 | tf_op jit(solution)/shard_map/ppermute | solution.py:171
  19.1 14.9 %collective-permute-start.4 = (bf16[512,128]{1,0:T(8,128)(2,1)}, bf16[512,128]{1,0:T(8,128)(2,1)S(1)}, u32[]{:S(2)}, u32[]{:S(2)}) collective-permute-start(bf16[512,128]{1,0:T(8,128)(2,1)} %get-tuple-element.29), channel_id=1, source_target_pairs={{0,5},{1,4},{2,7},{3,6},{4,1},{5,0},{6,3},{7,2},{8,13},{9,12},{10,... | collective-permute-start | bytes 393224 | tf_op jit(solution)/shard_map/ppermute | solution.py:171
  19.1 26.9 %collective-permute-start.5 = (bf16[512,128]{1,0:T(8,128)(2,1)}, bf16[512,128]{1,0:T(8,128)(2,1)S(1)}, u32[]{:S(2)}, u32[]{:S(2)}) collective-permute-start(bf16[512,128]{1,0:T(8,128)(2,1)} %get-tuple-element.30), channel_id=1, source_target_pairs={{0,6},{1,7},{2,4},{3,5},{4,2},{5,3},{6,0},{7,1},{8,14},{9,15},{10,... | collective-permute-start | bytes 393224 | tf_op jit(solution)/shard_map/ppermute | solution.py:171
  20.6 52.2 %copy-start.15 = (bf16[512,128]{1,0:T(8,128)(2,1)}, bf16[512,128]{1,0:T(8,128)(2,1)S(1)}, u32[]{:S(2)}) copy-start(bf16[512,128]{1,0:T(8,128)(2,1)S(1)} %collective-permute-done.refs_1_) | copy-start | bytes 393220
  20.6 27.3 %collective-permute-start.6 = (bf16[512,128]{1,0:T(8,128)(2,1)}, bf16[512,128]{1,0:T(8,128)(2,1)S(1)}, u32[]{:S(2)}, u32[]{:S(2)}) collective-permute-start(bf16[512,128]{1,0:T(8,128)(2,1)} %get-tuple-element.31), channel_id=1, source_target_pairs={{0,7},{1,6},{2,5},{3,4},{4,3},{5,2},{6,1},{7,0},{8,15},{9,14},{10,... | collective-permute-start | bytes 393224 | tf_op jit(solution)/shard_map/ppermute | solution.py:171
  25.1 47.7 %copy-start.16 = (bf16[512,128]{1,0:T(8,128)(2,1)}, bf16[512,128]{1,0:T(8,128)(2,1)S(1)}, u32[]{:S(2)}) copy-start(bf16[512,128]{1,0:T(8,128)(2,1)S(1)} %collective-permute-done.1.refs_2_) | copy-start | bytes 393220
  25.1 23.6 %collective-permute-start.7 = (bf16[512,128]{1,0:T(8,128)(2,1)}, bf16[512,128]{1,0:T(8,128)(2,1)S(1)}, u32[]{:S(2)}, u32[]{:S(2)}) collective-permute-start(bf16[512,128]{1,0:T(8,128)(2,1)} %get-tuple-element.32), channel_id=1, source_target_pairs={{0,8},{1,9},{2,10},{3,11},{4,12},{5,13},{6,14},{7,15},{8,0},{9,1},... | collective-permute-start | bytes 393224 | tf_op jit(solution)/shard_map/ppermute | solution.py:171
  30.8 42.0 %copy-start.8 = (bf16[512,128]{1,0:T(8,128)(2,1)}, bf16[512,128]{1,0:T(8,128)(2,1)S(1)}, u32[]{:S(2)}) copy-start(bf16[512,128]{1,0:T(8,128)(2,1)S(1)} %collective-permute-done.3.refs_4_) | copy-start | bytes 393220
  30.8 19.1 %collective-permute-start.8 = (bf16[512,128]{1,0:T(8,128)(2,1)}, bf16[512,128]{1,0:T(8,128)(2,1)S(1)}, u32[]{:S(2)}, u32[]{:S(2)}) collective-permute-start(bf16[512,128]{1,0:T(8,128)(2,1)} %get-tuple-element.33), channel_id=1, source_target_pairs={{0,9},{1,8},{2,11},{3,10},{4,13},{5,12},{6,15},{7,14},{8,1},{9,0},... | collective-permute-start | bytes 393224 | tf_op jit(solution)/shard_map/ppermute | solution.py:171
  34.1 38.7 %copy-start.9 = (bf16[512,128]{1,0:T(8,128)(2,1)}, bf16[512,128]{1,0:T(8,128)(2,1)S(1)}, u32[]{:S(2)}) copy-start(bf16[512,128]{1,0:T(8,128)(2,1)S(1)} %collective-permute-done.4.refs_5_) | copy-start | bytes 393220
  34.1 28.8 %collective-permute-start.9 = (bf16[512,128]{1,0:T(8,128)(2,1)}, bf16[512,128]{1,0:T(8,128)(2,1)S(1)}, u32[]{:S(2)}, u32[]{:S(2)}) collective-permute-start(bf16[512,128]{1,0:T(8,128)(2,1)} %get-tuple-element.34), channel_id=1, source_target_pairs={{0,10},{1,11},{2,8},{3,9},{4,14},{5,15},{6,12},{7,13},{8,2},{9,3},... | collective-permute-start | bytes 393224 | tf_op jit(solution)/shard_map/ppermute | solution.py:171
  46.0 26.8 %copy-start.10 = (bf16[512,128]{1,0:T(8,128)(2,1)}, bf16[512,128]{1,0:T(8,128)(2,1)S(1)}, u32[]{:S(2)}) copy-start(bf16[512,128]{1,0:T(8,128)(2,1)S(1)} %collective-permute-done.5.refs_6_) | copy-start | bytes 393220
  46.0 18.6 %collective-permute-start.10 = (bf16[512,128]{1,0:T(8,128)(2,1)}, bf16[512,128]{1,0:T(8,128)(2,1)S(1)}, u32[]{:S(2)}, u32[]{:S(2)}) collective-permute-start(bf16[512,128]{1,0:T(8,128)(2,1)} %get-tuple-element.35), channel_id=1, source_target_pairs={{0,11},{1,10},{2,9},{3,8},{4,15},{5,14},{6,13},{7,12},{8,3},{9,2},... | collective-permute-start | bytes 393224 | tf_op jit(solution)/shard_map/ppermute | solution.py:171
  47.9 24.9 %copy-start.7 = (bf16[512,128]{1,0:T(8,128)(2,1)}, bf16[512,128]{1,0:T(8,128)(2,1)S(1)}, u32[]{:S(2)}) copy-start(bf16[512,128]{1,0:T(8,128)(2,1)S(1)} %collective-permute-done.6.refs_0_.refs_1_.refs_2_.refs_3_.refs_7_.refs_12_.refs_13_.refs_14_.refs_15_) | copy-start | bytes 393220
  47.9 27.7 %collective-permute-start.2 = (bf16[512,128]{1,0:T(8,128)(2,1)}, bf16[512,128]{1,0:T(8,128)(2,1)S(1)}, u32[]{:S(2)}, u32[]{:S(2)}) collective-permute-start(bf16[512,128]{1,0:T(8,128)(2,1)} %get-tuple-element.27), channel_id=1, source_target_pairs={{0,3},{1,2},{2,1},{3,0},{4,7},{5,6},{6,5},{7,4},{8,11},{9,10},{10,... | collective-permute-start | bytes 393224 | tf_op jit(solution)/shard_map/ppermute | solution.py:171
  48.6 24.2 %copy-start.11 = (bf16[512,128]{1,0:T(8,128)(2,1)}, bf16[512,128]{1,0:T(8,128)(2,1)S(1)}, u32[]{:S(2)}) copy-start(bf16[512,128]{1,0:T(8,128)(2,1)S(1)} %collective-permute-done.7.refs_8_) | copy-start | bytes 393220
  48.6 27.0 %collective-permute-start.11 = (bf16[512,128]{1,0:T(8,128)(2,1)}, bf16[512,128]{1,0:T(8,128)(2,1)S(1)}, u32[]{:S(2)}, u32[]{:S(2)}) collective-permute-start(bf16[512,128]{1,0:T(8,128)(2,1)} %get-tuple-element.36), channel_id=1, source_target_pairs={{0,12},{1,13},{2,14},{3,15},{4,8},{5,9},{6,10},{7,11},{8,4},{9,5},... | collective-permute-start | bytes 393224 | tf_op jit(solution)/shard_map/ppermute | solution.py:171
  49.9 22.9 %copy-start.12 = (bf16[512,128]{1,0:T(8,128)(2,1)}, bf16[512,128]{1,0:T(8,128)(2,1)S(1)}, u32[]{:S(2)}) copy-start(bf16[512,128]{1,0:T(8,128)(2,1)S(1)} %collective-permute-done.8.refs_9_) | copy-start | bytes 393220
  49.9 25.8 %collective-permute-start.12 = (bf16[512,128]{1,0:T(8,128)(2,1)}, bf16[512,128]{1,0:T(8,128)(2,1)S(1)}, u32[]{:S(2)}, u32[]{:S(2)}) collective-permute-start(bf16[512,128]{1,0:T(8,128)(2,1)} %get-tuple-element.37), channel_id=1, source_target_pairs={{0,13},{1,12},{2,15},{3,14},{4,9},{5,8},{6,11},{7,10},{8,5},{9,4},... | collective-permute-start | bytes 393224 | tf_op jit(solution)/shard_map/ppermute | solution.py:171
  62.8 10.0 %copy-start.13 = (bf16[512,128]{1,0:T(8,128)(2,1)}, bf16[512,128]{1,0:T(8,128)(2,1)S(1)}, u32[]{:S(2)}) copy-start(bf16[512,128]{1,0:T(8,128)(2,1)S(1)} %collective-permute-done.9.refs_10_) | copy-start | bytes 393220
  62.8 12.9 %collective-permute-start.13 = (bf16[512,128]{1,0:T(8,128)(2,1)}, bf16[512,128]{1,0:T(8,128)(2,1)S(1)}, u32[]{:S(2)}, u32[]{:S(2)}) collective-permute-start(bf16[512,128]{1,0:T(8,128)(2,1)} %get-tuple-element.38), channel_id=1, source_target_pairs={{0,14},{1,15},{2,12},{3,13},{4,10},{5,11},{6,8},{7,9},{8,6},{9,7},... | collective-permute-start | bytes 393224 | tf_op jit(solution)/shard_map/ppermute | solution.py:171
  64.7 11.0 %collective-permute-start.14 = (bf16[512,128]{1,0:T(8,128)(2,1)}, bf16[512,128]{1,0:T(8,128)(2,1)S(1)}, u32[]{:S(2)}, u32[]{:S(2)}) collective-permute-start(bf16[512,128]{1,0:T(8,128)(2,1)} %get-tuple-element.39), channel_id=1, source_target_pairs={{0,15},{1,14},{2,13},{3,12},{4,11},{5,10},{6,9},{7,8},{8,7},{9,6},... | collective-permute-start | bytes 393224 | tf_op jit(solution)/shard_map/ppermute | solution.py:171
  76.5 38.8 %copy-start.3 = (bf16[256,2048]{1,0:T(8,128)(2,1)S(1)}, bf16[256,2048]{1,0:T(8,128)(2,1)}, u32[]{:S(2)}) copy-start(bf16[256,2048]{1,0:T(8,128)(2,1)} %out_gate_ref.1) | copy-start | bytes 3145732
  76.5 38.8 %copy-start.6 = (f32[2048]{0:T(1024)S(1)}, f32[2048]{0:T(1024)}, u32[]{:S(2)}) copy-start(f32[2048]{0:T(1024)} %param.13) | copy-start | bytes 24580
  81.1 34.1 %copy-start = (bf16[256,2048]{1,0:T(8,128)(2,1)S(1)}, bf16[256,2048]{1,0:T(8,128)(2,1)}, u32[]{:S(2)}) copy-start(bf16[256,2048]{1,0:T(8,128)(2,1)} %signal_ref.3) | copy-start | bytes 3145732
  81.1 34.1 %copy-start.1 = (bf16[256,2048]{1,0:T(8,128)(2,1)S(1)}, bf16[256,2048]{1,0:T(8,128)(2,1)}, u32[]{:S(2)}) copy-start(bf16[256,2048]{1,0:T(8,128)(2,1)} %gate_ref.3) | copy-start | bytes 3145732
  (6 other events, 11.7 us)
